TPU v7x, 128 devices: a whole 4x4x4 slice. The times are simulated.
128 devices in a mesh: row: 16 (over y_lo, x, core), col: 8 (over y_hi, z).
Axes of the slice: x: 4, y: 4 (y_hi: 2, y_lo: 2; y = y_hi * 2 + y_lo), z: 4, core: 2. Of those that a mesh axis runs over, the one named last changes fastest.
Arguments:
- embeddings: float32 [49152, 64], P(('row', 'col')), may hold values from -6 to 6
- inv_length: float32 [64], replicated, may hold values from 0.1 to 0.4
- noise: float32 [49152], P(('row', 'col')), may hold values from 0.1 to 1
- probes: bfloat16 [49152, 256], P(('row', 'col')), may hold values from -1.5 to 1.5
Outputs:
- applied: float32 [49152, 256], P(('row', 'col'))
All inputs are finite; a program needn't handle non-finite values.
Results may differ from a plain program's by a relative error of at most 0.0029.
Values may be sent and summed in bfloat16 or wider, within the bound.
No kernel may reach another device: no remote copies, remote signals or barrier semaphores. Data moves between devices by JAX's collectives and lax.ppermute only.
A program may use at most 192 MiB of HBM per device.

v0:
```python
import jax
import jax.numpy as jnp
from jax import lax
from jax.sharding import PartitionSpec as P


def kernel_tile(rows, row_sq, cols, col_sq, col_probes):
    gram = jnp.dot(
        rows, cols.T, precision=lax.Precision.HIGHEST, preferred_element_type=jnp.float32
    )
    dist = row_sq[:, None] + col_sq[None, :] - 2.0 * gram
    kernel = jnp.exp(-0.5 * dist).astype(jnp.bfloat16)
    return jnp.dot(kernel, col_probes, preferred_element_type=jnp.float32)


def on_device(embeddings, inv_length, noise, probes):
    scaled = embeddings * inv_length[None, :]
    own_sq = jnp.sum(scaled * scaled, axis=1)
    diag_term = noise[:, None] * probes.astype(jnp.float32)
    every = lax.all_gather(scaled, ("row", "col"), axis=0, tiled=True)
    every_sq = jnp.sum(every * every, axis=1)
    product = kernel_tile(
        scaled, own_sq, every, every_sq, lax.all_gather(probes, ("row", "col"), axis=0, tiled=True)
    )
    return product + diag_term


def solution(mesh):
    return jax.shard_map(
        on_device,
        mesh=mesh,
        in_specs=(P(("row", "col"), None), P(), P(("row", "col")), P(("row", "col"), None)),
        out_specs=P(("row", "col"), None),
        check_vma=False,
    )
```

profile of v0, /device:TPU:1, one launch (start us, length us, event | category | flops | bytes accessed | tf_op | source)
XLA Modules:
  0.0 696.6 jit_solution(2096074242026698704)
XLA Ops:
  6.5 0.0 all-gather.3.cloned.1.call-start
  6.5 1.6 multiply_reduce_fusion.1
  8.2 0.0 all-gather.3.cloned.1.call-update
  8.2 0.0 all-gather.5.cloned.1.call-start
  8.2 0.7 all-gather.5.cloned.1.call-update
  8.9 321.8 %all-gather.3.cloned.1.call-done = f32[49152,64]{0,1:T(8,128)} async-done(((f32[384,64]{0,1:T(8,128)}), f32[49152,64]{0,1:T(8,128)}) %all-gather.3.cloned.1.call-update) | async-done | bytes 12582928 | tf_op jit(solution)/shard_map/all_gather | solution.py:20
  330.7 5.8 multiply_reduce_fusion
  336.5 0.0 copy-start
  336.5 0.0 copy-start.1
  336.5 77.5 %exponential_convert_fusion = bf16[384,49152]{1,0:T(8,128)(2,1)} fusion(f32[384,64]{0,1:T(8,128)} %get-tuple-element.6, f32[49152,64]{0,1:T(8,128)} %all-gather.3.cloned.1.call-done, f32[49152]{0:T(1024)S(1)} %multiply_reduce_fusion, f32[384]{0:T(512)S(1)} %get-tuple-element.5), kind=kOutput, calls=%fused_computation | convolution fusion | flops 14589886464 | bytes 50628096 | tf_op jit(solution)/shard_map/dot_general | solution.py:8
  414.1 251.7 %all-gather.5.cloned.1.call-done = bf16[49152,256]{1,0:T(8,128)(2,1)} async-done(((bf16[384,256]{1,0:T(8,128)(2,1)}), bf16[49152,256]{1,0:T(8,128)(2,1)}) %all-gather.5.cloned.1.call-update) | async-done | bytes 25165840 | tf_op jit(solution)/shard_map/all_gather | solution.py:23
  665.8 0.0 copy-done
  665.8 0.0 copy-done.1
  665.8 24.0 %convolution_add_fusion = f32[384,256]{1,0:T(8,128)} fusion(bf16[384,49152]{1,0:T(8,128)(2,1)} %exponential_convert_fusion, bf16[49152,256]{1,0:T(8,128)(2,1)} %all-gather.5.cloned.1.call-done, bf16[384,256]{1,0:T(8,128)(2,1)S(1)} %copy-done, f32[384]{0:T(512)S(1)} %copy-done.1), kind=kOutput, calls=%fused_computation.2 | convolution fusion | flops 9663971328 | bytes 63505920 | tf_op jit(solution)/shard_map/dot_general | solution.py:13
Async XLA Ops:
  6.5 324.2 %all-gather.3.cloned.1.call-start = ((), (), s32[]{:S(2)}) async-start(), calls=%async_computation | async-start | bytes 12681216 | tf_op jit(solution)/shard_map/all_gather | solution.py:20
  8.2 657.6 %all-gather.5.cloned.1.call-start = ((), (), s32[]{:S(2)}) async-start(), calls=%async_computation.1 | async-start | bytes 25362432 | tf_op jit(solution)/shard_map/all_gather | solution.py:23
  336.5 329.3 %copy-start = (bf16[384,256]{1,0:T(8,128)(2,1)S(1)}, bf16[384,256]{1,0:T(8,128)(2,1)}, u32[]{:S(2)}) copy-start(bf16[384,256]{1,0:T(8,128)(2,1)} %param.7) | copy-start | bytes 589828
  336.5 329.2 %copy-start.1 = (f32[384]{0:T(512)S(1)}, f32[384]{0:T(512)}, u32[]{:S(2)}) copy-start(f32[384]{0:T(512)} %param.6) | copy-start | bytes 4612
Sparse Core Ops, SparseCore 0:
  9.0 321.6 all-gather.2
  332.4 333.2 all-gather.4
where the time goes:
time: 697 us
  waiting for transfers between devices  574 us (82%)
  matrix products  102 us (15%)
  between operations  13.4 us (2%)
  other arithmetic  7.37 us (1%)
    all_gather x1, waiting for transfers between devices, on_device(): every = lax.all_gather(scaled, ('row', 'col'), axis=0, tiled=True)  322 us
    all_gather x1, waiting for transfers between devices, on_device(): lax.all_gather(probes, ('row', 'col'), axis=0, tiled=True)  252 us
    dot_general x1, matrix products, kernel_tile(): jnp.dot(rows, cols.T, precision=lax.Precision.HIGHEST, preferred_element_...  77.5 us
    dot_general x1, matrix products, kernel_tile(): return jnp.dot(kernel, col_probes, preferred_element_type=jnp.float32)  24 us
  transfers between devices with their start and end apart: 2, of which 2 were waited for; matrix products, arithmetic and copies ran while one was open for 12% of the time, Pallas kernels for 0%

commit v1 on v0

v1 whole, which is shorter than its diff:
```python
import math

import jax
import jax.numpy as jnp
from jax import lax
from jax.experimental import pallas as pl
from jax.experimental.pallas import tpu as pltpu
from jax.sharding import PartitionSpec as P

ROOT_LOG2E = math.sqrt(math.log2(math.e))
NT = (((1,), (1,)), ((), ()))
LANES = 128
HALF = 64


def split_scaled(embeddings, inv_length):
    scaled = (embeddings * inv_length[None, :]) * ROOT_LOG2E
    high = lax.reduce_precision(scaled, 8, 7)
    return jnp.concatenate([high, scaled - high], axis=1).astype(jnp.bfloat16)


def augment(pair, is_col):
    count = pair.shape[0]
    wide = pair.astype(jnp.float32)
    swapped = pltpu.roll(wide, HALF, 1)
    whole = wide + swapped
    norm = jnp.sum(whole * whole, axis=1, keepdims=True) * -0.25
    first = norm.astype(jnp.bfloat16).astype(jnp.float32)
    rest = norm - first
    second = rest.astype(jnp.bfloat16).astype(jnp.float32)
    third = rest - second
    lane = lax.broadcasted_iota(jnp.int32, (count, LANES), 1)
    at, ones = (HALF + 3, HALF) if is_col else (HALF, HALF + 3)
    extra = jnp.where((lane >= ones) & (lane < ones + 3), 1.0, 0.0)
    extra = jnp.where(lane == at, first, extra)
    extra = jnp.where(lane == at + 1, second, extra)
    extra = jnp.where(lane == at + 2, third, extra)
    low = lane < HALF
    if is_col:
        left, right = jnp.where(low, wide, swapped), jnp.where(low, swapped, extra)
    else:
        left, right = wide, jnp.where(low, wide, extra)
    return left.astype(jnp.bfloat16), right.astype(jnp.bfloat16)


def tile_kernel(block, row_step):
    def body(row_ref, mine_ref, other_ref, out_ref, left, right, probes):
        rows = row_ref.shape[0] * row_ref.shape[1]
        groups = mine_ref.shape[0]

        def fill_rows(i, carry):
            a, b = augment(row_ref[i], False)
            at = pl.ds(pl.multiple_of(i * block, block), block)
            left[at, :LANES] = a
            left[at, LANES:] = b
            return carry

        lax.fori_loop(0, row_ref.shape[0], fill_rows, 0)
        per = 4
        for half, src in enumerate((mine_ref, other_ref)):
            for start in range(0, groups, per):
                def fill_cols(i, carry):
                    a, b = augment(src[start + i, :, :LANES], True)
                    at = pl.ds(pl.multiple_of(i * block, block), block)
                    right[at, :LANES] = a
                    right[at, LANES:] = b
                    probes[at, :] = src[start + i, :, LANES:]
                    return carry

                lax.fori_loop(0, per, fill_cols, 0)
                first = half == 0 and start == 0

                def step(i, carry):
                    at = pl.ds(pl.multiple_of(i * row_step, row_step), row_step)
                    gram = lax.dot_general(left[at, :], right[...], NT, preferred_element_type=jnp.float32)
                    kernel = jnp.exp2(gram).astype(jnp.bfloat16)
                    part = jnp.dot(kernel, probes[...], preferred_element_type=jnp.float32)
                    if first:
                        out_ref[at, :] = part
                    else:
                        out_ref[at, :] += part
                    return carry

                lax.fori_loop(0, rows // row_step, step, 0)

    return body


def tile_product(rows, mine, other):
    block = rows.shape[1]
    count = rows.shape[0] * block
    width = mine.shape[2] - LANES
    cols = 4 * block
    vmem = pl.BlockSpec(memory_space=pltpu.VMEM)
    return pl.pallas_call(
        tile_kernel(block, 1024),
        in_specs=[vmem] * 3,
        out_specs=vmem,
        out_shape=jax.ShapeDtypeStruct((count, width), jnp.float32),
        scratch_shapes=[
            pltpu.VMEM((count, 2 * LANES), jnp.bfloat16),
            pltpu.VMEM((cols, 2 * LANES), jnp.bfloat16),
            pltpu.VMEM((cols, width), jnp.bfloat16),
        ],
        compiler_params=pltpu.CompilerParams(vmem_limit_bytes=56 << 20),
        name="tile_product",
    )(rows, mine, other)


def solution(mesh):
    row_size, col_size = mesh.shape["row"], mesh.shape["col"]
    same_core = [list(range(core, row_size, 2)) for core in range(2)]
    chips = row_size // 2

    def on_device(embeddings, inv_length, noise, probes):
        block, width = probes.shape
        pair = split_scaled(embeddings, inv_length)
        packed = jnp.concatenate([pair, probes], axis=1)
        rows = lax.all_to_all(jnp.broadcast_to(pair[None], (col_size, *pair.shape)), "col", 0, 0)
        mine = lax.all_to_all(
            jnp.broadcast_to(packed[None], (chips, *packed.shape)), "row", 0, 0, axis_index_groups=same_core
        )
        other = lax.ppermute(mine, "row", [(i, i ^ 1) for i in range(row_size)])
        partial = tile_product(rows, mine, other)
        sent = partial.reshape(col_size, block, width).astype(jnp.bfloat16)
        got = lax.all_to_all(sent, "col", 0, 0)
        return jnp.sum(got.astype(jnp.float32), axis=0) + noise[:, None] * probes.astype(jnp.float32)

    return jax.shard_map(
        on_device,
        mesh=mesh,
        in_specs=(P(("row", "col"), None), P(), P(("row", "col")), P(("row", "col"), None)),
        out_specs=P(("row", "col"), None),
        check_vma=False,
    )
```

time: 697 us -> 123 us (0.18)
  waiting for transfers between devices: 574 us -> 0.01 us
  matrix products: 102 us -> 0 us
  blocking collectives: 0 us -> 80.4 us
  Pallas kernels: 0 us -> 33.1 us
  between operations: 13.4 us -> 0.08 us
    all_gather x2 -> x0, waiting for transfers between devices: 574 us -> none  [the longest x1 322 us: on_device(): every = lax.all_gather(scaled, ('row', 'col'), axis=0, tiled=True)]
    dot_general x2 -> x0, matrix products: 102 us -> none  [the longest x1 77.5 us: kernel_tile(): jnp.dot(rows, cols.T, precision=lax.Precision.HIGHEST, preferred_element_...]
    all_to_all x0 -> x3, blocking collectives: none -> 80.4 us  [the longest x1 34.6 us: on_device(): lax.all_to_all(jnp.broadcast_to(packed[None], (chips, *packed.shape)), 'r...]
    pallas_call x0 -> x1, Pallas kernels: none -> 33.1 us  [tile_product(): pl.pallas_call(tile_kernel(block, 1024), in_specs=[vmem] * 3, out_specs=v...]
    reduce_sum x2 -> x1, other arithmetic: 7.37 us -> 0.22 us  [on_device(): jnp.sum(got.astype(jnp.float32), axis=0)]
  transfers between devices with their start and end apart: 2 -> 1, of which waited for: 2 -> 0; matrix products, arithmetic and copies ran while one was open for 12% -> 0% of each run, Pallas kernels for 0% -> 0%
where the time goes in v1:
time: 123 us; the launch traced here: 121 us
  blocking collectives  80.4 us (65%)
  Pallas kernels  33.1 us (27%)
  other arithmetic  5.18 us (4%)
  starting transfers between devices  1.75 us (1%)
    all_to_all x1, blocking collectives, on_device(): lax.all_to_all(jnp.broadcast_to(packed[None], (chips, *packed.shape)), 'r...  34.6 us
    pallas_call x1, Pallas kernels, tile_product(): pl.pallas_call(tile_kernel(block, 1024), in_specs=[vmem] * 3, out_specs=v...  33.1 us
    all_to_all x1, blocking collectives, on_device(): got = lax.all_to_all(sent, 'col', 0, 0)  25.3 us
    all_to_all x1, blocking collectives, on_device(): lax.all_to_all(jnp.broadcast_to(pair[None], (col_size, *pair.shape)), 'co...  20.5 us
  transfers between devices with their start and end apart: 1, of which 0 were waited for; matrix products, arithmetic and copies ran while one was open for 0% of the time, Pallas kernels for 0%

profile of v1, /device:TPU:1, one launch (start us, length us, event | category | flops | bytes accessed | tf_op | source)
XLA Modules:
  0.0 121.2 jit_solution(9398986563365069708)
XLA Ops:
  0.0 1.0 reduce-precision_convert_fusion
  1.0 0.1 copy.7
  1.1 0.1 copy.8
  1.2 1.1 pad_maximum_fusion
  2.3 0.2 broadcast_in_dim.5
  2.5 34.6 %all_to_all.15.mine_ref = bf16[8,384,384]{2,1,0:T(8,128)(2,1)S(1)} all-to-all(bf16[8,384,384]{2,1,0:T(8,128)(2,1)S(1)} %broadcast_in_dim.5), channel_id=1, replica_groups={{0,16,32,48,64,80,96,112},{8,24,40,56,72,88,104,120},{1,17,33,49,65,81,..., dimensions={0} | all-to-all | bytes 4718592 | tf_op jit(solution)/shard_map/all_to_all | solution.py:120
  37.1 0.0 copy-start
  37.1 1.8 %collective-permute-start = (bf16[8,384,384]{2,1,0:T(8,128)(2,1)S(1)}, bf16[8,384,384]{2,1,0:T(8,128)(2,1)}, u32[]{:S(2)}, u32[]{:S(2)}) collective-permute-start(bf16[8,384,384]{2,1,0:T(8,128)(2,1)S(1)} %all_to_all.15.mine_ref), channel_id=1, source_target_pairs={{0,8},{8,0},{16,24},{24,16},{32,40},{40,32},{48,56},{56,48},{64,72... | collective-permute-start | bytes 7077896 | tf_op jit(solution)/shard_map/ppermute | solution.py:123
  38.9 0.1 copy.6
  39.0 0.1 broadcast_in_dim.4
  39.1 20.5 %all_to_all.16.row_ref = bf16[8,384,128]{2,1,0:T(8,128)(2,1)} all-to-all(bf16[8,384,128]{2,1,0:T(8,128)(2,1)S(1)} %broadcast_in_dim.4), channel_id=1, replica_groups=mesh['row'=16,'col'=8] {'col'}, dimensions={0} | all-to-all | bytes 1572864 | tf_op jit(solution)/shard_map/all_to_all | solution.py:119
  59.6 0.0 collective-permute-done.other_ref
  59.6 0.0 copy-done
  59.6 33.1 %tile_product.1 = f32[3072,256]{1,0:T(8,128)} custom-call(bf16[8,384,128]{2,1,0:T(8,128)(2,1)} %all_to_all.16.row_ref, bf16[8,384,384]{2,1,0:T(8,128)(2,1)} %copy-done, bf16[8,384,384]{2,1,0:T(8,128)(2,1)} %collective-permute-done.other_ref), custom_call_target="tpu_custom_call" | custom-call | tf_op jit(solution)/shard_map/tile_product/pallas_call | solution.py:95
  92.7 2.0 %convert_element_type.17 = bf16[3072,256]{1,0:T(8,128)(2,1)S(1)} convert(f32[3072,256]{1,0:T(8,128)} %tile_product.1) | non-fusion elementwise | flops 786432 | bytes 4718592 | tf_op jit(solution)/shard_map/convert_element_type | solution.py:125
  94.7 0.0 copy-start.1
  94.7 0.0 copy-start.2
  94.7 25.3 %all_to_all.17 = bf16[8,384,256]{2,1,0:T(8,128)(2,1)S(1)} all-to-all(bf16[8,384,256]{2,1,0:T(8,128)(2,1)S(1)} %bitcast.1), channel_id=1, replica_groups=mesh['row'=16,'col'=8] {'col'}, dimensions={0} | all-to-all | bytes 3145728 | tf_op jit(solution)/shard_map/all_to_all | solution.py:126
  120.1 0.2 convert_reduce_fusion
  120.3 0.0 copy-done.1
  120.3 0.0 copy-done.2
  120.3 0.9 multiply_add_fusion
  (1 shorter events, 0.0 us)
Async XLA Ops:
  37.1 22.5 %copy-start = (bf16[8,384,384]{2,1,0:T(8,128)(2,1)}, bf16[8,384,384]{2,1,0:T(8,128)(2,1)S(1)}, u32[]{:S(2)}) copy-start(bf16[8,384,384]{2,1,0:T(8,128)(2,1)S(1)} %all_to_all.15.mine_ref) | copy-start | bytes 7077892
  37.1 22.5 %collective-permute-start = (bf16[8,384,384]{2,1,0:T(8,128)(2,1)S(1)}, bf16[8,384,384]{2,1,0:T(8,128)(2,1)}, u32[]{:S(2)}, u32[]{:S(2)}) collective-permute-start(bf16[8,384,384]{2,1,0:T(8,128)(2,1)S(1)} %all_to_all.15.mine_ref), channel_id=1, source_target_pairs={{0,8},{8,0},{16,24},{24,16},{32,40},{40,32},{48,56},{56,48},{64,72... | collective-permute-start | bytes 7077896 | tf_op jit(solution)/shard_map/ppermute | solution.py:123
  94.7 25.6 %copy-start.1 = (bf16[384,256]{1,0:T(8,128)(2,1)S(1)}, bf16[384,256]{1,0:T(8,128)(2,1)}, u32[]{:S(2)}) copy-start(bf16[384,256]{1,0:T(8,128)(2,1)} %param.7) | copy-start | bytes 589828
  94.7 25.6 %copy-start.2 = (f32[384]{0:T(512)S(1)}, f32[384]{0:T(512)}, u32[]{:S(2)}) copy-start(f32[384]{0:T(512)} %param.6) | copy-start | bytes 4612

commit v2 on v0

v2 whole, which is shorter than its diff:
```python
import math

import jax
import jax.numpy as jnp
from jax import lax
from jax.experimental import pallas as pl
from jax.experimental.pallas import tpu as pltpu
from jax.sharding import PartitionSpec as P


ROOT_LOG2E = math.sqrt(math.log2(math.e))
NT = (((1,), (1,)), ((), ()))
LANES = 128
HALF = 64
AXES = ("row", "col")
VMEM = pl.BlockSpec(memory_space=pltpu.VMEM)


def place(x, y, z, core):
    return ((y % 2) * 8 + x * 2 + core) * 8 + (y // 2) * 4 + z


def swap(value, axes, flip):
    flips = flip if isinstance(flip, tuple) else (flip, flip)
    pairs = []
    for x in range(4):
        for y in range(4):
            for z in range(4):
                for core in range(2):
                    to = {"x": x, "y": y, "z": z}
                    to[axes[core]] ^= flips[core]
                    pairs.append((place(x, y, z, core), place(to["x"], to["y"], to["z"], core)))
    return lax.ppermute(value, AXES, pairs)


def partner(value):
    return lax.ppermute(value, AXES, [(i, i ^ 8) for i in range(128)])


def augment(pair, is_col):
    count = pair.shape[0]
    wide = pair.astype(jnp.float32)
    swapped = pltpu.roll(wide, HALF, 1)
    whole = wide + swapped
    norm = jnp.sum(whole * whole, axis=1, keepdims=True) * -0.25
    first = norm.astype(jnp.bfloat16).astype(jnp.float32)
    rest = norm - first
    second = rest.astype(jnp.bfloat16).astype(jnp.float32)
    third = rest - second
    lane = lax.broadcasted_iota(jnp.int32, (count, LANES), 1)
    at, ones = (HALF + 3, HALF) if is_col else (HALF, HALF + 3)
    extra = jnp.where((lane >= ones) & (lane < ones + 3), 1.0, 0.0)
    extra = jnp.where(lane == at, first, extra)
    extra = jnp.where(lane == at + 1, second, extra)
    extra = jnp.where(lane == at + 2, third, extra)
    low = lane < HALF
    if is_col:
        return pair, jnp.where(low, wide, extra).astype(jnp.bfloat16)
    return jnp.where(low, wide, swapped).astype(jnp.bfloat16), jnp.where(low, swapped, extra).astype(jnp.bfloat16)


def pack_own(embeddings_t, inv_length, probes):
    block, width = probes.shape

    def body(emb_hbm, inv_hbm, probe_hbm, own_ref, pair_ref, emb_ref, inv_ref, sems):
        copies = [
            pltpu.make_async_copy(emb_hbm, emb_ref, sems.at[0]),
            pltpu.make_async_copy(inv_hbm, inv_ref, sems.at[1]),
            pltpu.make_async_copy(probe_hbm, own_ref.at[:, LANES:], sems.at[2]),
        ]
        for copy in copies:
            copy.start()
        copies[0].wait()
        copies[1].wait()
        emb = emb_ref[...]
        twice = jnp.concatenate([emb, emb], axis=0).T
        inv = inv_ref[...]
        scaled = (twice * jnp.concatenate([inv, inv], axis=1)) * ROOT_LOG2E
        high = scaled.astype(jnp.bfloat16).astype(jnp.float32)
        lane = lax.broadcasted_iota(jnp.int32, (block, LANES), 1)
        pair = jnp.where(lane < HALF, high, scaled - high).astype(jnp.bfloat16)
        pair_ref[...] = pair
        own_ref[:, :LANES] = pair
        copies[2].wait()

    return pl.pallas_call(
        body,
        in_specs=[pl.BlockSpec(memory_space=pltpu.HBM)] * 3,
        out_specs=[VMEM] * 2,
        out_shape=[
            jax.ShapeDtypeStruct((block, LANES + width), jnp.bfloat16),
            jax.ShapeDtypeStruct((block, LANES), jnp.bfloat16),
        ],
        scratch_shapes=[
            pltpu.VMEM(embeddings_t.shape, jnp.float32),
            pltpu.VMEM(inv_length.shape, jnp.float32),
            pltpu.SemaphoreType.DMA((3,)),
        ],
        compiler_params=pltpu.CompilerParams(vmem_limit_bytes=8 << 20),
        name="pack_own",
    )(embeddings_t, inv_length, probes)


def join(a, b):
    def body(a_ref, b_ref, out_ref):
        out_ref[: a.shape[0], :] = a_ref[...]
        out_ref[a.shape[0] :, :] = b_ref[...]

    return pl.pallas_call(
        body,
        in_specs=[VMEM] * 2,
        out_specs=VMEM,
        out_shape=jax.ShapeDtypeStruct((a.shape[0] + b.shape[0], a.shape[1]), a.dtype),
        compiler_params=pltpu.CompilerParams(vmem_limit_bytes=8 << 20),
    )(a, b)


def prepare_rows(block, sources, groups):
    def body(*refs):
        ins, outs = refs[: len(sources)], refs[len(sources) :]
        for group, out in zip(groups, outs, strict=True):
            for i, (source, k) in enumerate(group):
                a, b = augment(ins[source][k * block : (k + 1) * block, :], False)
                out[i * block : (i + 1) * block, :LANES] = a
                out[i * block : (i + 1) * block, LANES:] = b

    return pl.pallas_call(
        body,
        in_specs=[VMEM] * len(sources),
        out_specs=[VMEM] * len(groups),
        out_shape=[jax.ShapeDtypeStruct((len(g) * block, 2 * LANES), jnp.bfloat16) for g in groups],
        compiler_params=pltpu.CompilerParams(vmem_limit_bytes=12 << 20),
        name="prepare_rows",
    )(*sources)


def params(mib):
    return pltpu.CompilerParams(vmem_limit_bytes=mib << 20)


def cost(rows, cols, width):
    return pl.CostEstimate(
        flops=4 * rows * cols * 2 * LANES, transcendentals=rows * cols, bytes_accessed=4 * rows * width
    )


def fold(row_ref, at, column, probe):
    gram = lax.dot_general(row_ref[at, :], column, NT, preferred_element_type=jnp.float32)
    return jnp.dot(jnp.exp2(gram).astype(jnp.bfloat16), probe, preferred_element_type=jnp.float32)


def accumulate(rows, olds, packs, steps):
    block = 384
    width = packs[0].shape[1] - LANES
    n, m, p = len(rows), len(olds), len(packs)
    cols = sum(q.shape[0] for q in packs)

    def body(*refs):
        row_refs, old_refs, pack_refs = refs[:n], refs[n : n + m], refs[n + m : n + m + p]
        out_refs, (right, probes) = refs[n + m + p : -2], refs[-2:]
        start = 0
        for src in pack_refs:
            for k in range(0, src.shape[0], block):
                a, b = augment(src[k : k + block, :LANES], True)
                right[start : start + block, :LANES] = a
                right[start : start + block, LANES:] = b
                probes[start : start + block, :] = src[k : k + block, LANES:]
                start += block
        for k in range(n):
            step = steps[k]

            def one(i, carry):
                at = pl.ds(pl.multiple_of(i * step, step), step)
                part = fold(row_refs[k], at, right[...], probes[...])
                out_refs[k][at, :] = old_refs[k][at, :] + part if m else part
                return carry

            lax.fori_loop(0, rows[k].shape[0] // step, one, 0)

    return pl.pallas_call(
        body,
        in_specs=[VMEM] * (n + m + p),
        out_specs=[VMEM] * (n + 2),
        out_shape=[jax.ShapeDtypeStruct((r.shape[0], width), jnp.float32) for r in rows]
        + [jax.ShapeDtypeStruct((cols, 2 * LANES), jnp.bfloat16), jax.ShapeDtypeStruct((cols, width), jnp.bfloat16)],
        input_output_aliases={n + i: i for i in range(m)},
        cost_estimate=cost(sum(r.shape[0] for r in rows), cols, width),
        compiler_params=params(28),
    )(*rows, *olds, *packs)


def apply_rows(rows, old, columns, step):
    count, width = rows.shape[0], columns[0][1].shape[1]
    flat = [a for pair in columns for a in pair]
    lead = [rows] if old is None else [rows, old]

    def body(*refs):
        row_ref, out_ref, rest = refs[0], refs[-1], refs[len(lead) : -1]

        def one(i, carry):
            at = pl.ds(pl.multiple_of(i * step, step), step)
            part = None if old is None else refs[1][at, :]
            for k in range(0, len(rest), 2):
                more = fold(row_ref, at, rest[k][...], rest[k + 1][...])
                part = more if part is None else part + more
            out_ref[at, :] = part
            return carry

        lax.fori_loop(0, count // step, one, 0)

    return pl.pallas_call(
        body,
        in_specs=[VMEM] * (len(lead) + len(flat)),
        out_specs=VMEM,
        out_shape=jax.ShapeDtypeStruct((count, width), jnp.float32),
        input_output_aliases={} if old is None else {1: 0},
        cost_estimate=cost(count, sum(c[0].shape[0] for c in columns), width),
        compiler_params=params(28),
    )(*lead, *flat)


def on_device(embeddings, inv_length, noise, probes):
    block = probes.shape[0]
    own, pair = pack_own(embeddings.T, inv_length[None, :], probes)

    first_axis, second_axis = ("x", "y"), ("y", "x")
    beside = swap(own, first_axis, 1)
    rows_a = swap(pair, "zz", (1, 3))
    pairs = join(pair, rows_a)
    rows_b = swap(pairs, "zz", (3, 1))
    pack_a = join(own, beside)
    pack_b = swap(pack_a, first_axis, 3)
    pack_c = swap(pack_a, second_axis, 1)
    pack_d = swap(pack_a, second_axis, 3)
    other_pairs = partner(pairs)
    other_b = partner(rows_b)
    row_far, row_near, row_own = prepare_rows(
        block,
        [pairs, rows_b, other_pairs, other_b],
        [[(2, 0), (2, 1), (3, 1), (3, 0)], [(0, 1), (1, 1), (1, 0)], [(0, 0)]],
    )
    rows, steps = [row_far, row_near], (768, 1152)
    far, near, right_a, probes_a = accumulate(rows, [], [pack_a], steps)

    pack_e = swap(pack_b, second_axis, 1)
    pack_f = swap(pack_b, second_axis, 3)
    pack_g = swap(pack_d, second_axis, 1)
    far, near, right_b, probes_b = accumulate(rows, [far, near], [pack_b, pack_c], steps)

    pack_h = swap(pack_e, second_axis, 3)
    far, near, right_c, probes_c = accumulate(rows, [far, near], [pack_d, pack_e], steps)

    last = [pack_f, pack_g, pack_h]
    far, right_d, probes_d = accumulate([row_far], [far], last, (768,))
    got = partner(far)
    near = apply_rows(row_near, near, [(right_d, probes_d)], 1152)
    sums = near + got[block:]
    in_a = swap(sums[: 2 * block].astype(jnp.bfloat16), "zz", (1, 3))
    columns = [(right_a, probes_a), (right_b, probes_b), (right_c, probes_c), (right_d, probes_d)]
    own_sum = apply_rows(row_own, None, columns, 384)
    passed = (sums[2 * block :] + in_a[block:].astype(jnp.float32)).astype(jnp.bfloat16)
    in_b = swap(passed, "zz", (3, 1))
    result = own_sum + got[:block] + noise[:, None] * probes.astype(jnp.float32)
    return result + in_a[:block].astype(jnp.float32) + in_b.astype(jnp.float32)


def solution(mesh):
    return jax.shard_map(
        on_device,
        mesh=mesh,
        in_specs=(P(("row", "col"), None), P(), P(("row", "col")), P(("row", "col"), None)),
        out_specs=P(("row", "col"), None),
        check_vma=False,
    )
```

time: 697 us -> 78.9 us (0.11)
  waiting for transfers between devices: 574 us -> 18.4 us
  matrix products: 102 us -> 0 us
  Pallas kernels: 0 us -> 28.7 us
  starting transfers between devices: 0.04 us -> 26.9 us
  between operations: 13.4 us -> 0.19 us
    all_gather x2 -> x0, waiting for transfers between devices: 574 us -> none  [the longest x1 322 us: on_device(): every = lax.all_gather(scaled, ('row', 'col'), axis=0, tiled=True)]
    dot_general x2 -> x0, matrix products: 102 us -> none  [the longest x1 77.5 us: kernel_tile(): jnp.dot(rows, cols.T, precision=lax.Precision.HIGHEST, preferred_element_...]
    pallas_call x0 -> x10, Pallas kernels: none -> 28.7 us  [the longest x4 20.8 us: accumulate(): pl.pallas_call(body, in_specs=[VMEM] * (n + m + p), out_specs=[VMEM] * (n...]
    ppermute x0 -> x15, starting transfers between devices: none -> 26.9 us  [the longest x12 17 us: swap(): return lax.ppermute(value, AXES, pairs)]
    ppermute x0 -> x15, waiting for transfers between devices: none -> 18.4 us  [the longest x12 17 us: swap(): return lax.ppermute(value, AXES, pairs)]
    reduce_sum x2 -> x0, other arithmetic: 7.37 us -> none  [the longest x1 5.75 us: on_device(): every_sq = jnp.sum(every * every, axis=1)]
  transfers between devices with their start and end apart: 2 -> 15, of which waited for: 2 -> 7; matrix products, arithmetic and copies ran while one was open for 12% -> 0% of each run, Pallas kernels for 0% -> 30%
where the time goes in v2:
time: 78.9 us; the launch traced here: 77.9 us
  Pallas kernels  28.7 us (36%)
  starting transfers between devices  26.9 us (34%)
  waiting for transfers between devices  18.4 us (23%)
  local copies, waits for them, and re-layouts  2.53 us (3%)
  other arithmetic  1.11 us (1%)
    pallas_call x4, Pallas kernels, accumulate(): pl.pallas_call(body, in_specs=[VMEM] * (n + m + p), out_specs=[VMEM] * (n...  20.8 us
    ppermute x12, starting transfers between devices, swap(): return lax.ppermute(value, AXES, pairs)  17 us
    ppermute x12, waiting for transfers between devices, swap(): return lax.ppermute(value, AXES, pairs)  17 us
    ppermute x3, starting transfers between devices, partner(): return lax.ppermute(value, AXES, [(i, i ^ 8) for i in range(128)])  9.89 us
    pallas_call x2, Pallas kernels, apply_rows(): pl.pallas_call(body, in_specs=[VMEM] * (len(lead) + len(flat)), out_specs...  6.2 us
    unnamed x10, local copies, waits for them, and re-layouts  2.49 us
  transfers between devices with their start and end apart: 15, of which 7 were waited for; matrix products, arithmetic and copies ran while one was open for 0% of the time, Pallas kernels for 30%

profile of v2, /device:TPU:1, one launch (start us, length us, event | category | flops | bytes accessed | tf_op | source)
XLA Modules:
  0.0 77.9 jit_solution(3605017073823859107)
XLA Ops:
  0.0 0.0 copy-start
  0.0 0.9 %copy-done = bf16[384,256]{1,0:T(8,128)(2,1)S(1)} copy-done((bf16[384,256]{1,0:T(8,128)(2,1)S(1)}, bf16[384,256]{1,0:T(8,128)(2,1)}, u32[]{:S(2)}) %copy-start) | copy-done | bytes 196632
  0.9 0.0 copy-start.2
  0.9 0.9 %copy-done.2 = f32[384,64]{0,1:T(8,128)S(1)} copy-done((f32[384,64]{0,1:T(8,128)S(1)}, f32[384,64]{0,1:T(8,128)}, u32[]{:S(2)}) %copy-start.2) | copy-done | bytes 98328
  1.8 0.0 copy-start.3
  1.8 0.7 copy-done.3
  2.5 0.3 pack_own.1
  2.8 2.2 %collective-permute-start.4 = (bf16[384,384]{1,0:T(8,128)(2,1)S(1)}, bf16[384,384]{1,0:T(8,128)(2,1)S(1)}, u32[]{:S(2)}, u32[]{:S(2)}) collective-permute-start(bf16[384,384]{1,0:T(8,128)(2,1)S(1)} %get-tuple-element.29.a_ref), channel_id=1, source_target_pairs={{0,16},{8,72},{1,17},{9,73},{2,18},{10,74},{3,19},{11,75},{64,80},... | collective-permute-start | bytes 884744 | tf_op jit(solution)/shard_map/ppermute | solution.py:33
  5.0 4.4 %collective-permute-done.4.b_ref = bf16[384,384]{1,0:T(8,128)(2,1)S(1)} collective-permute-done((bf16[384,384]{1,0:T(8,128)(2,1)S(1)}, bf16[384,384]{1,0:T(8,128)(2,1)S(1)}, u32[]{:S(2)}, u32[]{:S(2)}) %collective-permute-start.4) | collective-permute-done | bytes 294944 | tf_op jit(solution)/shard_map/ppermute | solution.py:33
  9.4 0.1 shard_map.47.refs_2_
  9.5 3.0 %collective-permute-start.5 = (bf16[768,384]{1,0:T(8,128)(2,1)S(1)}, bf16[768,384]{1,0:T(8,128)(2,1)S(1)}, u32[]{:S(2)}, u32[]{:S(2)}) collective-permute-start(bf16[768,384]{1,0:T(8,128)(2,1)S(1)} %shard_map.47.refs_2_), channel_id=1, source_target_pairs={{0,48},{8,76},{1,49},{9,77},{2,50},{10,78},{3,51},{11,79},{64,112}... | collective-permute-start | bytes 1769480 | tf_op jit(solution)/shard_map/ppermute | solution.py:33
  12.4 3.8 %collective-permute-start = (bf16[384,128]{1,0:T(8,128)(2,1)S(1)}, bf16[384,128]{1,0:T(8,128)(2,1)S(1)}, u32[]{:S(2)}, u32[]{:S(2)}) collective-permute-start(bf16[384,128]{1,0:T(8,128)(2,1)S(1)} %get-tuple-element.25.a_ref), channel_id=1, source_target_pairs={{0,1},{8,11},{1,0},{9,10},{2,3},{10,9},{3,2},{11,8},{64,65},{72,75... | collective-permute-start | bytes 294920 | tf_op jit(solution)/shard_map/ppermute | solution.py:33
  16.2 2.3 %collective-permute-done.b_ref = bf16[384,128]{1,0:T(8,128)(2,1)S(1)} collective-permute-done((bf16[384,128]{1,0:T(8,128)(2,1)S(1)}, bf16[384,128]{1,0:T(8,128)(2,1)S(1)}, u32[]{:S(2)}, u32[]{:S(2)}) %collective-permute-start) | collective-permute-done | bytes 98336 | tf_op jit(solution)/shard_map/ppermute | solution.py:33
  18.5 0.1 collective-permute-start.1
  18.6 2.6 %collective-permute-start.7 = (bf16[768,384]{1,0:T(8,128)(2,1)S(1)}, bf16[768,384]{1,0:T(8,128)(2,1)S(1)}, u32[]{:S(2)}, u32[]{:S(2)}) collective-permute-start(bf16[768,384]{1,0:T(8,128)(2,1)S(1)} %shard_map.47.refs_2_), channel_id=1, source_target_pairs={{0,68},{8,56},{1,69},{9,57},{2,70},{10,58},{3,71},{11,59},{64,4},{... | collective-permute-start | bytes 1769480 | tf_op jit(solution)/shard_map/ppermute | solution.py:33
  21.2 0.0 collective-permute-done.5.refs_4_
  21.2 0.0 collective-permute-start.8
  21.2 1.5 %collective-permute-start.6 = (bf16[768,384]{1,0:T(8,128)(2,1)S(1)}, bf16[768,384]{1,0:T(8,128)(2,1)S(1)}, u32[]{:S(2)}, u32[]{:S(2)}) collective-permute-start(bf16[768,384]{1,0:T(8,128)(2,1)S(1)} %shard_map.47.refs_2_), channel_id=1, source_target_pairs={{0,64},{8,24},{1,65},{9,25},{2,66},{10,26},{3,67},{11,27},{64,0},{... | collective-permute-start | bytes 1769480 | tf_op jit(solution)/shard_map/ppermute | solution.py:33
  22.6 6.1 %collective-permute-start.2 = (bf16[768,128]{1,0:T(8,128)(2,1)S(1)}, bf16[768,128]{1,0:T(8,128)(2,1)S(1)}, u32[]{:S(2)}, u32[]{:S(2)}) collective-permute-start(bf16[768,128]{1,0:T(8,128)(2,1)S(1)} %shard_map.46.refs_0_), channel_id=1, source_target_pairs={{0,8},{1,9},{2,10},{3,11},{4,12},{5,13},{6,14},{7,15},{8,0},{9,1},... | collective-permute-start | bytes 589832 | tf_op jit(solution)/shard_map/ppermute | solution.py:37
  28.7 0.0 collective-permute-done.1.refs_1_
  28.7 0.0 collective-permute-start.3
  28.7 1.1 %collective-permute-done.2.refs_2_ = bf16[768,128]{1,0:T(8,128)(2,1)S(1)} collective-permute-done((bf16[768,128]{1,0:T(8,128)(2,1)S(1)}, bf16[768,128]{1,0:T(8,128)(2,1)S(1)}, u32[]{:S(2)}, u32[]{:S(2)}) %collective-permute-start.2) | collective-permute-done | bytes 196640 | tf_op jit(solution)/shard_map/ppermute | solution.py:37
  29.8 0.4 collective-permute-done.3.refs_3_
  30.2 1.3 %prepare_rows.1 = (bf16[1536,256]{1,0:T(8,128)(2,1)S(1)}, bf16[1152,256]{1,0:T(8,128)(2,1)S(1)}, bf16[384,256]{1,0:T(8,128)(2,1)S(1)}) custom-call(bf16[768,128]{1,0:T(8,128)(2,1)S(1)} %shard_map.46.refs_0_, bf16[768,128]{1,0:T(8,128)(2,1)S(1)} %collective-permute-done.1.refs_1_, bf16[768,128]{1,0:T(8,128)(2,1)S(1)} %collective-permute-done.2.refs_2_, ...), custom_call_target="tpu_custom_call" | custom-call | tf_op jit(solution)/shard_map/prepare_rows/pallas_call | solution.py:127
  31.5 3.4 %shard_map.48 = (f32[1536,256]{1,0:T(8,128)S(1)}, f32[1152,256]{1,0:T(8,128)S(1)}, bf16[768,256]{1,0:T(8,128)(2,1)S(1)}, bf16[768,256]{1,0:T(8,128)(2,1)S(1)}) custom-call(bf16[1536,256]{1,0:T(8,128)(2,1)S(1)} %get-tuple-element.27.refs_0_, bf16[1152,256]{1,0:T(8,128)(2,1)S(1)} %get-tuple-element.28.refs_1_.refs_0_, bf16[768,384]{1,0:T(8,128)(2,1)S(1)} %shard_map.47.refs_2_), custom_call_target="tpu_custom_call" | custom-call | flops 2113929216 | bytes 2752512 | tf_op jit(solution)/shard_map/pallas_call | solution.py:180
  34.9 0.1 collective-permute-start.9
  35.0 0.0 collective-permute-done.7.refs_4_
  35.0 0.1 collective-permute-start.10
  35.1 0.0 collective-permute-done.8.refs_5_
  35.1 2.8 %collective-permute-start.11 = (bf16[768,384]{1,0:T(8,128)(2,1)S(1)}, bf16[768,384]{1,0:T(8,128)(2,1)S(1)}, u32[]{:S(2)}, u32[]{:S(2)}) collective-permute-start(bf16[768,384]{1,0:T(8,128)(2,1)S(1)} %collective-permute-done.8.refs_5_), channel_id=1, source_target_pairs={{0,68},{8,56},{1,69},{9,57},{2,70},{10,58},{3,71},{11,59},{64,4},{... | collective-permute-start | bytes 1769480 | tf_op jit(solution)/shard_map/ppermute | solution.py:33
  37.9 0.0 collective-permute-done.6.refs_5_
  37.9 6.0 %shard_map.49 = (f32[1536,256]{1,0:T(8,128)S(1)}, f32[1152,256]{1,0:T(8,128)S(1)}, bf16[1536,256]{1,0:T(8,128)(2,1)S(1)}, bf16[1536,256]{1,0:T(8,128)(2,1)S(1)}) custom-call(bf16[1536,256]{1,0:T(8,128)(2,1)S(1)} %get-tuple-element.27.refs_0_, bf16[1152,256]{1,0:T(8,128)(2,1)S(1)} %get-tuple-element.28.refs_1_.refs_0_, ...), custom_call_target="tpu_custom_call", output_to_operand_aliasing={{0}: (2, {}), {1}: (3, {})} | custom-call | flops 4227858432 | bytes 2752512 | tf_op jit(solution)/shard_map/pallas_call | solution.py:180
  44.0 6.0 %shard_map.50 = (f32[1536,256]{1,0:T(8,128)S(1)}, f32[1152,256]{1,0:T(8,128)S(1)}, bf16[1536,256]{1,0:T(8,128)(2,1)S(1)}, bf16[1536,256]{1,0:T(8,128)(2,1)S(1)}) custom-call(bf16[1536,256]{1,0:T(8,128)(2,1)S(1)} %get-tuple-element.27.refs_0_, bf16[1152,256]{1,0:T(8,128)(2,1)S(1)} %get-tuple-element.28.refs_1_.refs_0_, ...), custom_call_target="tpu_custom_call", output_to_operand_aliasing={{0}: (2, {}), {1}: (3, {})} | custom-call | flops 4227858432 | bytes 2752512 | tf_op jit(solution)/shard_map/pallas_call | solution.py:180
  50.0 0.0 collective-permute-done.10.refs_3_
  50.0 0.0 collective-permute-done.9.refs_2_
  50.0 1.5 %collective-permute-done.11.refs_4_ = bf16[768,384]{1,0:T(8,128)(2,1)S(1)} collective-permute-done((bf16[768,384]{1,0:T(8,128)(2,1)S(1)}, bf16[768,384]{1,0:T(8,128)(2,1)S(1)}, u32[]{:S(2)}, u32[]{:S(2)}) %collective-permute-start.11) | collective-permute-done | bytes 589856 | tf_op jit(solution)/shard_map/ppermute | solution.py:33
  51.5 5.4 %shard_map.51 = (f32[1536,256]{1,0:T(8,128)S(1)}, bf16[2304,256]{1,0:T(8,128)(2,1)S(1)}, bf16[2304,256]{1,0:T(8,128)(2,1)S(1)}) custom-call(bf16[1536,256]{1,0:T(8,128)(2,1)S(1)} %get-tuple-element.27.refs_0_, f32[1536,256]{1,0:T(8,128)S(1)} %get-tuple-element.40.refs_1_, ...), custom_call_target="tpu_custom_call", output_to_operand_aliasing={{0}: (1, {})} | custom-call | flops 3623878656 | bytes 1572864 | tf_op jit(solution)/shard_map/pallas_call | solution.py:180
  56.9 3.8 %collective-permute-start.12 = (f32[1536,256]{1,0:T(8,128)S(1)}, f32[1536,256]{1,0:T(8,128)S(1)}, u32[]{:S(2)}, u32[]{:S(2)}) collective-permute-start(f32[1536,256]{1,0:T(8,128)S(1)} %get-tuple-element.43), channel_id=1, source_target_pairs={{0,8},{1,9},{2,10},{3,11},{4,12},{5,13},{6,14},{7,15},{8,0},{9,1},... | collective-permute-start | bytes 4718600 | tf_op jit(solution)/shard_map/ppermute | solution.py:37
  60.7 3.1 %shard_map.53 = f32[1152,256]{1,0:T(8,128)S(1)} custom-call(bf16[1152,256]{1,0:T(8,128)(2,1)S(1)} %get-tuple-element.28.refs_1_.refs_0_, f32[1152,256]{1,0:T(8,128)S(1)} %get-tuple-element.44.refs_1_, bf16[2304,256]{1,0:T(8,128)(2,1)S(1)} %get-tuple-element.41.refs_7_.refs_2_, ...), custom_call_target="tpu_custom_call", output_to_operand_aliasing={{}: (1, {})} | custom-call | flops 2717908992 | bytes 1179648 | tf_op jit(solution)/shard_map/pallas_call | solution.py:211
  63.9 0.0 collective-permute-done.12
  63.9 0.2 slice_add_fusion
  64.1 0.9 %collective-permute-start.13 = (bf16[768,256]{1,0:T(8,128)(2,1)S(1)}, bf16[768,256]{1,0:T(8,128)(2,1)S(1)}, u32[]{:S(2)}, u32[]{:S(2)}) collective-permute-start(bf16[768,256]{1,0:T(8,128)(2,1)S(1)} %slice.45), channel_id=1, source_target_pairs={{0,1},{8,11},{1,0},{9,10},{2,3},{10,9},{3,2},{11,8},{64,65},{72,75... | collective-permute-start | bytes 1179656 | tf_op jit(solution)/shard_map/ppermute | solution.py:33
  64.9 7.0 %collective-permute-done.13 = bf16[768,256]{1,0:T(8,128)(2,1)S(1)} collective-permute-done((bf16[768,256]{1,0:T(8,128)(2,1)S(1)}, bf16[768,256]{1,0:T(8,128)(2,1)S(1)}, u32[]{:S(2)}, u32[]{:S(2)}) %collective-permute-start.13) | collective-permute-done | bytes 393248 | tf_op jit(solution)/shard_map/ppermute | solution.py:33
  72.0 0.1 collective-permute-start.14
  72.1 0.0 copy-start.1
  72.1 0.0 copy-start.4
  72.2 3.1 %shard_map.52 = f32[384,256]{1,0:T(8,128)S(1)} custom-call(bf16[384,256]{1,0:T(8,128)(2,1)S(1)} %get-tuple-element.26.refs_0_, bf16[768,256]{1,0:T(8,128)(2,1)S(1)} %get-tuple-element.30.refs_1_, bf16[768,256]{1,0:T(8,128)(2,1)S(1)} %get-tuple-element.31.refs_2_, bf16[1536,256]{1,0:T(8,128)(2,1)S(1)} %get-tuple-element.34.refs_3_, ...), custom_call_target="tpu_custom_call" | custom-call | flops 2415919104 | bytes 393216 | tf_op jit(solution)/shard_map/pallas_call | solution.py:211
  75.2 1.7 %collective-permute-done.14 = bf16[384,256]{1,0:T(8,128)(2,1)S(1)} collective-permute-done((bf16[384,256]{1,0:T(8,128)(2,1)S(1)}, bf16[384,256]{1,0:T(8,128)(2,1)S(1)}, u32[]{:S(2)}, u32[]{:S(2)}) %collective-permute-start.14) | collective-permute-done | bytes 196640 | tf_op jit(solution)/shard_map/ppermute | solution.py:33
  76.9 0.0 copy-done.1
  76.9 0.0 copy-done.4
  76.9 0.9 %fusion.3 = f32[384,256]{1,0:T(8,128)} fusion(f32[384,256]{1,0:T(8,128)S(1)} %shard_map.52, f32[1536,256]{1,0:T(8,128)S(1)} %collective-permute-done.12, bf16[384,256]{1,0:T(8,128)(2,1)S(1)} %collective-permute-done.14, bf16[384,256]{1,0:T(8,128)(2,1)S(1)} %copy-done.1, bf16[768,256]{1,0:T(8,128)(2,1)S(1)} %collective-permute-done.13, f32[384]{0:T(512)S(1)} %copy-done.4), kind=kLoop, calls=%fused_computation.7 | loop fusion | flops 786432 | bytes 1771008 | tf_op jit(solution)/shard_map/add | solution.py:264
  (3 shorter events, 0.1 us)
Async XLA Ops:
  0.0 0.9 %copy-start = (bf16[384,256]{1,0:T(8,128)(2,1)S(1)}, bf16[384,256]{1,0:T(8,128)(2,1)}, u32[]{:S(2)}) copy-start(bf16[384,256]{1,0:T(8,128)(2,1)} %probe_hbm.1) | copy-start | bytes 589828
  0.9 0.9 %copy-start.2 = (f32[384,64]{0,1:T(8,128)S(1)}, f32[384,64]{0,1:T(8,128)}, u32[]{:S(2)}) copy-start(f32[384,64]{0,1:T(8,128)} %param.4) | copy-start | bytes 294916
  1.8 0.7 copy-start.3
  2.8 6.6 %collective-permute-start.4 = (bf16[384,384]{1,0:T(8,128)(2,1)S(1)}, bf16[384,384]{1,0:T(8,128)(2,1)S(1)}, u32[]{:S(2)}, u32[]{:S(2)}) collective-permute-start(bf16[384,384]{1,0:T(8,128)(2,1)S(1)} %get-tuple-element.29.a_ref), channel_id=1, source_target_pairs={{0,16},{8,72},{1,17},{9,73},{2,18},{10,74},{3,19},{11,75},{64,80},... | collective-permute-start | bytes 884744 | tf_op jit(solution)/shard_map/ppermute | solution.py:33
  9.5 11.7 %collective-permute-start.5 = (bf16[768,384]{1,0:T(8,128)(2,1)S(1)}, bf16[768,384]{1,0:T(8,128)(2,1)S(1)}, u32[]{:S(2)}, u32[]{:S(2)}) collective-permute-start(bf16[768,384]{1,0:T(8,128)(2,1)S(1)} %shard_map.47.refs_2_), channel_id=1, source_target_pairs={{0,48},{8,76},{1,49},{9,77},{2,50},{10,78},{3,51},{11,79},{64,112}... | collective-permute-start | bytes 1769480 | tf_op jit(solution)/shard_map/ppermute | solution.py:33
  12.4 6.1 %collective-permute-start = (bf16[384,128]{1,0:T(8,128)(2,1)S(1)}, bf16[384,128]{1,0:T(8,128)(2,1)S(1)}, u32[]{:S(2)}, u32[]{:S(2)}) collective-permute-start(bf16[384,128]{1,0:T(8,128)(2,1)S(1)} %get-tuple-element.25.a_ref), channel_id=1, source_target_pairs={{0,1},{8,11},{1,0},{9,10},{2,3},{10,9},{3,2},{11,8},{64,65},{72,75... | collective-permute-start | bytes 294920 | tf_op jit(solution)/shard_map/ppermute | solution.py:33
  18.5 10.2 %collective-permute-start.1 = (bf16[768,128]{1,0:T(8,128)(2,1)S(1)}, bf16[768,128]{1,0:T(8,128)(2,1)S(1)}, u32[]{:S(2)}, u32[]{:S(2)}) collective-permute-start(bf16[768,128]{1,0:T(8,128)(2,1)S(1)} %shard_map.46.refs_0_), channel_id=1, source_target_pairs={{0,3},{8,9},{1,2},{9,8},{2,1},{10,11},{3,0},{11,10},{64,67},{72,73... | collective-permute-start | bytes 589832 | tf_op jit(solution)/shard_map/ppermute | solution.py:33
  18.6 16.4 %collective-permute-start.7 = (bf16[768,384]{1,0:T(8,128)(2,1)S(1)}, bf16[768,384]{1,0:T(8,128)(2,1)S(1)}, u32[]{:S(2)}, u32[]{:S(2)}) collective-permute-start(bf16[768,384]{1,0:T(8,128)(2,1)S(1)} %shard_map.47.refs_2_), channel_id=1, source_target_pairs={{0,68},{8,56},{1,69},{9,57},{2,70},{10,58},{3,71},{11,59},{64,4},{... | collective-permute-start | bytes 1769480 | tf_op jit(solution)/shard_map/ppermute | solution.py:33
  21.2 13.9 %collective-permute-start.8 = (bf16[768,384]{1,0:T(8,128)(2,1)S(1)}, bf16[768,384]{1,0:T(8,128)(2,1)S(1)}, u32[]{:S(2)}, u32[]{:S(2)}) collective-permute-start(bf16[768,384]{1,0:T(8,128)(2,1)S(1)} %collective-permute-done.5.refs_4_), channel_id=1, source_target_pairs={{0,64},{8,24},{1,65},{9,25},{2,66},{10,26},{3,67},{11,27},{64,0},{... | collective-permute-start | bytes 1769480 | tf_op jit(solution)/shard_map/ppermute | solution.py:33
  21.2 16.7 %collective-permute-start.6 = (bf16[768,384]{1,0:T(8,128)(2,1)S(1)}, bf16[768,384]{1,0:T(8,128)(2,1)S(1)}, u32[]{:S(2)}, u32[]{:S(2)}) collective-permute-start(bf16[768,384]{1,0:T(8,128)(2,1)S(1)} %shard_map.47.refs_2_), channel_id=1, source_target_pairs={{0,64},{8,24},{1,65},{9,25},{2,66},{10,26},{3,67},{11,27},{64,0},{... | collective-permute-start | bytes 1769480 | tf_op jit(solution)/shard_map/ppermute | solution.py:33
  22.6 7.2 %collective-permute-start.2 = (bf16[768,128]{1,0:T(8,128)(2,1)S(1)}, bf16[768,128]{1,0:T(8,128)(2,1)S(1)}, u32[]{:S(2)}, u32[]{:S(2)}) collective-permute-start(bf16[768,128]{1,0:T(8,128)(2,1)S(1)} %shard_map.46.refs_0_), channel_id=1, source_target_pairs={{0,8},{1,9},{2,10},{3,11},{4,12},{5,13},{6,14},{7,15},{8,0},{9,1},... | collective-permute-start | bytes 589832 | tf_op jit(solution)/shard_map/ppermute | solution.py:37
  28.7 1.4 %collective-permute-start.3 = (bf16[768,128]{1,0:T(8,128)(2,1)S(1)}, bf16[768,128]{1,0:T(8,128)(2,1)S(1)}, u32[]{:S(2)}, u32[]{:S(2)}) collective-permute-start(bf16[768,128]{1,0:T(8,128)(2,1)S(1)} %collective-permute-done.1.refs_1_), channel_id=1, source_target_pairs={{0,8},{1,9},{2,10},{3,11},{4,12},{5,13},{6,14},{7,15},{8,0},{9,1},... | collective-permute-start | bytes 589832 | tf_op jit(solution)/shard_map/ppermute | solution.py:37
  34.9 15.1 %collective-permute-start.9 = (bf16[768,384]{1,0:T(8,128)(2,1)S(1)}, bf16[768,384]{1,0:T(8,128)(2,1)S(1)}, u32[]{:S(2)}, u32[]{:S(2)}) collective-permute-start(bf16[768,384]{1,0:T(8,128)(2,1)S(1)} %collective-permute-done.5.refs_4_), channel_id=1, source_target_pairs={{0,68},{8,56},{1,69},{9,57},{2,70},{10,58},{3,71},{11,59},{64,4},{... | collective-permute-start | bytes 1769480 | tf_op jit(solution)/shard_map/ppermute | solution.py:33
  35.0 15.0 %collective-permute-start.10 = (bf16[768,384]{1,0:T(8,128)(2,1)S(1)}, bf16[768,384]{1,0:T(8,128)(2,1)S(1)}, u32[]{:S(2)}, u32[]{:S(2)}) collective-permute-start(bf16[768,384]{1,0:T(8,128)(2,1)S(1)} %collective-permute-done.7.refs_4_), channel_id=1, source_target_pairs={{0,64},{8,24},{1,65},{9,25},{2,66},{10,26},{3,67},{11,27},{64,0},{... | collective-permute-start | bytes 1769480 | tf_op jit(solution)/shard_map/ppermute | solution.py:33
  35.1 16.4 %collective-permute-start.11 = (bf16[768,384]{1,0:T(8,128)(2,1)S(1)}, bf16[768,384]{1,0:T(8,128)(2,1)S(1)}, u32[]{:S(2)}, u32[]{:S(2)}) collective-permute-start(bf16[768,384]{1,0:T(8,128)(2,1)S(1)} %collective-permute-done.8.refs_5_), channel_id=1, source_target_pairs={{0,68},{8,56},{1,69},{9,57},{2,70},{10,58},{3,71},{11,59},{64,4},{... | collective-permute-start | bytes 1769480 | tf_op jit(solution)/shard_map/ppermute | solution.py:33
  56.9 6.9 %collective-permute-start.12 = (f32[1536,256]{1,0:T(8,128)S(1)}, f32[1536,256]{1,0:T(8,128)S(1)}, u32[]{:S(2)}, u32[]{:S(2)}) collective-permute-start(f32[1536,256]{1,0:T(8,128)S(1)} %get-tuple-element.43), channel_id=1, source_target_pairs={{0,8},{1,9},{2,10},{3,11},{4,12},{5,13},{6,14},{7,15},{8,0},{9,1},... | collective-permute-start | bytes 4718600 | tf_op jit(solution)/shard_map/ppermute | solution.py:37
  64.1 7.9 %collective-permute-start.13 = (bf16[768,256]{1,0:T(8,128)(2,1)S(1)}, bf16[768,256]{1,0:T(8,128)(2,1)S(1)}, u32[]{:S(2)}, u32[]{:S(2)}) collective-permute-start(bf16[768,256]{1,0:T(8,128)(2,1)S(1)} %slice.45), channel_id=1, source_target_pairs={{0,1},{8,11},{1,0},{9,10},{2,3},{10,9},{3,2},{11,8},{64,65},{72,75... | collective-permute-start | bytes 1179656 | tf_op jit(solution)/shard_map/ppermute | solution.py:33
  72.0 4.9 %collective-permute-start.14 = (bf16[384,256]{1,0:T(8,128)(2,1)S(1)}, bf16[384,256]{1,0:T(8,128)(2,1)S(1)}, u32[]{:S(2)}, u32[]{:S(2)}) collective-permute-start(bf16[384,256]{1,0:T(8,128)(2,1)S(1)} %fusion), channel_id=1, source_target_pairs={{0,3},{8,9},{1,2},{9,8},{2,1},{10,11},{3,0},{11,10},{64,67},{72,73... | collective-permute-start | bytes 589832 | tf_op jit(solution)/shard_map/ppermute | solution.py:33
  72.1 4.8 %copy-start.1 = (bf16[384,256]{1,0:T(8,128)(2,1)S(1)}, bf16[384,256]{1,0:T(8,128)(2,1)}, u32[]{:S(2)}) copy-start(bf16[384,256]{1,0:T(8,128)(2,1)} %probe_hbm.1) | copy-start | bytes 589828
  72.1 4.8 %copy-start.4 = (f32[384]{0:T(512)S(1)}, f32[384]{0:T(512)}, u32[]{:S(2)}) copy-start(f32[384]{0:T(512)} %param.6) | copy-start | bytes 4612

commit v3 on v2

--- a/solution.py
+++ b/solution.py
@@ -20,15 +20,14 @@
     return ((y % 2) * 8 + x * 2 + core) * 8 + (y // 2) * 4 + z
 
 
-def swap(value, axes, flip):
-    flips = flip if isinstance(flip, tuple) else (flip, flip)
+def swap(value, moves):
     pairs = []
     for x in range(4):
         for y in range(4):
             for z in range(4):
-                for core in range(2):
+                for core, (axis, flip) in enumerate(moves):
                     to = {"x": x, "y": y, "z": z}
-                    to[axes[core]] ^= flips[core]
+                    to[axis] ^= flip
                     pairs.append((place(x, y, z, core), place(to["x"], to["y"], to["z"], core)))
     return lax.ppermute(value, AXES, pairs)
 
@@ -96,7 +95,7 @@
             pltpu.VMEM(inv_length.shape, jnp.float32),
             pltpu.SemaphoreType.DMA((3,)),
         ],
-        compiler_params=pltpu.CompilerParams(vmem_limit_bytes=8 << 20),
+        compiler_params=pltpu.CompilerParams(vmem_limit_bytes=64900 << 10),
         name="pack_own",
     )(embeddings_t, inv_length, probes)
 
@@ -149,11 +148,11 @@
     return jnp.dot(jnp.exp2(gram).astype(jnp.bfloat16), probe, preferred_element_type=jnp.float32)
 
 
-def accumulate(rows, olds, packs, steps):
+def accumulate(rows, olds, packs, out_types):
+    n, m, p = len(rows), len(olds), len(packs)
+    width = packs[0].shape[1] - LANES
+    cols = sum(q.shape[0] for q in packs)
     block = 384
-    width = packs[0].shape[1] - LANES
-    n, m, p = len(rows), len(olds), len(packs)
-    cols = sum(q.shape[0] for q in packs)
 
     def body(*refs):
         row_refs, old_refs, pack_refs = refs[:n], refs[n : n + m], refs[n + m : n + m + p]
@@ -167,101 +166,90 @@
                 probes[start : start + block, :] = src[k : k + block, LANES:]
                 start += block
         for k in range(n):
-            step = steps[k]
-
-            def one(i, carry):
-                at = pl.ds(pl.multiple_of(i * step, step), step)
-                part = fold(row_refs[k], at, right[...], probes[...])
-                out_refs[k][at, :] = old_refs[k][at, :] + part if m else part
-                return carry
-
-            lax.fori_loop(0, rows[k].shape[0] // step, one, 0)
+            part = fold(row_refs[k], slice(None), right[...], probes[...])
+            out_refs[k][...] = (old_refs[k][...] + part if m else part).astype(out_refs[k].dtype)
 
     return pl.pallas_call(
         body,
         in_specs=[VMEM] * (n + m + p),
         out_specs=[VMEM] * (n + 2),
-        out_shape=[jax.ShapeDtypeStruct((r.shape[0], width), jnp.float32) for r in rows]
+        out_shape=[jax.ShapeDtypeStruct((r.shape[0], width), t) for r, t in zip(rows, out_types, strict=True)]
         + [jax.ShapeDtypeStruct((cols, 2 * LANES), jnp.bfloat16), jax.ShapeDtypeStruct((cols, width), jnp.bfloat16)],
-        input_output_aliases={n + i: i for i in range(m)},
         cost_estimate=cost(sum(r.shape[0] for r in rows), cols, width),
         compiler_params=params(28),
     )(*rows, *olds, *packs)
 
 
-def apply_rows(rows, old, columns, step):
-    count, width = rows.shape[0], columns[0][1].shape[1]
+def apply_rows(rows, first_row, count, old, columns, out_type):
+    width = columns[0][1].shape[1]
     flat = [a for pair in columns for a in pair]
     lead = [rows] if old is None else [rows, old]
 
     def body(*refs):
         row_ref, out_ref, rest = refs[0], refs[-1], refs[len(lead) : -1]
-
-        def one(i, carry):
-            at = pl.ds(pl.multiple_of(i * step, step), step)
-            part = None if old is None else refs[1][at, :]
-            for k in range(0, len(rest), 2):
-                more = fold(row_ref, at, rest[k][...], rest[k + 1][...])
-                part = more if part is None else part + more
-            out_ref[at, :] = part
-            return carry
-
-        lax.fori_loop(0, count // step, one, 0)
+        part = None if old is None else refs[1][...]
+        for k in range(0, len(rest), 2):
+            more = fold(row_ref, pl.ds(first_row, count), rest[k][...], rest[k + 1][...])
+            part = more if part is None else part + more
+        out_ref[...] = part.astype(out_type)
 
     return pl.pallas_call(
         body,
         in_specs=[VMEM] * (len(lead) + len(flat)),
         out_specs=VMEM,
-        out_shape=jax.ShapeDtypeStruct((count, width), jnp.float32),
-        input_output_aliases={} if old is None else {1: 0},
+        out_shape=jax.ShapeDtypeStruct((count, width), out_type),
         cost_estimate=cost(count, sum(c[0].shape[0] for c in columns), width),
         compiler_params=params(28),
     )(*lead, *flat)
 
 
+COL_MOVES = ((("x", 1), ("x", 3)), (("x", 3), ("y", 1)), (("y", 1), ("x", 1)))
+ROW_MOVES = ((("z", 1), ("z", 3)), (("z", 3), ("y", 3)), (("y", 3), ("z", 1)))
+
+
 def on_device(embeddings, inv_length, noise, probes):
     block = probes.shape[0]
+    two = 2 * block
+    f32, bf16 = jnp.float32, jnp.bfloat16
+    move_a, move_b, move_c = COL_MOVES
+    move_p, move_q, move_r = ROW_MOVES
     own, pair = pack_own(embeddings.T, inv_length[None, :], probes)
 
-    first_axis, second_axis = ("x", "y"), ("y", "x")
-    beside = swap(own, first_axis, 1)
-    rows_a = swap(pair, "zz", (1, 3))
-    pairs = join(pair, rows_a)
-    rows_b = swap(pairs, "zz", (3, 1))
-    pack_a = join(own, beside)
-    pack_b = swap(pack_a, first_axis, 3)
-    pack_c = swap(pack_a, second_axis, 1)
-    pack_d = swap(pack_a, second_axis, 3)
-    other_pairs = partner(pairs)
-    other_b = partner(rows_b)
-    row_far, row_near, row_own = prepare_rows(
-        block,
-        [pairs, rows_b, other_pairs, other_b],
-        [[(2, 0), (2, 1), (3, 1), (3, 0)], [(0, 1), (1, 1), (1, 0)], [(0, 0)]],
+    got_a = swap(own, move_a)
+    rows_p = swap(pair, move_p)
+    pairs = join(pair, rows_p)
+    rows_q = swap(pairs, move_q)
+    pack_a = join(own, got_a)
+    pack_b = swap(pack_a, move_b)
+    pack_c = swap(pack_a, move_c)
+    other_a = partner(pack_a)
+    quads = join(pairs, rows_q)
+    rows_r = swap(quads, move_r)
+    row_f1, row_f2, row_n1, row_n2 = prepare_rows(
+        block, [quads, rows_r], [[(1, 2), (1, 3)], [(1, 0), (1, 1)], [(0, 2), (0, 3)], [(0, 0), (0, 1)]]
     )
-    rows, steps = [row_far, row_near], (768, 1152)
-    far, near, right_a, probes_a = accumulate(rows, [], [pack_a], steps)
-
-    pack_e = swap(pack_b, second_axis, 1)
-    pack_f = swap(pack_b, second_axis, 3)
-    pack_g = swap(pack_d, second_axis, 1)
-    far, near, right_b, probes_b = accumulate(rows, [far, near], [pack_b, pack_c], steps)
-
-    pack_h = swap(pack_e, second_axis, 3)
-    far, near, right_c, probes_c = accumulate(rows, [far, near], [pack_d, pack_e], steps)
-
-    last = [pack_f, pack_g, pack_h]
-    far, right_d, probes_d = accumulate([row_far], [far], last, (768,))
-    got = partner(far)
-    near = apply_rows(row_near, near, [(right_d, probes_d)], 1152)
-    sums = near + got[block:]
-    in_a = swap(sums[: 2 * block].astype(jnp.bfloat16), "zz", (1, 3))
-    columns = [(right_a, probes_a), (right_b, probes_b), (right_c, probes_c), (right_d, probes_d)]
-    own_sum = apply_rows(row_own, None, columns, 384)
-    passed = (sums[2 * block :] + in_a[block:].astype(jnp.float32)).astype(jnp.bfloat16)
-    in_b = swap(passed, "zz", (3, 1))
-    result = own_sum + got[:block] + noise[:, None] * probes.astype(jnp.float32)
-    return result + in_a[:block].astype(jnp.float32) + in_b.astype(jnp.float32)
+    far = [row_f1, row_f2]
+    f1, f2, *aug_a = accumulate(far, [], [pack_a, other_a], [f32, f32])
+
+    other_b, other_c = partner(pack_b), partner(pack_c)
+    pack_d = swap(pack_b, move_c)
+    f1, f2, *aug_b = accumulate(far, [f1, f2], [pack_b, other_b], [f32, f32])
+    f1, f2, *aug_c = accumulate(far, [f1, f2], [pack_c, other_c], [f32, f32])
+    other_d = partner(pack_d)
+    n1 = apply_rows(row_n1, 0, two, None, [aug_a, aug_b], f32)
+    f1, *aug_d = accumulate([row_f1], [f1], [pack_d, other_d], [bf16])
+    in_1 = swap(f1, move_r)
+    f2 = apply_rows(row_f2, 0, two, f2, [aug_d], bf16)
+    in_2 = swap(f2, move_r)
+    n1 = apply_rows(row_n1, 0, two, n1, [aug_c, aug_d], f32)
+    in_3 = swap((n1 + in_1.astype(f32)).astype(bf16), move_q)
+    columns = [aug_a, aug_b, aug_c, aug_d]
+    beside = apply_rows(row_n2, block, block, None, columns, f32)
+    passed = beside + in_2[block:].astype(f32) + in_3[block:].astype(f32)
+    in_4 = swap(passed.astype(bf16), move_p)
+    total = apply_rows(row_n2, 0, block, None, columns, f32)
+    total = total + in_2[:block].astype(f32) + in_3[:block].astype(f32) + in_4.astype(f32)
+    return total + noise[:, None] * probes.astype(f32)
 
 
 def solution(mesh):

time: 78.9 us -> 79.3 us (level); the launches traced: 77.9 us -> 79.1 us
  starting transfers between devices: 26.9 us -> 32 us
  waiting for transfers between devices: 18.4 us -> 14.8 us
  local copies, waits for them, and re-layouts: 2.53 us -> 0.98 us
  Pallas kernels: 28.7 us -> 30.1 us
    pallas_call x4, Pallas kernels: 20.8 us -> 11.8 us  [accumulate(): pl.pallas_call(body, in_specs=[VMEM] * (n + m + p), out_specs=[VMEM] * (n...]
    pallas_call x2 -> x5, Pallas kernels: 6.2 us -> 15 us  [apply_rows(): pl.pallas_call(body, in_specs=[VMEM] * (len(lead) + len(flat)), out_specs...]
    ppermute x12 -> x11, starting transfers between devices: 17 us -> 19.9 us  [swap(): return lax.ppermute(value, AXES, pairs)]
    ppermute x3 -> x4, starting transfers between devices: 9.89 us -> 12.1 us  [partner(): return lax.ppermute(value, AXES, [(i, i ^ 8) for i in range(128)])]
    ppermute x12 -> x11, waiting for transfers between devices: 17 us -> 14.8 us  [swap(): return lax.ppermute(value, AXES, pairs)]
    pallas_call x1, Pallas kernels: 0.33 us -> 1.85 us  [pack_own(): pl.pallas_call(body, in_specs=[pl.BlockSpec(memory_space=pltpu.HBM)] * 3,...]
    unnamed x10 -> x8, local copies, waits for them, and re-layouts: 2.49 us -> 0.98 us
    ppermute x3 -> x4, waiting for transfers between devices: 1.44 us -> 0.01 us  [partner(): return lax.ppermute(value, AXES, [(i, i ^ 8) for i in range(128)])]
  transfers between devices with their start and end apart: 15 -> 15, of which waited for: 7 -> 5; matrix products, arithmetic and copies ran while one was open for 0% -> 0% of each run, Pallas kernels for 30% -> 33%
where the time goes in v3:
time: 79.3 us; the launch traced here: 79.1 us
  starting transfers between devices  32 us (40%)
  Pallas kernels  30.1 us (38%)
  waiting for transfers between devices  14.8 us (19%)
  other arithmetic  1.03 us (1%)
  local copies, waits for them, and re-layouts  0.98 us (1%)
    ppermute x11, starting transfers between devices, swap(): return lax.ppermute(value, AXES, pairs)  19.9 us
    pallas_call x5, Pallas kernels, apply_rows(): pl.pallas_call(body, in_specs=[VMEM] * (len(lead) + len(flat)), out_specs...  15 us
    ppermute x11, waiting for transfers between devices, swap(): return lax.ppermute(value, AXES, pairs)  14.8 us
    ppermute x4, starting transfers between devices, partner(): return lax.ppermute(value, AXES, [(i, i ^ 8) for i in range(128)])  12.1 us
    pallas_call x4, Pallas kernels, accumulate(): pl.pallas_call(body, in_specs=[VMEM] * (n + m + p), out_specs=[VMEM] * (n...  11.8 us
    pallas_call x1, Pallas kernels, pack_own(): pl.pallas_call(body, in_specs=[pl.BlockSpec(memory_space=pltpu.HBM)] * 3,...  1.85 us
  transfers between devices with their start and end apart: 15, of which 5 were waited for; matrix products, arithmetic and copies ran while one was open for 0% of the time, Pallas kernels for 33%

profile of v3, /device:TPU:1, one launch (start us, length us, event | category | flops | bytes accessed | tf_op | source)
XLA Modules:
  0.0 79.1 jit_solution(6508143600447991011)
XLA Ops:
  0.0 1.8 %pack_own.1 = (bf16[384,384]{1,0:T(8,128)(2,1)}, bf16[384,128]{1,0:T(8,128)(2,1)}) custom-call(f32[64,384]{1,0:T(8,128)} %bitcast.2, f32[1,64]{1,0:T(1,128)} %bitcast.3, bf16[384,256]{1,0:T(8,128)(2,1)} %probe_hbm.1), custom_call_target="tpu_custom_call" | custom-call | tf_op jit(solution)/shard_map/pack_own/pallas_call | solution.py:85
  1.9 3.4 %collective-permute-start.3 = (bf16[384,384]{1,0:T(8,128)(2,1)}, bf16[384,384]{1,0:T(8,128)(2,1)S(1)}, u32[]{:S(2)}, u32[]{:S(2)}) collective-permute-start(bf16[384,384]{1,0:T(8,128)(2,1)} %get-tuple-element.30.a_ref), channel_id=1, source_target_pairs={{0,16},{8,56},{1,17},{9,57},{2,18},{10,58},{3,19},{11,59},{64,80},... | collective-permute-start | bytes 884744 | tf_op jit(solution)/shard_map/ppermute | solution.py:32
  5.2 4.3 %collective-permute-done.3.b_ref = bf16[384,384]{1,0:T(8,128)(2,1)S(1)} collective-permute-done((bf16[384,384]{1,0:T(8,128)(2,1)}, bf16[384,384]{1,0:T(8,128)(2,1)S(1)}, u32[]{:S(2)}, u32[]{:S(2)}) %collective-permute-start.3) | collective-permute-done | bytes 294944 | tf_op jit(solution)/shard_map/ppermute | solution.py:32
  9.6 0.0 copy-start
  9.6 1.0 %copy-done = bf16[384,384]{1,0:T(8,128)(2,1)S(1)} copy-done((bf16[384,384]{1,0:T(8,128)(2,1)S(1)}, bf16[384,384]{1,0:T(8,128)(2,1)}, u32[]{:S(2)}) %copy-start) | copy-done | bytes 294936
  10.5 0.0 copy-start.1
  10.5 0.1 shard_map.48.refs_2_
  10.6 1.6 %collective-permute-start.5 = (bf16[768,384]{1,0:T(8,128)(2,1)S(1)}, bf16[768,384]{1,0:T(8,128)(2,1)S(1)}, u32[]{:S(2)}, u32[]{:S(2)}) collective-permute-start(bf16[768,384]{1,0:T(8,128)(2,1)S(1)} %shard_map.48.refs_2_), channel_id=1, source_target_pairs={{0,48},{8,72},{1,49},{9,73},{2,50},{10,74},{3,51},{11,75},{64,112}... | collective-permute-start | bytes 1769480 | tf_op jit(solution)/shard_map/ppermute | solution.py:32
  12.1 0.3 collective-permute-start.7
  12.4 0.0 copy-done.1
  12.4 3.8 %collective-permute-start = (bf16[384,128]{1,0:T(8,128)(2,1)S(1)}, bf16[384,128]{1,0:T(8,128)(2,1)S(1)}, u32[]{:S(2)}, u32[]{:S(2)}) collective-permute-start(bf16[384,128]{1,0:T(8,128)(2,1)S(1)} %copy-done.1), channel_id=1, source_target_pairs={{0,1},{8,11},{1,0},{9,10},{2,3},{10,9},{3,2},{11,8},{64,65},{72,75... | collective-permute-start | bytes 294920 | tf_op jit(solution)/shard_map/ppermute | solution.py:32
  16.2 2.3 %collective-permute-done.b_ref = bf16[384,128]{1,0:T(8,128)(2,1)S(1)} collective-permute-done((bf16[384,128]{1,0:T(8,128)(2,1)S(1)}, bf16[384,128]{1,0:T(8,128)(2,1)S(1)}, u32[]{:S(2)}, u32[]{:S(2)}) %collective-permute-start) | collective-permute-done | bytes 98336 | tf_op jit(solution)/shard_map/ppermute | solution.py:32
  18.5 2.0 %collective-permute-start.1 = (bf16[768,128]{1,0:T(8,128)(2,1)S(1)}, bf16[768,128]{1,0:T(8,128)(2,1)S(1)}, u32[]{:S(2)}, u32[]{:S(2)}) collective-permute-start(bf16[768,128]{1,0:T(8,128)(2,1)S(1)} %shard_map.46.a_ref), channel_id=1, source_target_pairs={{0,3},{8,76},{1,2},{9,77},{2,1},{10,78},{3,0},{11,79},{64,67},{72,... | collective-permute-start | bytes 589832 | tf_op jit(solution)/shard_map/ppermute | solution.py:32
  20.5 1.5 %collective-permute-done.5.refs_4_ = bf16[768,384]{1,0:T(8,128)(2,1)S(1)} collective-permute-done((bf16[768,384]{1,0:T(8,128)(2,1)S(1)}, bf16[768,384]{1,0:T(8,128)(2,1)S(1)}, u32[]{:S(2)}, u32[]{:S(2)}) %collective-permute-start.5) | collective-permute-done | bytes 589856 | tf_op jit(solution)/shard_map/ppermute | solution.py:32
  22.0 1.0 %collective-permute-start.9 = (bf16[768,384]{1,0:T(8,128)(2,1)S(1)}, bf16[768,384]{1,0:T(8,128)(2,1)S(1)}, u32[]{:S(2)}, u32[]{:S(2)}) collective-permute-start(bf16[768,384]{1,0:T(8,128)(2,1)S(1)} %collective-permute-done.5.refs_4_), channel_id=1, source_target_pairs={{0,64},{8,24},{1,65},{9,25},{2,66},{10,26},{3,67},{11,27},{64,0},{... | collective-permute-start | bytes 1769480 | tf_op jit(solution)/shard_map/ppermute | solution.py:32
  23.0 2.0 %collective-permute-start.4 = (bf16[768,384]{1,0:T(8,128)(2,1)S(1)}, bf16[768,384]{1,0:T(8,128)(2,1)S(1)}, u32[]{:S(2)}, u32[]{:S(2)}) collective-permute-start(bf16[768,384]{1,0:T(8,128)(2,1)S(1)} %shard_map.48.refs_2_), channel_id=1, source_target_pairs={{0,8},{1,9},{2,10},{3,11},{4,12},{5,13},{6,14},{7,15},{8,0},{9,1},... | collective-permute-start | bytes 1769480 | tf_op jit(solution)/shard_map/ppermute | solution.py:36
  25.0 0.0 collective-permute-done.1.b_ref
  25.0 0.8 %collective-permute-start.2 = (bf16[1536,128]{1,0:T(8,128)(2,1)S(1)}, bf16[1536,128]{1,0:T(8,128)(2,1)S(1)}, u32[]{:S(2)}, u32[]{:S(2)}) collective-permute-start(bf16[1536,128]{1,0:T(8,128)(2,1)S(1)} %shard_map.47.refs_0_), channel_id=1, source_target_pairs={{0,68},{8,9},{1,69},{9,8},{2,70},{10,11},{3,71},{11,10},{64,4},{72... | collective-permute-start | bytes 1179656 | tf_op jit(solution)/shard_map/ppermute | solution.py:32
  25.9 4.6 %collective-permute-start.6 = (bf16[768,384]{1,0:T(8,128)(2,1)S(1)}, bf16[768,384]{1,0:T(8,128)(2,1)S(1)}, u32[]{:S(2)}, u32[]{:S(2)}) collective-permute-start(bf16[768,384]{1,0:T(8,128)(2,1)S(1)} %collective-permute-done.5.refs_4_), channel_id=1, source_target_pairs={{0,8},{1,9},{2,10},{3,11},{4,12},{5,13},{6,14},{7,15},{8,0},{9,1},... | collective-permute-start | bytes 1769480 | tf_op jit(solution)/shard_map/ppermute | solution.py:36
  30.5 0.0 collective-permute-done.7.refs_4_
  30.5 0.0 collective-permute-start.8
  30.5 1.5 %collective-permute-done.2.refs_1_ = bf16[1536,128]{1,0:T(8,128)(2,1)S(1)} collective-permute-done((bf16[1536,128]{1,0:T(8,128)(2,1)S(1)}, bf16[1536,128]{1,0:T(8,128)(2,1)S(1)}, u32[]{:S(2)}, u32[]{:S(2)}) %collective-permute-start.2) | collective-permute-done | bytes 393248 | tf_op jit(solution)/shard_map/ppermute | solution.py:32
  32.0 1.3 %prepare_rows.1 = (bf16[768,256]{1,0:T(8,128)(2,1)S(1)}, bf16[768,256]{1,0:T(8,128)(2,1)S(1)}, bf16[768,256]{1,0:T(8,128)(2,1)S(1)}, bf16[768,256]{1,0:T(8,128)(2,1)S(1)}) custom-call(bf16[1536,128]{1,0:T(8,128)(2,1)S(1)} %shard_map.47.refs_0_, bf16[1536,128]{1,0:T(8,128)(2,1)S(1)} %collective-permute-done.2.refs_1_), custom_call_target="tpu_custom_call" | custom-call | tf_op jit(solution)/shard_map/prepare_rows/pallas_call | solution.py:126
  33.4 0.0 collective-permute-done.9.refs_2_
  33.4 5.5 %collective-permute-start.10 = (bf16[768,384]{1,0:T(8,128)(2,1)S(1)}, bf16[768,384]{1,0:T(8,128)(2,1)S(1)}, u32[]{:S(2)}, u32[]{:S(2)}) collective-permute-start(bf16[768,384]{1,0:T(8,128)(2,1)S(1)} %collective-permute-done.9.refs_2_), channel_id=1, source_target_pairs={{0,8},{1,9},{2,10},{3,11},{4,12},{5,13},{6,14},{7,15},{8,0},{9,1},... | collective-permute-start | bytes 1769480 | tf_op jit(solution)/shard_map/ppermute | solution.py:36
  38.9 0.0 collective-permute-done.4.refs_3_
  38.9 3.2 %shard_map.49 = (f32[768,256]{1,0:T(8,128)S(1)}, f32[768,256]{1,0:T(8,128)S(1)}, bf16[1536,256]{1,0:T(8,128)(2,1)S(1)}, bf16[1536,256]{1,0:T(8,128)(2,1)S(1)}) custom-call(bf16[768,256]{1,0:T(8,128)(2,1)S(1)} %get-tuple-element.28.refs_0_, bf16[768,256]{1,0:T(8,128)(2,1)S(1)} %get-tuple-element.29.refs_1_.refs_0_, bf16[768,384]{1,0:T(8,128)(2,1)S(1)} %shard_map.48.refs_2_, ...), custom_call_target="tpu_custom_call" | custom-call | flops 2415919104 | bytes 1572864 | tf_op jit(solution)/shard_map/pallas_call | solution.py:172
  42.2 0.0 collective-permute-done.6.refs_5_
  42.2 3.3 %shard_map.50 = (f32[768,256]{1,0:T(8,128)S(1)}, f32[768,256]{1,0:T(8,128)S(1)}, bf16[1536,256]{1,0:T(8,128)(2,1)S(1)}, bf16[1536,256]{1,0:T(8,128)(2,1)S(1)}) custom-call(bf16[768,256]{1,0:T(8,128)(2,1)S(1)} %get-tuple-element.28.refs_0_, bf16[768,256]{1,0:T(8,128)(2,1)S(1)} %get-tuple-element.29.refs_1_.refs_0_, f32[768,256]{1,0:T(8,128)S(1)} %get-tuple-element.33.refs_2_, ...), custom_call_target="tpu_custom_call" | custom-call | flops 2415919104 | bytes 1572864 | tf_op jit(solution)/shard_map/pallas_call | solution.py:172
  45.4 0.0 collective-permute-done.8.refs_5_
  45.4 3.3 %shard_map.51 = (f32[768,256]{1,0:T(8,128)S(1)}, f32[768,256]{1,0:T(8,128)S(1)}, bf16[1536,256]{1,0:T(8,128)(2,1)S(1)}, bf16[1536,256]{1,0:T(8,128)(2,1)S(1)}) custom-call(bf16[768,256]{1,0:T(8,128)(2,1)S(1)} %get-tuple-element.28.refs_0_, bf16[768,256]{1,0:T(8,128)(2,1)S(1)} %get-tuple-element.29.refs_1_.refs_0_, f32[768,256]{1,0:T(8,128)S(1)} %get-tuple-element.37.refs_2_, ...), custom_call_target="tpu_custom_call" | custom-call | flops 2415919104 | bytes 1572864 | tf_op jit(solution)/shard_map/pallas_call | solution.py:172
  48.7 0.0 collective-permute-done.10.refs_3_
  48.7 2.0 %shard_map.52 = (bf16[768,256]{1,0:T(8,128)(2,1)S(1)}, bf16[1536,256]{1,0:T(8,128)(2,1)S(1)}, bf16[1536,256]{1,0:T(8,128)(2,1)S(1)}) custom-call(bf16[768,256]{1,0:T(8,128)(2,1)S(1)} %get-tuple-element.28.refs_0_, f32[768,256]{1,0:T(8,128)S(1)} %get-tuple-element.41.refs_1_, bf16[768,384]{1,0:T(8,128)(2,1)S(1)} %collective-permute-done.9.refs_2_, ...), custom_call_target="tpu_custom_call" | custom-call | flops 1207959552 | bytes 786432 | tf_op jit(solution)/shard_map/pallas_call | solution.py:172
  50.7 0.3 collective-permute-start.12
  51.1 4.0 %shard_map.55.refs_1_ = f32[768,256]{1,0:T(8,128)S(1)} custom-call(bf16[768,256]{1,0:T(8,128)(2,1)S(1)} %get-tuple-element.45.refs_0_, bf16[1536,256]{1,0:T(8,128)(2,1)S(1)} %get-tuple-element.31.refs_1_, bf16[1536,256]{1,0:T(8,128)(2,1)S(1)} %get-tuple-element.32.refs_2_, bf16[1536,256]{1,0:T(8,128)(2,1)S(1)} %get-tuple-element.35.refs_3_, ...), custom_call_target="tpu_custom_call" | custom-call | flops 2415919104 | bytes 786432 | tf_op jit(solution)/shard_map/pallas_call | solution.py:196
  55.0 1.5 %shard_map.54 = bf16[768,256]{1,0:T(8,128)(2,1)S(1)} custom-call(bf16[768,256]{1,0:T(8,128)(2,1)S(1)} %get-tuple-element.29.refs_1_.refs_0_, f32[768,256]{1,0:T(8,128)S(1)} %get-tuple-element.44.refs_1_, bf16[1536,256]{1,0:T(8,128)(2,1)S(1)} %get-tuple-element.42.refs_7_.refs_2_.refs_4_, bf16[1536,256]{1,0:T(8,128)(2,1)S(1)} %get-tuple-element.43.refs_8_.refs_3_.refs_5_), custom_call_target="tpu_custom_call" | custom-call | flops 1207959552 | bytes 786432 | tf_op jit(solution)/shard_map/pallas_call | solution.py:196
  56.6 1.5 %collective-permute-start.11 = (bf16[768,256]{1,0:T(8,128)(2,1)S(1)}, bf16[768,256]{1,0:T(8,128)(2,1)S(1)}, u32[]{:S(2)}, u32[]{:S(2)}) collective-permute-start(bf16[768,256]{1,0:T(8,128)(2,1)S(1)} %shard_map.54), channel_id=1, source_target_pairs={{0,68},{8,9},{1,69},{9,8},{2,70},{10,11},{3,71},{11,10},{64,4},{72... | collective-permute-start | bytes 1179656 | tf_op jit(solution)/shard_map/ppermute | solution.py:32
  58.1 2.8 %shard_map.56 = f32[768,256]{1,0:T(8,128)S(1)} custom-call(bf16[768,256]{1,0:T(8,128)(2,1)S(1)} %get-tuple-element.45.refs_0_, f32[768,256]{1,0:T(8,128)S(1)} %shard_map.55.refs_1_, bf16[1536,256]{1,0:T(8,128)(2,1)S(1)} %get-tuple-element.39.refs_5_.refs_2_, bf16[1536,256]{1,0:T(8,128)(2,1)S(1)} %get-tuple-element.40.refs_6_.refs_3_, ...), custom_call_target="tpu_custom_call" | custom-call | flops 2415919104 | bytes 786432 | tf_op jit(solution)/shard_map/pallas_call | solution.py:196
  60.9 0.0 collective-permute-done.12
  60.9 0.1 add_convert_fusion
  61.0 2.0 %collective-permute-start.13 = (bf16[768,256]{1,0:T(8,128)(2,1)S(1)}, bf16[768,256]{1,0:T(8,128)(2,1)S(1)}, u32[]{:S(2)}, u32[]{:S(2)}) collective-permute-start(bf16[768,256]{1,0:T(8,128)(2,1)S(1)} %add_convert_fusion), channel_id=1, source_target_pairs={{0,3},{8,76},{1,2},{9,77},{2,1},{10,78},{3,0},{11,79},{64,67},{72,... | collective-permute-start | bytes 1179656 | tf_op jit(solution)/shard_map/ppermute | solution.py:32
  63.0 3.4 %shard_map.57 = f32[384,256]{1,0:T(8,128)S(1)} custom-call(bf16[768,256]{1,0:T(8,128)(2,1)S(1)} %get-tuple-element.27.refs_0_, bf16[1536,256]{1,0:T(8,128)(2,1)S(1)} %get-tuple-element.31.refs_1_, bf16[1536,256]{1,0:T(8,128)(2,1)S(1)} %get-tuple-element.32.refs_2_, bf16[1536,256]{1,0:T(8,128)(2,1)S(1)} %get-tuple-element.35.refs_3_, ...), custom_call_target="tpu_custom_call" | custom-call | flops 2415919104 | bytes 393216 | tf_op jit(solution)/shard_map/pallas_call | solution.py:196
  66.3 0.0 collective-permute-done.11
  66.3 5.1 %collective-permute-done.13 = bf16[768,256]{1,0:T(8,128)(2,1)S(1)} collective-permute-done((bf16[768,256]{1,0:T(8,128)(2,1)S(1)}, bf16[768,256]{1,0:T(8,128)(2,1)S(1)}, u32[]{:S(2)}, u32[]{:S(2)}) %collective-permute-start.13) | collective-permute-done | bytes 393248 | tf_op jit(solution)/shard_map/ppermute | solution.py:32
  71.5 0.1 add_convert_fusion.1
  71.5 0.0 copy-start.2
  71.5 0.0 copy-start.3
  71.5 3.3 %collective-permute-start.14 = (bf16[384,256]{1,0:T(8,128)(2,1)S(1)}, bf16[384,256]{1,0:T(8,128)(2,1)S(1)}, u32[]{:S(2)}, u32[]{:S(2)}) collective-permute-start(bf16[384,256]{1,0:T(8,128)(2,1)S(1)} %add_convert_fusion.1), channel_id=1, source_target_pairs={{0,1},{8,11},{1,0},{9,10},{2,3},{10,9},{3,2},{11,8},{64,65},{72,75... | collective-permute-start | bytes 589832 | tf_op jit(solution)/shard_map/ppermute | solution.py:32
  74.8 3.4 %shard_map.53 = f32[384,256]{1,0:T(8,128)S(1)} custom-call(bf16[768,256]{1,0:T(8,128)(2,1)S(1)} %get-tuple-element.27.refs_0_, bf16[1536,256]{1,0:T(8,128)(2,1)S(1)} %get-tuple-element.31.refs_1_, bf16[1536,256]{1,0:T(8,128)(2,1)S(1)} %get-tuple-element.32.refs_2_, bf16[1536,256]{1,0:T(8,128)(2,1)S(1)} %get-tuple-element.35.refs_3_, ...), custom_call_target="tpu_custom_call" | custom-call | flops 2415919104 | bytes 393216 | tf_op jit(solution)/shard_map/pallas_call | solution.py:196
  78.2 0.0 collective-permute-done.14
  78.2 0.0 copy-done.2
  78.2 0.0 copy-done.3
  78.2 0.9 %multiply_add_fusion = f32[384,256]{1,0:T(8,128)} fusion(bf16[384,256]{1,0:T(8,128)(2,1)S(1)} %copy-done.2, bf16[384,256]{1,0:T(8,128)(2,1)S(1)} %collective-permute-done.14, f32[384,256]{1,0:T(8,128)S(1)} %shard_map.53, bf16[768,256]{1,0:T(8,128)(2,1)S(1)} %collective-permute-done.13, bf16[768,256]{1,0:T(8,128)(2,1)S(1)} %collective-permute-done.11, ...), kind=kLoop, calls=%fused_computation.1 | loop fusion | flops 884736 | bytes 1574400 | tf_op jit(solution)/shard_map/add | solution.py:252
  (2 shorter events, 0.0 us)
Async XLA Ops:
  1.9 7.7 %collective-permute-start.3 = (bf16[384,384]{1,0:T(8,128)(2,1)}, bf16[384,384]{1,0:T(8,128)(2,1)S(1)}, u32[]{:S(2)}, u32[]{:S(2)}) collective-permute-start(bf16[384,384]{1,0:T(8,128)(2,1)} %get-tuple-element.30.a_ref), channel_id=1, source_target_pairs={{0,16},{8,56},{1,17},{9,57},{2,18},{10,58},{3,19},{11,59},{64,80},... | collective-permute-start | bytes 884744 | tf_op jit(solution)/shard_map/ppermute | solution.py:32
  9.6 1.0 %copy-start = (bf16[384,384]{1,0:T(8,128)(2,1)S(1)}, bf16[384,384]{1,0:T(8,128)(2,1)}, u32[]{:S(2)}) copy-start(bf16[384,384]{1,0:T(8,128)(2,1)} %get-tuple-element.30.a_ref) | copy-start | bytes 884740
  10.5 1.9 %copy-start.1 = (bf16[384,128]{1,0:T(8,128)(2,1)S(1)}, bf16[384,128]{1,0:T(8,128)(2,1)}, u32[]{:S(2)}) copy-start(bf16[384,128]{1,0:T(8,128)(2,1)} %get-tuple-element.26.a_ref) | copy-start | bytes 294916
  10.6 11.5 %collective-permute-start.5 = (bf16[768,384]{1,0:T(8,128)(2,1)S(1)}, bf16[768,384]{1,0:T(8,128)(2,1)S(1)}, u32[]{:S(2)}, u32[]{:S(2)}) collective-permute-start(bf16[768,384]{1,0:T(8,128)(2,1)S(1)} %shard_map.48.refs_2_), channel_id=1, source_target_pairs={{0,48},{8,72},{1,49},{9,73},{2,50},{10,74},{3,51},{11,75},{64,112}... | collective-permute-start | bytes 1769480 | tf_op jit(solution)/shard_map/ppermute | solution.py:32
  12.1 18.4 %collective-permute-start.7 = (bf16[768,384]{1,0:T(8,128)(2,1)S(1)}, bf16[768,384]{1,0:T(8,128)(2,1)S(1)}, u32[]{:S(2)}, u32[]{:S(2)}) collective-permute-start(bf16[768,384]{1,0:T(8,128)(2,1)S(1)} %shard_map.48.refs_2_), channel_id=1, source_target_pairs={{0,64},{8,24},{1,65},{9,25},{2,66},{10,26},{3,67},{11,27},{64,0},{... | collective-permute-start | bytes 1769480 | tf_op jit(solution)/shard_map/ppermute | solution.py:32
  12.4 6.1 %collective-permute-start = (bf16[384,128]{1,0:T(8,128)(2,1)S(1)}, bf16[384,128]{1,0:T(8,128)(2,1)S(1)}, u32[]{:S(2)}, u32[]{:S(2)}) collective-permute-start(bf16[384,128]{1,0:T(8,128)(2,1)S(1)} %copy-done.1), channel_id=1, source_target_pairs={{0,1},{8,11},{1,0},{9,10},{2,3},{10,9},{3,2},{11,8},{64,65},{72,75... | collective-permute-start | bytes 294920 | tf_op jit(solution)/shard_map/ppermute | solution.py:32
  18.5 6.5 %collective-permute-start.1 = (bf16[768,128]{1,0:T(8,128)(2,1)S(1)}, bf16[768,128]{1,0:T(8,128)(2,1)S(1)}, u32[]{:S(2)}, u32[]{:S(2)}) collective-permute-start(bf16[768,128]{1,0:T(8,128)(2,1)S(1)} %shard_map.46.a_ref), channel_id=1, source_target_pairs={{0,3},{8,76},{1,2},{9,77},{2,1},{10,78},{3,0},{11,79},{64,67},{72,... | collective-permute-start | bytes 589832 | tf_op jit(solution)/shard_map/ppermute | solution.py:32
  22.0 11.3 %collective-permute-start.9 = (bf16[768,384]{1,0:T(8,128)(2,1)S(1)}, bf16[768,384]{1,0:T(8,128)(2,1)S(1)}, u32[]{:S(2)}, u32[]{:S(2)}) collective-permute-start(bf16[768,384]{1,0:T(8,128)(2,1)S(1)} %collective-permute-done.5.refs_4_), channel_id=1, source_target_pairs={{0,64},{8,24},{1,65},{9,25},{2,66},{10,26},{3,67},{11,27},{64,0},{... | collective-permute-start | bytes 1769480 | tf_op jit(solution)/shard_map/ppermute | solution.py:32
  23.0 15.9 %collective-permute-start.4 = (bf16[768,384]{1,0:T(8,128)(2,1)S(1)}, bf16[768,384]{1,0:T(8,128)(2,1)S(1)}, u32[]{:S(2)}, u32[]{:S(2)}) collective-permute-start(bf16[768,384]{1,0:T(8,128)(2,1)S(1)} %shard_map.48.refs_2_), channel_id=1, source_target_pairs={{0,8},{1,9},{2,10},{3,11},{4,12},{5,13},{6,14},{7,15},{8,0},{9,1},... | collective-permute-start | bytes 1769480 | tf_op jit(solution)/shard_map/ppermute | solution.py:36
  25.0 7.0 %collective-permute-start.2 = (bf16[1536,128]{1,0:T(8,128)(2,1)S(1)}, bf16[1536,128]{1,0:T(8,128)(2,1)S(1)}, u32[]{:S(2)}, u32[]{:S(2)}) collective-permute-start(bf16[1536,128]{1,0:T(8,128)(2,1)S(1)} %shard_map.47.refs_0_), channel_id=1, source_target_pairs={{0,68},{8,9},{1,69},{9,8},{2,70},{10,11},{3,71},{11,10},{64,4},{72... | collective-permute-start | bytes 1179656 | tf_op jit(solution)/shard_map/ppermute | solution.py:32
  25.9 16.3 %collective-permute-start.6 = (bf16[768,384]{1,0:T(8,128)(2,1)S(1)}, bf16[768,384]{1,0:T(8,128)(2,1)S(1)}, u32[]{:S(2)}, u32[]{:S(2)}) collective-permute-start(bf16[768,384]{1,0:T(8,128)(2,1)S(1)} %collective-permute-done.5.refs_4_), channel_id=1, source_target_pairs={{0,8},{1,9},{2,10},{3,11},{4,12},{5,13},{6,14},{7,15},{8,0},{9,1},... | collective-permute-start | bytes 1769480 | tf_op jit(solution)/shard_map/ppermute | solution.py:36
  30.5 14.9 %collective-permute-start.8 = (bf16[768,384]{1,0:T(8,128)(2,1)S(1)}, bf16[768,384]{1,0:T(8,128)(2,1)S(1)}, u32[]{:S(2)}, u32[]{:S(2)}) collective-permute-start(bf16[768,384]{1,0:T(8,128)(2,1)S(1)} %collective-permute-done.7.refs_4_), channel_id=1, source_target_pairs={{0,8},{1,9},{2,10},{3,11},{4,12},{5,13},{6,14},{7,15},{8,0},{9,1},... | collective-permute-start | bytes 1769480 | tf_op jit(solution)/shard_map/ppermute | solution.py:36
  33.4 15.3 %collective-permute-start.10 = (bf16[768,384]{1,0:T(8,128)(2,1)S(1)}, bf16[768,384]{1,0:T(8,128)(2,1)S(1)}, u32[]{:S(2)}, u32[]{:S(2)}) collective-permute-start(bf16[768,384]{1,0:T(8,128)(2,1)S(1)} %collective-permute-done.9.refs_2_), channel_id=1, source_target_pairs={{0,8},{1,9},{2,10},{3,11},{4,12},{5,13},{6,14},{7,15},{8,0},{9,1},... | collective-permute-start | bytes 1769480 | tf_op jit(solution)/shard_map/ppermute | solution.py:36
  50.7 10.1 %collective-permute-start.12 = (bf16[768,256]{1,0:T(8,128)(2,1)S(1)}, bf16[768,256]{1,0:T(8,128)(2,1)S(1)}, u32[]{:S(2)}, u32[]{:S(2)}) collective-permute-start(bf16[768,256]{1,0:T(8,128)(2,1)S(1)} %get-tuple-element.46), channel_id=1, source_target_pairs={{0,68},{8,9},{1,69},{9,8},{2,70},{10,11},{3,71},{11,10},{64,4},{72... | collective-permute-start | bytes 1179656 | tf_op jit(solution)/shard_map/ppermute | solution.py:32
  56.6 9.8 %collective-permute-start.11 = (bf16[768,256]{1,0:T(8,128)(2,1)S(1)}, bf16[768,256]{1,0:T(8,128)(2,1)S(1)}, u32[]{:S(2)}, u32[]{:S(2)}) collective-permute-start(bf16[768,256]{1,0:T(8,128)(2,1)S(1)} %shard_map.54), channel_id=1, source_target_pairs={{0,68},{8,9},{1,69},{9,8},{2,70},{10,11},{3,71},{11,10},{64,4},{72... | collective-permute-start | bytes 1179656 | tf_op jit(solution)/shard_map/ppermute | solution.py:32
  61.0 10.5 %collective-permute-start.13 = (bf16[768,256]{1,0:T(8,128)(2,1)S(1)}, bf16[768,256]{1,0:T(8,128)(2,1)S(1)}, u32[]{:S(2)}, u32[]{:S(2)}) collective-permute-start(bf16[768,256]{1,0:T(8,128)(2,1)S(1)} %add_convert_fusion), channel_id=1, source_target_pairs={{0,3},{8,76},{1,2},{9,77},{2,1},{10,78},{3,0},{11,79},{64,67},{72,... | collective-permute-start | bytes 1179656 | tf_op jit(solution)/shard_map/ppermute | solution.py:32
  71.5 6.7 %copy-start.2 = (bf16[384,256]{1,0:T(8,128)(2,1)S(1)}, bf16[384,256]{1,0:T(8,128)(2,1)}, u32[]{:S(2)}) copy-start(bf16[384,256]{1,0:T(8,128)(2,1)} %probe_hbm.1) | copy-start | bytes 589828
  71.5 6.7 %copy-start.3 = (f32[384]{0:T(512)S(1)}, f32[384]{0:T(512)}, u32[]{:S(2)}) copy-start(f32[384]{0:T(512)} %param.6) | copy-start | bytes 4612
  71.5 6.7 %collective-permute-start.14 = (bf16[384,256]{1,0:T(8,128)(2,1)S(1)}, bf16[384,256]{1,0:T(8,128)(2,1)S(1)}, u32[]{:S(2)}, u32[]{:S(2)}) collective-permute-start(bf16[384,256]{1,0:T(8,128)(2,1)S(1)} %add_convert_fusion.1), channel_id=1, source_target_pairs={{0,1},{8,11},{1,0},{9,10},{2,3},{10,9},{3,2},{11,8},{64,65},{72,75... | collective-permute-start | bytes 589832 | tf_op jit(solution)/shard_map/ppermute | solution.py:32

commit v4 on v3

--- a/solution.py
+++ b/solution.py
@@ -101,15 +101,17 @@
 
 
 def join(a, b):
+    width = b.shape[1]
+
     def body(a_ref, b_ref, out_ref):
-        out_ref[: a.shape[0], :] = a_ref[...]
+        out_ref[: a.shape[0], :] = a_ref[:, :width]
         out_ref[a.shape[0] :, :] = b_ref[...]
 
     return pl.pallas_call(
         body,
         in_specs=[VMEM] * 2,
         out_specs=VMEM,
-        out_shape=jax.ShapeDtypeStruct((a.shape[0] + b.shape[0], a.shape[1]), a.dtype),
+        out_shape=jax.ShapeDtypeStruct((a.shape[0] + b.shape[0], width), a.dtype),
         compiler_params=pltpu.CompilerParams(vmem_limit_bytes=8 << 20),
     )(a, b)
 
@@ -129,7 +131,6 @@
         out_specs=[VMEM] * len(groups),
         out_shape=[jax.ShapeDtypeStruct((len(g) * block, 2 * LANES), jnp.bfloat16) for g in groups],
         compiler_params=pltpu.CompilerParams(vmem_limit_bytes=12 << 20),
-        name="prepare_rows",
     )(*sources)
 
 
@@ -180,8 +181,8 @@
     )(*rows, *olds, *packs)
 
 
-def apply_rows(rows, first_row, count, old, columns, out_type):
-    width = columns[0][1].shape[1]
+def apply_rows(rows, old, columns, out_type):
+    count, width = rows.shape[0], columns[0][1].shape[1]
     flat = [a for pair in columns for a in pair]
     lead = [rows] if old is None else [rows, old]
 
@@ -189,7 +190,7 @@
         row_ref, out_ref, rest = refs[0], refs[-1], refs[len(lead) : -1]
         part = None if old is None else refs[1][...]
         for k in range(0, len(rest), 2):
-            more = fold(row_ref, pl.ds(first_row, count), rest[k][...], rest[k + 1][...])
+            more = fold(row_ref, slice(None), rest[k][...], rest[k + 1][...])
             part = more if part is None else part + more
         out_ref[...] = part.astype(out_type)
 
@@ -207,17 +208,21 @@
 ROW_MOVES = ((("z", 1), ("z", 3)), (("z", 3), ("y", 3)), (("y", 3), ("z", 1)))
 
 
+def diagonal(noise, probes):
+    return lax.optimization_barrier(noise[:, None] * probes.astype(jnp.float32))
+
+
 def on_device(embeddings, inv_length, noise, probes):
     block = probes.shape[0]
-    two = 2 * block
     f32, bf16 = jnp.float32, jnp.bfloat16
     move_a, move_b, move_c = COL_MOVES
     move_p, move_q, move_r = ROW_MOVES
     own, pair = pack_own(embeddings.T, inv_length[None, :], probes)
+    diag = diagonal(noise, probes)
 
     got_a = swap(own, move_a)
     rows_p = swap(pair, move_p)
-    pairs = join(pair, rows_p)
+    pairs = join(own, rows_p)
     rows_q = swap(pairs, move_q)
     pack_a = join(own, got_a)
     pack_b = swap(pack_a, move_b)
@@ -225,31 +230,32 @@
     other_a = partner(pack_a)
     quads = join(pairs, rows_q)
     rows_r = swap(quads, move_r)
-    row_f1, row_f2, row_n1, row_n2 = prepare_rows(
-        block, [quads, rows_r], [[(1, 2), (1, 3)], [(1, 0), (1, 1)], [(0, 2), (0, 3)], [(0, 0), (0, 1)]]
-    )
-    far = [row_f1, row_f2]
-    f1, f2, *aug_a = accumulate(far, [], [pack_a, other_a], [f32, f32])
+
+    near = prepare_rows(block, [quads], [[(0, 2), (0, 3)], [(0, 1)], [(0, 0)]])
+    row_n, row_p, row_own = near
+    n, beside, total, *aug_a = accumulate(near, [], [pack_a, other_a], [f32, f32, f32])
 
     other_b, other_c = partner(pack_b), partner(pack_c)
     pack_d = swap(pack_b, move_c)
+    far = prepare_rows(block, [rows_r], [[(0, 2), (0, 3)], [(0, 0), (0, 1)]])
+    f1 = apply_rows(far[0], None, [aug_a], f32)
+    f2 = apply_rows(far[1], None, [aug_a], f32)
     f1, f2, *aug_b = accumulate(far, [f1, f2], [pack_b, other_b], [f32, f32])
+    other_d = partner(pack_d)
     f1, f2, *aug_c = accumulate(far, [f1, f2], [pack_c, other_c], [f32, f32])
-    other_d = partner(pack_d)
-    n1 = apply_rows(row_n1, 0, two, None, [aug_a, aug_b], f32)
-    f1, *aug_d = accumulate([row_f1], [f1], [pack_d, other_d], [bf16])
+    f1, *aug_d = accumulate(far[:1], [f1], [pack_d, other_d], [bf16])
     in_1 = swap(f1, move_r)
-    f2 = apply_rows(row_f2, 0, two, f2, [aug_d], bf16)
+    f2 = apply_rows(far[1], f2, [aug_d], bf16)
     in_2 = swap(f2, move_r)
-    n1 = apply_rows(row_n1, 0, two, n1, [aug_c, aug_d], f32)
-    in_3 = swap((n1 + in_1.astype(f32)).astype(bf16), move_q)
-    columns = [aug_a, aug_b, aug_c, aug_d]
-    beside = apply_rows(row_n2, block, block, None, columns, f32)
+
+    columns = [aug_b, aug_c, aug_d]
+    n = apply_rows(row_n, n, columns, f32)
+    in_3 = swap((n + in_1.astype(f32)).astype(bf16), move_q)
+    beside = apply_rows(row_p, beside, columns, f32)
     passed = beside + in_2[block:].astype(f32) + in_3[block:].astype(f32)
     in_4 = swap(passed.astype(bf16), move_p)
-    total = apply_rows(row_n2, 0, block, None, columns, f32)
-    total = total + in_2[:block].astype(f32) + in_3[:block].astype(f32) + in_4.astype(f32)
-    return total + noise[:, None] * probes.astype(f32)
+    total = apply_rows(row_own, total, columns, f32)
+    return total + diag + in_2[:block].astype(f32) + in_3[:block].astype(f32) + in_4.astype(f32)
 
 
 def solution(mesh):

time: 79.3 us -> 77.5 us (0.977)
  Pallas kernels: 30.1 us -> 28.4 us
    pallas_call x5 -> x6, Pallas kernels: 15 us -> 12.9 us  [apply_rows(): pl.pallas_call(body, in_specs=[VMEM] * (len(lead) + len(flat)), out_specs...]
    ppermute x4, starting transfers between devices: 12.1 us -> 13.7 us  [partner(): return lax.ppermute(value, AXES, [(i, i ^ 8) for i in range(128)])]
    ppermute x11, starting transfers between devices: 19.9 us -> 18.8 us  [swap(): return lax.ppermute(value, AXES, pairs)]
  transfers between devices with their start and end apart: 15 -> 15, of which waited for: 5 -> 5; matrix products, arithmetic and copies ran while one was open for 0% -> 0% of each run, Pallas kernels for 33% -> 32%
where the time goes in v4:
time: 77.5 us; the launch traced here: 77.4 us
  starting transfers between devices  32.5 us (42%)
  Pallas kernels  28.4 us (37%)
  waiting for transfers between devices  14.2 us (18%)
  other arithmetic  1.1 us (1%)
  local copies, waits for them, and re-layouts  0.98 us (1%)
    ppermute x11, starting transfers between devices, swap(): return lax.ppermute(value, AXES, pairs)  18.8 us
    ppermute x11, waiting for transfers between devices, swap(): return lax.ppermute(value, AXES, pairs)  14.2 us
    ppermute x4, starting transfers between devices, partner(): return lax.ppermute(value, AXES, [(i, i ^ 8) for i in range(128)])  13.7 us
    pallas_call x6, Pallas kernels, apply_rows(): pl.pallas_call(body, in_specs=[VMEM] * (len(lead) + len(flat)), out_specs...  12.9 us
    pallas_call x4, Pallas kernels, accumulate(): pl.pallas_call(body, in_specs=[VMEM] * (n + m + p), out_specs=[VMEM] * (n...  12.2 us
    pallas_call x1, Pallas kernels, pack_own(): pl.pallas_call(body, in_specs=[pl.BlockSpec(memory_space=pltpu.HBM)] * 3,...  1.84 us
  transfers between devices with their start and end apart: 15, of which 5 were waited for; matrix products, arithmetic and copies ran while one was open for 0% of the time, Pallas kernels for 32%

profile of v4, /device:TPU:1, one launch (start us, length us, event | category | flops | bytes accessed | tf_op | source)
XLA Modules:
  0.0 77.4 jit_solution(8824308023413740051)
XLA Ops:
  0.0 1.8 %pack_own.1 = (bf16[384,384]{1,0:T(8,128)(2,1)}, bf16[384,128]{1,0:T(8,128)(2,1)}) custom-call(f32[64,384]{1,0:T(8,128)} %bitcast.2, f32[1,64]{1,0:T(1,128)} %bitcast.3, bf16[384,256]{1,0:T(8,128)(2,1)} %probe_hbm.1), custom_call_target="tpu_custom_call" | custom-call | tf_op jit(solution)/shard_map/pack_own/pallas_call | solution.py:85
  1.9 3.4 %collective-permute-start.2 = (bf16[384,384]{1,0:T(8,128)(2,1)}, bf16[384,384]{1,0:T(8,128)(2,1)S(1)}, u32[]{:S(2)}, u32[]{:S(2)}) collective-permute-start(bf16[384,384]{1,0:T(8,128)(2,1)} %get-tuple-element.28.a_ref), channel_id=1, source_target_pairs={{0,16},{8,56},{1,17},{9,57},{2,18},{10,58},{3,19},{11,59},{64,80},... | collective-permute-start | bytes 884744 | tf_op jit(solution)/shard_map/ppermute | solution.py:32
  5.2 4.3 %collective-permute-done.2.b_ref = bf16[384,384]{1,0:T(8,128)(2,1)S(1)} collective-permute-done((bf16[384,384]{1,0:T(8,128)(2,1)}, bf16[384,384]{1,0:T(8,128)(2,1)S(1)}, u32[]{:S(2)}, u32[]{:S(2)}) %collective-permute-start.2) | collective-permute-done | bytes 294944 | tf_op jit(solution)/shard_map/ppermute | solution.py:32
  9.6 0.0 copy-start
  9.6 1.0 %copy-done = bf16[384,384]{1,0:T(8,128)(2,1)S(1)} copy-done((bf16[384,384]{1,0:T(8,128)(2,1)S(1)}, bf16[384,384]{1,0:T(8,128)(2,1)}, u32[]{:S(2)}) %copy-start) | copy-done | bytes 294936
  10.5 0.0 copy-start.3
  10.5 0.1 shard_map.49.refs_3_
  10.6 1.6 %collective-permute-start.5 = (bf16[768,384]{1,0:T(8,128)(2,1)S(1)}, bf16[768,384]{1,0:T(8,128)(2,1)S(1)}, u32[]{:S(2)}, u32[]{:S(2)}) collective-permute-start(bf16[768,384]{1,0:T(8,128)(2,1)S(1)} %shard_map.49.refs_3_), channel_id=1, source_target_pairs={{0,48},{8,72},{1,49},{9,73},{2,50},{10,74},{3,51},{11,75},{64,112}... | collective-permute-start | bytes 1769480 | tf_op jit(solution)/shard_map/ppermute | solution.py:32
  12.1 0.0 copy-done.3
  12.1 3.8 %collective-permute-start = (bf16[384,128]{1,0:T(8,128)(2,1)S(1)}, bf16[384,128]{1,0:T(8,128)(2,1)S(1)}, u32[]{:S(2)}, u32[]{:S(2)}) collective-permute-start(bf16[384,128]{1,0:T(8,128)(2,1)S(1)} %copy-done.3), channel_id=1, source_target_pairs={{0,1},{8,11},{1,0},{9,10},{2,3},{10,9},{3,2},{11,8},{64,65},{72,75... | collective-permute-start | bytes 294920 | tf_op jit(solution)/shard_map/ppermute | solution.py:32
  15.9 2.3 %collective-permute-done.b_ref = bf16[384,128]{1,0:T(8,128)(2,1)S(1)} collective-permute-done((bf16[384,128]{1,0:T(8,128)(2,1)S(1)}, bf16[384,128]{1,0:T(8,128)(2,1)S(1)}, u32[]{:S(2)}, u32[]{:S(2)}) %collective-permute-start) | collective-permute-done | bytes 98336 | tf_op jit(solution)/shard_map/ppermute | solution.py:32
  18.2 2.3 %collective-permute-start.1 = (bf16[768,128]{1,0:T(8,128)(2,1)S(1)}, bf16[768,128]{1,0:T(8,128)(2,1)S(1)}, u32[]{:S(2)}, u32[]{:S(2)}) collective-permute-start(bf16[768,128]{1,0:T(8,128)(2,1)S(1)} %shard_map.46.a_ref), channel_id=1, source_target_pairs={{0,3},{8,76},{1,2},{9,77},{2,1},{10,78},{3,0},{11,79},{64,67},{72,... | collective-permute-start | bytes 589832 | tf_op jit(solution)/shard_map/ppermute | solution.py:32
  20.5 0.0 collective-permute-start.7
  20.5 4.1 %collective-permute-start.3 = (bf16[768,384]{1,0:T(8,128)(2,1)S(1)}, bf16[768,384]{1,0:T(8,128)(2,1)S(1)}, u32[]{:S(2)}, u32[]{:S(2)}) collective-permute-start(bf16[768,384]{1,0:T(8,128)(2,1)S(1)} %shard_map.49.refs_3_), channel_id=1, source_target_pairs={{0,8},{1,9},{2,10},{3,11},{4,12},{5,13},{6,14},{7,15},{8,0},{9,1},... | collective-permute-start | bytes 1769480 | tf_op jit(solution)/shard_map/ppermute | solution.py:36
  24.6 0.0 collective-permute-done.1.b_ref
  24.6 0.1 collective-permute-start.4
  24.7 0.0 collective-permute-done.5.refs_4_
  24.7 0.1 collective-permute-start.9
  24.8 5.1 %collective-permute-start.6 = (bf16[768,384]{1,0:T(8,128)(2,1)S(1)}, bf16[768,384]{1,0:T(8,128)(2,1)S(1)}, u32[]{:S(2)}, u32[]{:S(2)}) collective-permute-start(bf16[768,384]{1,0:T(8,128)(2,1)S(1)} %collective-permute-done.5.refs_4_), channel_id=1, source_target_pairs={{0,8},{1,9},{2,10},{3,11},{4,12},{5,13},{6,14},{7,15},{8,0},{9,1},... | collective-permute-start | bytes 1769480 | tf_op jit(solution)/shard_map/ppermute | solution.py:36
  29.9 0.7 shard_map.48
  30.6 1.0 %collective-permute-done.4.refs_0_ = bf16[1536,128]{1,0:T(8,128)(2,1)S(1)} collective-permute-done((bf16[1536,128]{1,0:T(8,128)(2,1)S(1)}, bf16[1536,128]{1,0:T(8,128)(2,1)S(1)}, u32[]{:S(2)}, u32[]{:S(2)}) %collective-permute-start.4) | collective-permute-done | bytes 393248 | tf_op jit(solution)/shard_map/ppermute | solution.py:32
  31.6 0.7 shard_map.51
  32.3 0.0 collective-permute-done.7.refs_4_
  32.3 4.2 %collective-permute-start.8 = (bf16[768,384]{1,0:T(8,128)(2,1)S(1)}, bf16[768,384]{1,0:T(8,128)(2,1)S(1)}, u32[]{:S(2)}, u32[]{:S(2)}) collective-permute-start(bf16[768,384]{1,0:T(8,128)(2,1)S(1)} %collective-permute-done.7.refs_4_), channel_id=1, source_target_pairs={{0,8},{1,9},{2,10},{3,11},{4,12},{5,13},{6,14},{7,15},{8,0},{9,1},... | collective-permute-start | bytes 1769480 | tf_op jit(solution)/shard_map/ppermute | solution.py:36
  36.5 0.0 collective-permute-done.3.refs_4_
  36.5 3.7 %shard_map.50 = (f32[768,256]{1,0:T(8,128)S(1)}, f32[384,256]{1,0:T(8,128)S(1)}, f32[384,256]{1,0:T(8,128)S(1)}, bf16[1536,256]{1,0:T(8,128)(2,1)S(1)}, bf16[1536,256]{1,0:T(8,128)(2,1)S(1)}) custom-call(bf16[768,256]{1,0:T(8,128)(2,1)S(1)} %get-tuple-element.31.refs_0_, bf16[384,256]{1,0:T(8,128)(2,1)S(1)} %get-tuple-element.32.refs_1_.refs_0_, ...), custom_call_target="tpu_custom_call" | custom-call | flops 2415919104 | bytes 1572864 | tf_op jit(solution)/shard_map/pallas_call | solution.py:173
  40.2 0.0 collective-permute-done.9.refs_2_
  40.2 0.3 collective-permute-start.10
  40.5 1.5 %shard_map.52.refs_2_ = f32[768,256]{1,0:T(8,128)S(1)} custom-call(bf16[768,256]{1,0:T(8,128)(2,1)S(1)} %get-tuple-element.34.refs_0_, bf16[1536,256]{1,0:T(8,128)(2,1)S(1)} %get-tuple-element.36.refs_1_, bf16[1536,256]{1,0:T(8,128)(2,1)S(1)} %get-tuple-element.37.refs_2_), custom_call_target="tpu_custom_call" | custom-call | flops 1207959552 | bytes 786432 | tf_op jit(solution)/shard_map/pallas_call | solution.py:197
  42.0 1.5 %shard_map.53.refs_3_ = f32[768,256]{1,0:T(8,128)S(1)} custom-call(bf16[768,256]{1,0:T(8,128)(2,1)S(1)} %get-tuple-element.35.refs_0_.refs_1_, bf16[1536,256]{1,0:T(8,128)(2,1)S(1)} %get-tuple-element.36.refs_1_, bf16[1536,256]{1,0:T(8,128)(2,1)S(1)} %get-tuple-element.37.refs_2_), custom_call_target="tpu_custom_call" | custom-call | flops 1207959552 | bytes 786432 | tf_op jit(solution)/shard_map/pallas_call | solution.py:197
  43.6 0.0 collective-permute-done.6.refs_5_
  43.6 3.3 %shard_map.54 = (f32[768,256]{1,0:T(8,128)S(1)}, f32[768,256]{1,0:T(8,128)S(1)}, bf16[1536,256]{1,0:T(8,128)(2,1)S(1)}, bf16[1536,256]{1,0:T(8,128)(2,1)S(1)}) custom-call(bf16[768,256]{1,0:T(8,128)(2,1)S(1)} %get-tuple-element.34.refs_0_, bf16[768,256]{1,0:T(8,128)(2,1)S(1)} %get-tuple-element.35.refs_0_.refs_1_, f32[768,256]{1,0:T(8,128)S(1)} %shard_map.52.refs_2_, ...), custom_call_target="tpu_custom_call" | custom-call | flops 2415919104 | bytes 1572864 | tf_op jit(solution)/shard_map/pallas_call | solution.py:173
  46.9 0.0 collective-permute-done.8.refs_5_
  46.9 3.3 %shard_map.55 = (f32[768,256]{1,0:T(8,128)S(1)}, f32[768,256]{1,0:T(8,128)S(1)}, bf16[1536,256]{1,0:T(8,128)(2,1)S(1)}, bf16[1536,256]{1,0:T(8,128)(2,1)S(1)}) custom-call(bf16[768,256]{1,0:T(8,128)(2,1)S(1)} %get-tuple-element.34.refs_0_, bf16[768,256]{1,0:T(8,128)(2,1)S(1)} %get-tuple-element.35.refs_0_.refs_1_, f32[768,256]{1,0:T(8,128)S(1)} %get-tuple-element.40.refs_2_, ...), custom_call_target="tpu_custom_call" | custom-call | flops 2415919104 | bytes 1572864 | tf_op jit(solution)/shard_map/pallas_call | solution.py:173
  50.1 0.0 collective-permute-done.10.refs_3_
  50.1 2.0 %shard_map.56 = (bf16[768,256]{1,0:T(8,128)(2,1)S(1)}, bf16[1536,256]{1,0:T(8,128)(2,1)S(1)}, bf16[1536,256]{1,0:T(8,128)(2,1)S(1)}) custom-call(bf16[768,256]{1,0:T(8,128)(2,1)S(1)} %get-tuple-element.34.refs_0_, f32[768,256]{1,0:T(8,128)S(1)} %get-tuple-element.44.refs_1_, bf16[768,384]{1,0:T(8,128)(2,1)S(1)} %collective-permute-done.9.refs_2_, ...), custom_call_target="tpu_custom_call" | custom-call | flops 1207959552 | bytes 786432 | tf_op jit(solution)/shard_map/pallas_call | solution.py:173
  52.2 0.3 collective-permute-start.12
  52.5 1.5 %shard_map.58 = bf16[768,256]{1,0:T(8,128)(2,1)S(1)} custom-call(bf16[768,256]{1,0:T(8,128)(2,1)S(1)} %get-tuple-element.35.refs_0_.refs_1_, f32[768,256]{1,0:T(8,128)S(1)} %get-tuple-element.47.refs_1_, bf16[1536,256]{1,0:T(8,128)(2,1)S(1)} %get-tuple-element.45.refs_6_.refs_2_, bf16[1536,256]{1,0:T(8,128)(2,1)S(1)} %get-tuple-element.46.refs_7_.refs_3_), custom_call_target="tpu_custom_call" | custom-call | flops 1207959552 | bytes 786432 | tf_op jit(solution)/shard_map/pallas_call | solution.py:197
  54.0 1.5 %collective-permute-start.11 = (bf16[768,256]{1,0:T(8,128)(2,1)S(1)}, bf16[768,256]{1,0:T(8,128)(2,1)S(1)}, u32[]{:S(2)}, u32[]{:S(2)}) collective-permute-start(bf16[768,256]{1,0:T(8,128)(2,1)S(1)} %shard_map.58), channel_id=1, source_target_pairs={{0,68},{8,9},{1,69},{9,8},{2,70},{10,11},{3,71},{11,10},{64,4},{72... | collective-permute-start | bytes 1179656 | tf_op jit(solution)/shard_map/ppermute | solution.py:32
  55.6 4.0 %shard_map.59 = f32[768,256]{1,0:T(8,128)S(1)} custom-call(bf16[768,256]{1,0:T(8,128)(2,1)S(1)} %get-tuple-element.31.refs_0_, f32[768,256]{1,0:T(8,128)S(1)} %get-tuple-element.48.refs_1_, bf16[1536,256]{1,0:T(8,128)(2,1)S(1)} %get-tuple-element.38.refs_2_, bf16[1536,256]{1,0:T(8,128)(2,1)S(1)} %get-tuple-element.39.refs_3_, ...), custom_call_target="tpu_custom_call" | custom-call | flops 3623878656 | bytes 786432 | tf_op jit(solution)/shard_map/pallas_call | solution.py:197
  59.6 0.0 collective-permute-done.12
  59.6 0.1 add_convert_fusion
  59.7 2.8 %collective-permute-start.13 = (bf16[768,256]{1,0:T(8,128)(2,1)S(1)}, bf16[768,256]{1,0:T(8,128)(2,1)S(1)}, u32[]{:S(2)}, u32[]{:S(2)}) collective-permute-start(bf16[768,256]{1,0:T(8,128)(2,1)S(1)} %add_convert_fusion), channel_id=1, source_target_pairs={{0,3},{8,76},{1,2},{9,77},{2,1},{10,78},{3,0},{11,79},{64,67},{72,... | collective-permute-start | bytes 1179656 | tf_op jit(solution)/shard_map/ppermute | solution.py:32
  62.5 2.1 %shard_map.60 = f32[384,256]{1,0:T(8,128)S(1)} custom-call(bf16[384,256]{1,0:T(8,128)(2,1)S(1)} %get-tuple-element.32.refs_1_.refs_0_, f32[384,256]{1,0:T(8,128)S(1)} %get-tuple-element.50.refs_1_, bf16[1536,256]{1,0:T(8,128)(2,1)S(1)} %get-tuple-element.38.refs_2_, bf16[1536,256]{1,0:T(8,128)(2,1)S(1)} %get-tuple-element.39.refs_3_, ...), custom_call_target="tpu_custom_call" | custom-call | flops 1811939328 | bytes 393216 | tf_op jit(solution)/shard_map/pallas_call | solution.py:197
  64.6 0.0 copy-start.1
  64.6 0.0 copy-start.2
  64.6 0.0 collective-permute-done.11
  64.7 5.7 %collective-permute-done.13 = bf16[768,256]{1,0:T(8,128)(2,1)S(1)} collective-permute-done((bf16[768,256]{1,0:T(8,128)(2,1)S(1)}, bf16[768,256]{1,0:T(8,128)(2,1)S(1)}, u32[]{:S(2)}, u32[]{:S(2)}) %collective-permute-start.13) | collective-permute-done | bytes 393248 | tf_op jit(solution)/shard_map/ppermute | solution.py:32
  70.4 0.1 add_convert_fusion.1
  70.5 3.0 %collective-permute-start.14 = (bf16[384,256]{1,0:T(8,128)(2,1)S(1)}, bf16[384,256]{1,0:T(8,128)(2,1)S(1)}, u32[]{:S(2)}, u32[]{:S(2)}) collective-permute-start(bf16[384,256]{1,0:T(8,128)(2,1)S(1)} %add_convert_fusion.1), channel_id=1, source_target_pairs={{0,1},{8,11},{1,0},{9,10},{2,3},{10,9},{3,2},{11,8},{64,65},{72,75... | collective-permute-start | bytes 589832 | tf_op jit(solution)/shard_map/ppermute | solution.py:32
  73.5 0.0 copy-done.1
  73.5 0.0 copy-done.2
  73.5 0.1 convert_multiply_fusion
  73.6 2.1 %shard_map.57 = f32[384,256]{1,0:T(8,128)S(1)} custom-call(bf16[384,256]{1,0:T(8,128)(2,1)S(1)} %get-tuple-element.30.refs_2_.refs_0_, f32[384,256]{1,0:T(8,128)S(1)} %get-tuple-element.33.refs_1_, bf16[1536,256]{1,0:T(8,128)(2,1)S(1)} %get-tuple-element.38.refs_2_, bf16[1536,256]{1,0:T(8,128)(2,1)S(1)} %get-tuple-element.39.refs_3_, ...), custom_call_target="tpu_custom_call" | custom-call | flops 1811939328 | bytes 393216 | tf_op jit(solution)/shard_map/pallas_call | solution.py:197
  75.8 0.8 %collective-permute-done.14 = bf16[384,256]{1,0:T(8,128)(2,1)S(1)} collective-permute-done((bf16[384,256]{1,0:T(8,128)(2,1)S(1)}, bf16[384,256]{1,0:T(8,128)(2,1)S(1)}, u32[]{:S(2)}, u32[]{:S(2)}) %collective-permute-start.14) | collective-permute-done | bytes 196640 | tf_op jit(solution)/shard_map/ppermute | solution.py:32
  76.6 0.8 %convert_add_fusion = f32[384,256]{1,0:T(8,128)} fusion(bf16[384,256]{1,0:T(8,128)(2,1)S(1)} %collective-permute-done.14, f32[384,256]{1,0:T(8,128)S(1)} %shard_map.57, f32[384,256]{1,0:T(8,128)S(1)} %convert_multiply_fusion, bf16[768,256]{1,0:T(8,128)(2,1)S(1)} %collective-permute-done.13, bf16[768,256]{1,0:T(8,128)(2,1)S(1)} %collective-permute-done.11), kind=kLoop, calls=%fused_computation.1 | loop fusion | flops 688128 | bytes 1769472 | tf_op jit(solution)/shard_map/add | solution.py:258
  (2 shorter events, 0.1 us)
Async XLA Ops:
  1.9 7.7 %collective-permute-start.2 = (bf16[384,384]{1,0:T(8,128)(2,1)}, bf16[384,384]{1,0:T(8,128)(2,1)S(1)}, u32[]{:S(2)}, u32[]{:S(2)}) collective-permute-start(bf16[384,384]{1,0:T(8,128)(2,1)} %get-tuple-element.28.a_ref), channel_id=1, source_target_pairs={{0,16},{8,56},{1,17},{9,57},{2,18},{10,58},{3,19},{11,59},{64,80},... | collective-permute-start | bytes 884744 | tf_op jit(solution)/shard_map/ppermute | solution.py:32
  9.6 1.0 %copy-start = (bf16[384,384]{1,0:T(8,128)(2,1)S(1)}, bf16[384,384]{1,0:T(8,128)(2,1)}, u32[]{:S(2)}) copy-start(bf16[384,384]{1,0:T(8,128)(2,1)} %get-tuple-element.28.a_ref) | copy-start | bytes 884740
  10.5 1.6 %copy-start.3 = (bf16[384,128]{1,0:T(8,128)(2,1)S(1)}, bf16[384,128]{1,0:T(8,128)(2,1)}, u32[]{:S(2)}) copy-start(bf16[384,128]{1,0:T(8,128)(2,1)} %get-tuple-element.29) | copy-start | bytes 294916
  10.6 14.1 %collective-permute-start.5 = (bf16[768,384]{1,0:T(8,128)(2,1)S(1)}, bf16[768,384]{1,0:T(8,128)(2,1)S(1)}, u32[]{:S(2)}, u32[]{:S(2)}) collective-permute-start(bf16[768,384]{1,0:T(8,128)(2,1)S(1)} %shard_map.49.refs_3_), channel_id=1, source_target_pairs={{0,48},{8,72},{1,49},{9,73},{2,50},{10,74},{3,51},{11,75},{64,112}... | collective-permute-start | bytes 1769480 | tf_op jit(solution)/shard_map/ppermute | solution.py:32
  12.1 6.1 %collective-permute-start = (bf16[384,128]{1,0:T(8,128)(2,1)S(1)}, bf16[384,128]{1,0:T(8,128)(2,1)S(1)}, u32[]{:S(2)}, u32[]{:S(2)}) collective-permute-start(bf16[384,128]{1,0:T(8,128)(2,1)S(1)} %copy-done.3), channel_id=1, source_target_pairs={{0,1},{8,11},{1,0},{9,10},{2,3},{10,9},{3,2},{11,8},{64,65},{72,75... | collective-permute-start | bytes 294920 | tf_op jit(solution)/shard_map/ppermute | solution.py:32
  18.2 6.3 %collective-permute-start.1 = (bf16[768,128]{1,0:T(8,128)(2,1)S(1)}, bf16[768,128]{1,0:T(8,128)(2,1)S(1)}, u32[]{:S(2)}, u32[]{:S(2)}) collective-permute-start(bf16[768,128]{1,0:T(8,128)(2,1)S(1)} %shard_map.46.a_ref), channel_id=1, source_target_pairs={{0,3},{8,76},{1,2},{9,77},{2,1},{10,78},{3,0},{11,79},{64,67},{72,... | collective-permute-start | bytes 589832 | tf_op jit(solution)/shard_map/ppermute | solution.py:32
  20.5 11.8 %collective-permute-start.7 = (bf16[768,384]{1,0:T(8,128)(2,1)S(1)}, bf16[768,384]{1,0:T(8,128)(2,1)S(1)}, u32[]{:S(2)}, u32[]{:S(2)}) collective-permute-start(bf16[768,384]{1,0:T(8,128)(2,1)S(1)} %shard_map.49.refs_3_), channel_id=1, source_target_pairs={{0,64},{8,24},{1,65},{9,25},{2,66},{10,26},{3,67},{11,27},{64,0},{... | collective-permute-start | bytes 1769480 | tf_op jit(solution)/shard_map/ppermute | solution.py:32
  20.5 16.0 %collective-permute-start.3 = (bf16[768,384]{1,0:T(8,128)(2,1)S(1)}, bf16[768,384]{1,0:T(8,128)(2,1)S(1)}, u32[]{:S(2)}, u32[]{:S(2)}) collective-permute-start(bf16[768,384]{1,0:T(8,128)(2,1)S(1)} %shard_map.49.refs_3_), channel_id=1, source_target_pairs={{0,8},{1,9},{2,10},{3,11},{4,12},{5,13},{6,14},{7,15},{8,0},{9,1},... | collective-permute-start | bytes 1769480 | tf_op jit(solution)/shard_map/ppermute | solution.py:36
  24.6 7.0 %collective-permute-start.4 = (bf16[1536,128]{1,0:T(8,128)(2,1)S(1)}, bf16[1536,128]{1,0:T(8,128)(2,1)S(1)}, u32[]{:S(2)}, u32[]{:S(2)}) collective-permute-start(bf16[1536,128]{1,0:T(8,128)(2,1)S(1)} %shard_map.47.refs_0_), channel_id=1, source_target_pairs={{0,68},{8,9},{1,69},{9,8},{2,70},{10,11},{3,71},{11,10},{64,4},{72... | collective-permute-start | bytes 1179656 | tf_op jit(solution)/shard_map/ppermute | solution.py:32
  24.7 15.5 %collective-permute-start.9 = (bf16[768,384]{1,0:T(8,128)(2,1)S(1)}, bf16[768,384]{1,0:T(8,128)(2,1)S(1)}, u32[]{:S(2)}, u32[]{:S(2)}) collective-permute-start(bf16[768,384]{1,0:T(8,128)(2,1)S(1)} %collective-permute-done.5.refs_4_), channel_id=1, source_target_pairs={{0,64},{8,24},{1,65},{9,25},{2,66},{10,26},{3,67},{11,27},{64,0},{... | collective-permute-start | bytes 1769480 | tf_op jit(solution)/shard_map/ppermute | solution.py:32
  24.8 18.8 %collective-permute-start.6 = (bf16[768,384]{1,0:T(8,128)(2,1)S(1)}, bf16[768,384]{1,0:T(8,128)(2,1)S(1)}, u32[]{:S(2)}, u32[]{:S(2)}) collective-permute-start(bf16[768,384]{1,0:T(8,128)(2,1)S(1)} %collective-permute-done.5.refs_4_), channel_id=1, source_target_pairs={{0,8},{1,9},{2,10},{3,11},{4,12},{5,13},{6,14},{7,15},{8,0},{9,1},... | collective-permute-start | bytes 1769480 | tf_op jit(solution)/shard_map/ppermute | solution.py:36
  32.3 14.6 %collective-permute-start.8 = (bf16[768,384]{1,0:T(8,128)(2,1)S(1)}, bf16[768,384]{1,0:T(8,128)(2,1)S(1)}, u32[]{:S(2)}, u32[]{:S(2)}) collective-permute-start(bf16[768,384]{1,0:T(8,128)(2,1)S(1)} %collective-permute-done.7.refs_4_), channel_id=1, source_target_pairs={{0,8},{1,9},{2,10},{3,11},{4,12},{5,13},{6,14},{7,15},{8,0},{9,1},... | collective-permute-start | bytes 1769480 | tf_op jit(solution)/shard_map/ppermute | solution.py:36
  40.2 9.9 %collective-permute-start.10 = (bf16[768,384]{1,0:T(8,128)(2,1)S(1)}, bf16[768,384]{1,0:T(8,128)(2,1)S(1)}, u32[]{:S(2)}, u32[]{:S(2)}) collective-permute-start(bf16[768,384]{1,0:T(8,128)(2,1)S(1)} %collective-permute-done.9.refs_2_), channel_id=1, source_target_pairs={{0,8},{1,9},{2,10},{3,11},{4,12},{5,13},{6,14},{7,15},{8,0},{9,1},... | collective-permute-start | bytes 1769480 | tf_op jit(solution)/shard_map/ppermute | solution.py:36
  52.2 7.4 %collective-permute-start.12 = (bf16[768,256]{1,0:T(8,128)(2,1)S(1)}, bf16[768,256]{1,0:T(8,128)(2,1)S(1)}, u32[]{:S(2)}, u32[]{:S(2)}) collective-permute-start(bf16[768,256]{1,0:T(8,128)(2,1)S(1)} %get-tuple-element.49), channel_id=1, source_target_pairs={{0,68},{8,9},{1,69},{9,8},{2,70},{10,11},{3,71},{11,10},{64,4},{72... | collective-permute-start | bytes 1179656 | tf_op jit(solution)/shard_map/ppermute | solution.py:32
  54.0 10.6 %collective-permute-start.11 = (bf16[768,256]{1,0:T(8,128)(2,1)S(1)}, bf16[768,256]{1,0:T(8,128)(2,1)S(1)}, u32[]{:S(2)}, u32[]{:S(2)}) collective-permute-start(bf16[768,256]{1,0:T(8,128)(2,1)S(1)} %shard_map.58), channel_id=1, source_target_pairs={{0,68},{8,9},{1,69},{9,8},{2,70},{10,11},{3,71},{11,10},{64,4},{72... | collective-permute-start | bytes 1179656 | tf_op jit(solution)/shard_map/ppermute | solution.py:32
  59.7 10.7 %collective-permute-start.13 = (bf16[768,256]{1,0:T(8,128)(2,1)S(1)}, bf16[768,256]{1,0:T(8,128)(2,1)S(1)}, u32[]{:S(2)}, u32[]{:S(2)}) collective-permute-start(bf16[768,256]{1,0:T(8,128)(2,1)S(1)} %add_convert_fusion), channel_id=1, source_target_pairs={{0,3},{8,76},{1,2},{9,77},{2,1},{10,78},{3,0},{11,79},{64,67},{72,... | collective-permute-start | bytes 1179656 | tf_op jit(solution)/shard_map/ppermute | solution.py:32
  64.6 8.9 %copy-start.1 = (bf16[384,256]{1,0:T(8,128)(2,1)S(1)}, bf16[384,256]{1,0:T(8,128)(2,1)}, u32[]{:S(2)}) copy-start(bf16[384,256]{1,0:T(8,128)(2,1)} %probe_hbm.1) | copy-start | bytes 589828
  64.6 8.9 %copy-start.2 = (f32[384]{0:T(512)S(1)}, f32[384]{0:T(512)}, u32[]{:S(2)}) copy-start(f32[384]{0:T(512)} %param.6) | copy-start | bytes 4612
  70.5 6.1 %collective-permute-start.14 = (bf16[384,256]{1,0:T(8,128)(2,1)S(1)}, bf16[384,256]{1,0:T(8,128)(2,1)S(1)}, u32[]{:S(2)}, u32[]{:S(2)}) collective-permute-start(bf16[384,256]{1,0:T(8,128)(2,1)S(1)} %add_convert_fusion.1), channel_id=1, source_target_pairs={{0,1},{8,11},{1,0},{9,10},{2,3},{10,9},{3,2},{11,8},{64,65},{72,75... | collective-permute-start | bytes 589832 | tf_op jit(solution)/shard_map/ppermute | solution.py:32

commit v5 on v4

--- a/solution.py
+++ b/solution.py
@@ -20,14 +20,16 @@
     return ((y % 2) * 8 + x * 2 + core) * 8 + (y // 2) * 4 + z
 
 
-def swap(value, moves):
+def swap(value, *steps):
     pairs = []
     for x in range(4):
         for y in range(4):
             for z in range(4):
-                for core, (axis, flip) in enumerate(moves):
+                for core in range(2):
                     to = {"x": x, "y": y, "z": z}
-                    to[axis] ^= flip
+                    for step in steps:
+                        axis, flip = step[core]
+                        to[axis] ^= flip
                     pairs.append((place(x, y, z, core), place(to["x"], to["y"], to["z"], core)))
     return lax.ppermute(value, AXES, pairs)
 
@@ -238,24 +240,27 @@
     other_b, other_c = partner(pack_b), partner(pack_c)
     pack_d = swap(pack_b, move_c)
     far = prepare_rows(block, [rows_r], [[(0, 2), (0, 3)], [(0, 0), (0, 1)]])
-    f1 = apply_rows(far[0], None, [aug_a], f32)
-    f2 = apply_rows(far[1], None, [aug_a], f32)
-    f1, f2, *aug_b = accumulate(far, [f1, f2], [pack_b, other_b], [f32, f32])
+    row_f1, row_f2 = far
+    f1 = apply_rows(row_f1, None, [aug_a], f32)
+    f1, *aug_b = accumulate([row_f1], [f1], [pack_b, other_b], [f32])
+    f1, *aug_c = accumulate([row_f1], [f1], [pack_c, other_c], [f32])
+    f2 = apply_rows(row_f2, None, [aug_a], f32)
     other_d = partner(pack_d)
-    f1, f2, *aug_c = accumulate(far, [f1, f2], [pack_c, other_c], [f32, f32])
-    f1, *aug_d = accumulate(far[:1], [f1], [pack_d, other_d], [bf16])
+    f2 = apply_rows(row_f2, f2, [aug_b, aug_c], f32)
+    f1, *aug_d = accumulate([row_f1], [f1], [pack_d, other_d], [bf16])
     in_1 = swap(f1, move_r)
-    f2 = apply_rows(far[1], f2, [aug_d], bf16)
+    f2 = apply_rows(row_f2, f2, [aug_d], bf16)
     in_2 = swap(f2, move_r)
 
     columns = [aug_b, aug_c, aug_d]
     n = apply_rows(row_n, n, columns, f32)
-    in_3 = swap((n + in_1.astype(f32)).astype(bf16), move_q)
     beside = apply_rows(row_p, beside, columns, f32)
-    passed = beside + in_2[block:].astype(f32) + in_3[block:].astype(f32)
-    in_4 = swap(passed.astype(bf16), move_p)
+    from_q = swap((n[:block] + in_1[:block].astype(f32)).astype(bf16), move_q)
+    from_qp = swap((n[block:] + in_1[block:].astype(f32)).astype(bf16), move_q, move_p)
+    from_p = swap((beside + in_2[block:].astype(f32)).astype(bf16), move_p)
     total = apply_rows(row_own, total, columns, f32)
-    return total + diag + in_2[:block].astype(f32) + in_3[:block].astype(f32) + in_4.astype(f32)
+    total = total + diag + in_2[:block].astype(f32)
+    return total + from_q.astype(f32) + from_qp.astype(f32) + from_p.astype(f32)
 
 
 def solution(mesh):

time: 77.5 us -> 77.9 us (level)
  waiting for transfers between devices: 14.2 us -> 15.1 us
  starting transfers between devices: 32.5 us -> 31.6 us
    pallas_call x6 -> x7, Pallas kernels: 12.9 us -> 15.6 us  [apply_rows(): pl.pallas_call(body, in_specs=[VMEM] * (len(lead) + len(flat)), out_specs...]
    pallas_call x4, Pallas kernels: 12.2 us -> 9.79 us  [accumulate(): pl.pallas_call(body, in_specs=[VMEM] * (n + m + p), out_specs=[VMEM] * (n...]
    ppermute x4, starting transfers between devices: 13.7 us -> 12.4 us  [partner(): return lax.ppermute(value, AXES, [(i, i ^ 8) for i in range(128)])]
    ppermute x11 -> x12, waiting for transfers between devices: 14.2 us -> 15.1 us  [swap(): return lax.ppermute(value, AXES, pairs)]
    ppermute x11 -> x12, starting transfers between devices: 18.8 us -> 19.1 us  [swap(): return lax.ppermute(value, AXES, pairs)]
  transfers between devices with their start and end apart: 15 -> 16, of which waited for: 5 -> 6; matrix products, arithmetic and copies ran while one was open for 0% -> 0% of each run, Pallas kernels for 32% -> 32%
where the time goes in v5:
time: 77.9 us; the launch traced here: 77.8 us
  starting transfers between devices  31.6 us (41%)
  Pallas kernels  28.8 us (37%)
  waiting for transfers between devices  15.1 us (19%)
  other arithmetic  1.11 us (1%)
  local copies, waits for them, and re-layouts  0.97 us (1%)
    ppermute x12, starting transfers between devices, swap(): return lax.ppermute(value, AXES, pairs)  19.1 us
    pallas_call x7, Pallas kernels, apply_rows(): pl.pallas_call(body, in_specs=[VMEM] * (len(lead) + len(flat)), out_specs...  15.6 us
    ppermute x12, waiting for transfers between devices, swap(): return lax.ppermute(value, AXES, pairs)  15.1 us
    ppermute x4, starting transfers between devices, partner(): return lax.ppermute(value, AXES, [(i, i ^ 8) for i in range(128)])  12.4 us
    pallas_call x4, Pallas kernels, accumulate(): pl.pallas_call(body, in_specs=[VMEM] * (n + m + p), out_specs=[VMEM] * (n...  9.79 us
    pallas_call x1, Pallas kernels, pack_own(): pl.pallas_call(body, in_specs=[pl.BlockSpec(memory_space=pltpu.HBM)] * 3,...  1.84 us
  transfers between devices with their start and end apart: 16, of which 6 were waited for; matrix products, arithmetic and copies ran while one was open for 0% of the time, Pallas kernels for 32%

profile of v5, /device:TPU:1, one launch (start us, length us, event | category | flops | bytes accessed | tf_op | source)
XLA Modules:
  0.0 77.8 jit_solution(12717728770357412637)
XLA Ops:
  0.0 1.8 %pack_own.1 = (bf16[384,384]{1,0:T(8,128)(2,1)}, bf16[384,128]{1,0:T(8,128)(2,1)}) custom-call(f32[64,384]{1,0:T(8,128)} %bitcast.2, f32[1,64]{1,0:T(1,128)} %bitcast.3, bf16[384,256]{1,0:T(8,128)(2,1)} %probe_hbm.1), custom_call_target="tpu_custom_call" | custom-call | tf_op jit(solution)/shard_map/pack_own/pallas_call | solution.py:87
  1.8 3.4 %collective-permute-start.2 = (bf16[384,384]{1,0:T(8,128)(2,1)}, bf16[384,384]{1,0:T(8,128)(2,1)S(1)}, u32[]{:S(2)}, u32[]{:S(2)}) collective-permute-start(bf16[384,384]{1,0:T(8,128)(2,1)} %get-tuple-element.26.a_ref), channel_id=1, source_target_pairs={{0,16},{8,56},{1,17},{9,57},{2,18},{10,58},{3,19},{11,59},{64,80},... | collective-permute-start | bytes 884744 | tf_op jit(solution)/shard_map/ppermute | solution.py:34
  5.2 4.3 %collective-permute-done.2.b_ref = bf16[384,384]{1,0:T(8,128)(2,1)S(1)} collective-permute-done((bf16[384,384]{1,0:T(8,128)(2,1)}, bf16[384,384]{1,0:T(8,128)(2,1)S(1)}, u32[]{:S(2)}, u32[]{:S(2)}) %collective-permute-start.2) | collective-permute-done | bytes 294944 | tf_op jit(solution)/shard_map/ppermute | solution.py:34
  9.5 0.0 copy-start
  9.5 1.0 %copy-done = bf16[384,384]{1,0:T(8,128)(2,1)S(1)} copy-done((bf16[384,384]{1,0:T(8,128)(2,1)S(1)}, bf16[384,384]{1,0:T(8,128)(2,1)}, u32[]{:S(2)}) %copy-start) | copy-done | bytes 294936
  10.5 0.0 copy-start.3
  10.5 0.1 shard_map.49.refs_3_
  10.6 1.6 %collective-permute-start.5 = (bf16[768,384]{1,0:T(8,128)(2,1)S(1)}, bf16[768,384]{1,0:T(8,128)(2,1)S(1)}, u32[]{:S(2)}, u32[]{:S(2)}) collective-permute-start(bf16[768,384]{1,0:T(8,128)(2,1)S(1)} %shard_map.49.refs_3_), channel_id=1, source_target_pairs={{0,48},{8,72},{1,49},{9,73},{2,50},{10,74},{3,51},{11,75},{64,112}... | collective-permute-start | bytes 1769480 | tf_op jit(solution)/shard_map/ppermute | solution.py:34
  12.1 0.0 copy-done.3
  12.1 3.8 %collective-permute-start = (bf16[384,128]{1,0:T(8,128)(2,1)S(1)}, bf16[384,128]{1,0:T(8,128)(2,1)S(1)}, u32[]{:S(2)}, u32[]{:S(2)}) collective-permute-start(bf16[384,128]{1,0:T(8,128)(2,1)S(1)} %copy-done.3), channel_id=1, source_target_pairs={{0,1},{8,11},{1,0},{9,10},{2,3},{10,9},{3,2},{11,8},{64,65},{72,75... | collective-permute-start | bytes 294920 | tf_op jit(solution)/shard_map/ppermute | solution.py:34
  15.9 0.3 collective-permute-start.7
  16.2 2.0 %collective-permute-done.b_ref = bf16[384,128]{1,0:T(8,128)(2,1)S(1)} collective-permute-done((bf16[384,128]{1,0:T(8,128)(2,1)S(1)}, bf16[384,128]{1,0:T(8,128)(2,1)S(1)}, u32[]{:S(2)}, u32[]{:S(2)}) %collective-permute-start) | collective-permute-done | bytes 98336 | tf_op jit(solution)/shard_map/ppermute | solution.py:34
  18.2 2.3 %collective-permute-start.1 = (bf16[768,128]{1,0:T(8,128)(2,1)S(1)}, bf16[768,128]{1,0:T(8,128)(2,1)S(1)}, u32[]{:S(2)}, u32[]{:S(2)}) collective-permute-start(bf16[768,128]{1,0:T(8,128)(2,1)S(1)} %shard_map.46.a_ref), channel_id=1, source_target_pairs={{0,3},{8,76},{1,2},{9,77},{2,1},{10,78},{3,0},{11,79},{64,67},{72,... | collective-permute-start | bytes 589832 | tf_op jit(solution)/shard_map/ppermute | solution.py:34
  20.5 2.5 %collective-permute-start.3 = (bf16[768,384]{1,0:T(8,128)(2,1)S(1)}, bf16[768,384]{1,0:T(8,128)(2,1)S(1)}, u32[]{:S(2)}, u32[]{:S(2)}) collective-permute-start(bf16[768,384]{1,0:T(8,128)(2,1)S(1)} %shard_map.49.refs_3_), channel_id=1, source_target_pairs={{0,8},{1,9},{2,10},{3,11},{4,12},{5,13},{6,14},{7,15},{8,0},{9,1},... | collective-permute-start | bytes 1769480 | tf_op jit(solution)/shard_map/ppermute | solution.py:38
  23.0 1.4 %collective-permute-done.1.b_ref = bf16[768,128]{1,0:T(8,128)(2,1)S(1)} collective-permute-done((bf16[768,128]{1,0:T(8,128)(2,1)S(1)}, bf16[768,128]{1,0:T(8,128)(2,1)S(1)}, u32[]{:S(2)}, u32[]{:S(2)}) %collective-permute-start.1) | collective-permute-done | bytes 196640 | tf_op jit(solution)/shard_map/ppermute | solution.py:34
  24.4 0.1 collective-permute-start.4
  24.5 0.0 collective-permute-done.5.refs_2_
  24.5 0.1 collective-permute-start.9
  24.6 5.3 %collective-permute-start.6 = (bf16[768,384]{1,0:T(8,128)(2,1)S(1)}, bf16[768,384]{1,0:T(8,128)(2,1)S(1)}, u32[]{:S(2)}, u32[]{:S(2)}) collective-permute-start(bf16[768,384]{1,0:T(8,128)(2,1)S(1)} %collective-permute-done.5.refs_2_), channel_id=1, source_target_pairs={{0,8},{1,9},{2,10},{3,11},{4,12},{5,13},{6,14},{7,15},{8,0},{9,1},... | collective-permute-start | bytes 1769480 | tf_op jit(solution)/shard_map/ppermute | solution.py:38
  29.9 0.0 collective-permute-done.7.refs_2_
  29.9 0.0 collective-permute-start.8
  29.9 0.7 shard_map.48
  30.6 0.8 collective-permute-done.4.refs_0_
  31.4 0.7 shard_map.51
  32.1 0.0 collective-permute-done.3.refs_4_
  32.1 3.7 %shard_map.50 = (f32[768,256]{1,0:T(8,128)S(1)}, f32[384,256]{1,0:T(8,128)S(1)}, f32[384,256]{1,0:T(8,128)S(1)}, bf16[1536,256]{1,0:T(8,128)(2,1)S(1)}, bf16[1536,256]{1,0:T(8,128)(2,1)S(1)}) custom-call(bf16[768,256]{1,0:T(8,128)(2,1)S(1)} %get-tuple-element.29.refs_0_, bf16[384,256]{1,0:T(8,128)(2,1)S(1)} %get-tuple-element.30.refs_1_.refs_0_, ...), custom_call_target="tpu_custom_call" | custom-call | flops 2415919104 | bytes 1572864 | tf_op jit(solution)/shard_map/pallas_call | solution.py:175
  35.8 0.0 collective-permute-done.9.refs_2_
  35.8 4.6 %collective-permute-start.10 = (bf16[768,384]{1,0:T(8,128)(2,1)S(1)}, bf16[768,384]{1,0:T(8,128)(2,1)S(1)}, u32[]{:S(2)}, u32[]{:S(2)}) collective-permute-start(bf16[768,384]{1,0:T(8,128)(2,1)S(1)} %collective-permute-done.9.refs_2_), channel_id=1, source_target_pairs={{0,8},{1,9},{2,10},{3,11},{4,12},{5,13},{6,14},{7,15},{8,0},{9,1},... | collective-permute-start | bytes 1769480 | tf_op jit(solution)/shard_map/ppermute | solution.py:38
  40.4 1.5 %shard_map.57.refs_1_ = f32[768,256]{1,0:T(8,128)S(1)} custom-call(bf16[768,256]{1,0:T(8,128)(2,1)S(1)} %get-tuple-element.43.refs_0_, bf16[1536,256]{1,0:T(8,128)(2,1)S(1)} %get-tuple-element.33.refs_1_, bf16[1536,256]{1,0:T(8,128)(2,1)S(1)} %get-tuple-element.34.refs_2_), custom_call_target="tpu_custom_call" | custom-call | flops 1207959552 | bytes 786432 | tf_op jit(solution)/shard_map/pallas_call | solution.py:199
  41.9 1.5 %shard_map.52.refs_1_ = f32[768,256]{1,0:T(8,128)S(1)} custom-call(bf16[768,256]{1,0:T(8,128)(2,1)S(1)} %get-tuple-element.32.refs_0_, bf16[1536,256]{1,0:T(8,128)(2,1)S(1)} %get-tuple-element.33.refs_1_, bf16[1536,256]{1,0:T(8,128)(2,1)S(1)} %get-tuple-element.34.refs_2_), custom_call_target="tpu_custom_call" | custom-call | flops 1207959552 | bytes 786432 | tf_op jit(solution)/shard_map/pallas_call | solution.py:199
  43.5 0.0 collective-permute-done.6.refs_3_
  43.5 2.0 %shard_map.53 = (f32[768,256]{1,0:T(8,128)S(1)}, bf16[1536,256]{1,0:T(8,128)(2,1)S(1)}, bf16[1536,256]{1,0:T(8,128)(2,1)S(1)}) custom-call(bf16[768,256]{1,0:T(8,128)(2,1)S(1)} %get-tuple-element.32.refs_0_, f32[768,256]{1,0:T(8,128)S(1)} %shard_map.52.refs_1_, bf16[768,384]{1,0:T(8,128)(2,1)S(1)} %collective-permute-done.5.refs_2_, ...), custom_call_target="tpu_custom_call" | custom-call | flops 1207959552 | bytes 786432 | tf_op jit(solution)/shard_map/pallas_call | solution.py:175
  45.5 0.0 collective-permute-done.8.refs_3_
  45.5 2.0 %shard_map.54 = (f32[768,256]{1,0:T(8,128)S(1)}, bf16[1536,256]{1,0:T(8,128)(2,1)S(1)}, bf16[1536,256]{1,0:T(8,128)(2,1)S(1)}) custom-call(bf16[768,256]{1,0:T(8,128)(2,1)S(1)} %get-tuple-element.32.refs_0_, f32[768,256]{1,0:T(8,128)S(1)} %get-tuple-element.37.refs_1_, bf16[768,384]{1,0:T(8,128)(2,1)S(1)} %collective-permute-done.7.refs_2_, ...), custom_call_target="tpu_custom_call" | custom-call | flops 1207959552 | bytes 786432 | tf_op jit(solution)/shard_map/pallas_call | solution.py:175
  47.6 2.8 %shard_map.58.refs_1_ = f32[768,256]{1,0:T(8,128)S(1)} custom-call(bf16[768,256]{1,0:T(8,128)(2,1)S(1)} %get-tuple-element.43.refs_0_, f32[768,256]{1,0:T(8,128)S(1)} %shard_map.57.refs_1_, bf16[1536,256]{1,0:T(8,128)(2,1)S(1)} %get-tuple-element.35.refs_2_, bf16[1536,256]{1,0:T(8,128)(2,1)S(1)} %get-tuple-element.36.refs_3_, ...), custom_call_target="tpu_custom_call" | custom-call | flops 2415919104 | bytes 786432 | tf_op jit(solution)/shard_map/pallas_call | solution.py:199
  50.3 0.0 collective-permute-done.10.refs_3_
  50.3 2.0 %shard_map.55 = (bf16[768,256]{1,0:T(8,128)(2,1)S(1)}, bf16[1536,256]{1,0:T(8,128)(2,1)S(1)}, bf16[1536,256]{1,0:T(8,128)(2,1)S(1)}) custom-call(bf16[768,256]{1,0:T(8,128)(2,1)S(1)} %get-tuple-element.32.refs_0_, f32[768,256]{1,0:T(8,128)S(1)} %get-tuple-element.40.refs_1_, bf16[768,384]{1,0:T(8,128)(2,1)S(1)} %collective-permute-done.9.refs_2_, ...), custom_call_target="tpu_custom_call" | custom-call | flops 1207959552 | bytes 786432 | tf_op jit(solution)/shard_map/pallas_call | solution.py:175
  52.4 0.3 collective-permute-start.12
  52.7 1.5 %shard_map.59 = bf16[768,256]{1,0:T(8,128)(2,1)S(1)} custom-call(bf16[768,256]{1,0:T(8,128)(2,1)S(1)} %get-tuple-element.43.refs_0_, f32[768,256]{1,0:T(8,128)S(1)} %shard_map.58.refs_1_, bf16[1536,256]{1,0:T(8,128)(2,1)S(1)} %get-tuple-element.41.refs_6_.refs_2_, bf16[1536,256]{1,0:T(8,128)(2,1)S(1)} %get-tuple-element.42.refs_7_.refs_3_), custom_call_target="tpu_custom_call" | custom-call | flops 1207959552 | bytes 786432 | tf_op jit(solution)/shard_map/pallas_call | solution.py:199
  54.2 1.5 %collective-permute-start.11 = (bf16[768,256]{1,0:T(8,128)(2,1)S(1)}, bf16[768,256]{1,0:T(8,128)(2,1)S(1)}, u32[]{:S(2)}, u32[]{:S(2)}) collective-permute-start(bf16[768,256]{1,0:T(8,128)(2,1)S(1)} %shard_map.59), channel_id=1, source_target_pairs={{0,68},{8,9},{1,69},{9,8},{2,70},{10,11},{3,71},{11,10},{64,4},{72... | collective-permute-start | bytes 1179656 | tf_op jit(solution)/shard_map/ppermute | solution.py:34
  55.8 4.0 %shard_map.60 = f32[768,256]{1,0:T(8,128)S(1)} custom-call(bf16[768,256]{1,0:T(8,128)(2,1)S(1)} %get-tuple-element.29.refs_0_, f32[768,256]{1,0:T(8,128)S(1)} %get-tuple-element.44.refs_1_, bf16[1536,256]{1,0:T(8,128)(2,1)S(1)} %get-tuple-element.35.refs_2_, bf16[1536,256]{1,0:T(8,128)(2,1)S(1)} %get-tuple-element.36.refs_3_, ...), custom_call_target="tpu_custom_call" | custom-call | flops 3623878656 | bytes 786432 | tf_op jit(solution)/shard_map/pallas_call | solution.py:199
  59.8 2.1 %shard_map.61 = f32[384,256]{1,0:T(8,128)S(1)} custom-call(bf16[384,256]{1,0:T(8,128)(2,1)S(1)} %get-tuple-element.30.refs_1_.refs_0_, f32[384,256]{1,0:T(8,128)S(1)} %get-tuple-element.46.refs_1_, bf16[1536,256]{1,0:T(8,128)(2,1)S(1)} %get-tuple-element.35.refs_2_, bf16[1536,256]{1,0:T(8,128)(2,1)S(1)} %get-tuple-element.36.refs_3_, ...), custom_call_target="tpu_custom_call" | custom-call | flops 1811939328 | bytes 393216 | tf_op jit(solution)/shard_map/pallas_call | solution.py:199
  61.9 0.0 collective-permute-done.12
  61.9 0.1 fusion.1
  62.0 2.8 %collective-permute-start.13 = (bf16[384,256]{1,0:T(8,128)(2,1)S(1)}, bf16[384,256]{1,0:T(8,128)(2,1)S(1)}, u32[]{:S(2)}, u32[]{:S(2)}) collective-permute-start(bf16[384,256]{1,0:T(8,128)(2,1)S(1)} %get-tuple-element.47), channel_id=1, source_target_pairs={{0,3},{8,76},{1,2},{9,77},{2,1},{10,78},{3,0},{11,79},{64,67},{72,... | collective-permute-start | bytes 589832 | tf_op jit(solution)/shard_map/ppermute | solution.py:34
  64.8 0.0 copy-start.1
  64.8 0.0 copy-start.2
  64.8 2.8 %collective-permute-start.14 = (bf16[384,256]{1,0:T(8,128)(2,1)S(1)}, bf16[384,256]{1,0:T(8,128)(2,1)S(1)}, u32[]{:S(2)}, u32[]{:S(2)}) collective-permute-start(bf16[384,256]{1,0:T(8,128)(2,1)S(1)} %get-tuple-element.48), channel_id=1, source_target_pairs={{0,2},{8,79},{1,3},{9,78},{2,0},{10,77},{3,1},{11,76},{64,66},{72,... | collective-permute-start | bytes 589832 | tf_op jit(solution)/shard_map/ppermute | solution.py:34
  67.6 0.0 collective-permute-done.11
  67.7 0.3 collective-permute-start.15
  67.9 0.0 copy-done.1
  67.9 0.0 copy-done.2
  67.9 0.1 convert_multiply_fusion
  68.1 2.1 %shard_map.56 = f32[384,256]{1,0:T(8,128)S(1)} custom-call(bf16[384,256]{1,0:T(8,128)(2,1)S(1)} %get-tuple-element.28.refs_2_.refs_0_, f32[384,256]{1,0:T(8,128)S(1)} %get-tuple-element.31.refs_1_, bf16[1536,256]{1,0:T(8,128)(2,1)S(1)} %get-tuple-element.35.refs_2_, bf16[1536,256]{1,0:T(8,128)(2,1)S(1)} %get-tuple-element.36.refs_3_, ...), custom_call_target="tpu_custom_call" | custom-call | flops 1811939328 | bytes 393216 | tf_op jit(solution)/shard_map/pallas_call | solution.py:199
  70.2 0.0 collective-permute-done.13
  70.2 3.6 %collective-permute-done.14 = bf16[384,256]{1,0:T(8,128)(2,1)S(1)} collective-permute-done((bf16[384,256]{1,0:T(8,128)(2,1)S(1)}, bf16[384,256]{1,0:T(8,128)(2,1)S(1)}, u32[]{:S(2)}, u32[]{:S(2)}) %collective-permute-start.14) | collective-permute-done | bytes 196640 | tf_op jit(solution)/shard_map/ppermute | solution.py:34
  73.8 3.0 %collective-permute-done.15 = bf16[384,256]{1,0:T(8,128)(2,1)S(1)} collective-permute-done((bf16[384,256]{1,0:T(8,128)(2,1)S(1)}, bf16[384,256]{1,0:T(8,128)(2,1)S(1)}, u32[]{:S(2)}, u32[]{:S(2)}) %collective-permute-start.15) | collective-permute-done | bytes 196640 | tf_op jit(solution)/shard_map/ppermute | solution.py:34
  76.9 0.9 %convert_add_fusion = f32[384,256]{1,0:T(8,128)} fusion(bf16[384,256]{1,0:T(8,128)(2,1)S(1)} %collective-permute-done.15, bf16[384,256]{1,0:T(8,128)(2,1)S(1)} %collective-permute-done.14, bf16[384,256]{1,0:T(8,128)(2,1)S(1)} %collective-permute-done.13, f32[384,256]{1,0:T(8,128)S(1)} %shard_map.56, f32[384,256]{1,0:T(8,128)S(1)} %convert_multiply_fusion, ...), kind=kLoop, calls=%fused_computation.4 | loop fusion | flops 884736 | bytes 1966080 | tf_op jit(solution)/shard_map/add | solution.py:263
  (3 shorter events, 0.1 us)
Async XLA Ops:
  1.8 7.7 %collective-permute-start.2 = (bf16[384,384]{1,0:T(8,128)(2,1)}, bf16[384,384]{1,0:T(8,128)(2,1)S(1)}, u32[]{:S(2)}, u32[]{:S(2)}) collective-permute-start(bf16[384,384]{1,0:T(8,128)(2,1)} %get-tuple-element.26.a_ref), channel_id=1, source_target_pairs={{0,16},{8,56},{1,17},{9,57},{2,18},{10,58},{3,19},{11,59},{64,80},... | collective-permute-start | bytes 884744 | tf_op jit(solution)/shard_map/ppermute | solution.py:34
  9.5 1.0 %copy-start = (bf16[384,384]{1,0:T(8,128)(2,1)S(1)}, bf16[384,384]{1,0:T(8,128)(2,1)}, u32[]{:S(2)}) copy-start(bf16[384,384]{1,0:T(8,128)(2,1)} %get-tuple-element.26.a_ref) | copy-start | bytes 884740
  10.5 1.6 %copy-start.3 = (bf16[384,128]{1,0:T(8,128)(2,1)S(1)}, bf16[384,128]{1,0:T(8,128)(2,1)}, u32[]{:S(2)}) copy-start(bf16[384,128]{1,0:T(8,128)(2,1)} %get-tuple-element.27) | copy-start | bytes 294916
  10.6 13.9 %collective-permute-start.5 = (bf16[768,384]{1,0:T(8,128)(2,1)S(1)}, bf16[768,384]{1,0:T(8,128)(2,1)S(1)}, u32[]{:S(2)}, u32[]{:S(2)}) collective-permute-start(bf16[768,384]{1,0:T(8,128)(2,1)S(1)} %shard_map.49.refs_3_), channel_id=1, source_target_pairs={{0,48},{8,72},{1,49},{9,73},{2,50},{10,74},{3,51},{11,75},{64,112}... | collective-permute-start | bytes 1769480 | tf_op jit(solution)/shard_map/ppermute | solution.py:34
  12.1 6.1 %collective-permute-start = (bf16[384,128]{1,0:T(8,128)(2,1)S(1)}, bf16[384,128]{1,0:T(8,128)(2,1)S(1)}, u32[]{:S(2)}, u32[]{:S(2)}) collective-permute-start(bf16[384,128]{1,0:T(8,128)(2,1)S(1)} %copy-done.3), channel_id=1, source_target_pairs={{0,1},{8,11},{1,0},{9,10},{2,3},{10,9},{3,2},{11,8},{64,65},{72,75... | collective-permute-start | bytes 294920 | tf_op jit(solution)/shard_map/ppermute | solution.py:34
  15.9 14.0 %collective-permute-start.7 = (bf16[768,384]{1,0:T(8,128)(2,1)S(1)}, bf16[768,384]{1,0:T(8,128)(2,1)S(1)}, u32[]{:S(2)}, u32[]{:S(2)}) collective-permute-start(bf16[768,384]{1,0:T(8,128)(2,1)S(1)} %shard_map.49.refs_3_), channel_id=1, source_target_pairs={{0,64},{8,24},{1,65},{9,25},{2,66},{10,26},{3,67},{11,27},{64,0},{... | collective-permute-start | bytes 1769480 | tf_op jit(solution)/shard_map/ppermute | solution.py:34
  18.2 6.1 %collective-permute-start.1 = (bf16[768,128]{1,0:T(8,128)(2,1)S(1)}, bf16[768,128]{1,0:T(8,128)(2,1)S(1)}, u32[]{:S(2)}, u32[]{:S(2)}) collective-permute-start(bf16[768,128]{1,0:T(8,128)(2,1)S(1)} %shard_map.46.a_ref), channel_id=1, source_target_pairs={{0,3},{8,76},{1,2},{9,77},{2,1},{10,78},{3,0},{11,79},{64,67},{72,... | collective-permute-start | bytes 589832 | tf_op jit(solution)/shard_map/ppermute | solution.py:34
  20.5 11.6 %collective-permute-start.3 = (bf16[768,384]{1,0:T(8,128)(2,1)S(1)}, bf16[768,384]{1,0:T(8,128)(2,1)S(1)}, u32[]{:S(2)}, u32[]{:S(2)}) collective-permute-start(bf16[768,384]{1,0:T(8,128)(2,1)S(1)} %shard_map.49.refs_3_), channel_id=1, source_target_pairs={{0,8},{1,9},{2,10},{3,11},{4,12},{5,13},{6,14},{7,15},{8,0},{9,1},... | collective-permute-start | bytes 1769480 | tf_op jit(solution)/shard_map/ppermute | solution.py:38
  24.4 7.0 %collective-permute-start.4 = (bf16[1536,128]{1,0:T(8,128)(2,1)S(1)}, bf16[1536,128]{1,0:T(8,128)(2,1)S(1)}, u32[]{:S(2)}, u32[]{:S(2)}) collective-permute-start(bf16[1536,128]{1,0:T(8,128)(2,1)S(1)} %shard_map.47.refs_0_), channel_id=1, source_target_pairs={{0,68},{8,9},{1,69},{9,8},{2,70},{10,11},{3,71},{11,10},{64,4},{72... | collective-permute-start | bytes 1179656 | tf_op jit(solution)/shard_map/ppermute | solution.py:34
  24.5 11.3 %collective-permute-start.9 = (bf16[768,384]{1,0:T(8,128)(2,1)S(1)}, bf16[768,384]{1,0:T(8,128)(2,1)S(1)}, u32[]{:S(2)}, u32[]{:S(2)}) collective-permute-start(bf16[768,384]{1,0:T(8,128)(2,1)S(1)} %collective-permute-done.5.refs_2_), channel_id=1, source_target_pairs={{0,64},{8,24},{1,65},{9,25},{2,66},{10,26},{3,67},{11,27},{64,0},{... | collective-permute-start | bytes 1769480 | tf_op jit(solution)/shard_map/ppermute | solution.py:34
  24.6 18.9 %collective-permute-start.6 = (bf16[768,384]{1,0:T(8,128)(2,1)S(1)}, bf16[768,384]{1,0:T(8,128)(2,1)S(1)}, u32[]{:S(2)}, u32[]{:S(2)}) collective-permute-start(bf16[768,384]{1,0:T(8,128)(2,1)S(1)} %collective-permute-done.5.refs_2_), channel_id=1, source_target_pairs={{0,8},{1,9},{2,10},{3,11},{4,12},{5,13},{6,14},{7,15},{8,0},{9,1},... | collective-permute-start | bytes 1769480 | tf_op jit(solution)/shard_map/ppermute | solution.py:38
  29.9 15.6 %collective-permute-start.8 = (bf16[768,384]{1,0:T(8,128)(2,1)S(1)}, bf16[768,384]{1,0:T(8,128)(2,1)S(1)}, u32[]{:S(2)}, u32[]{:S(2)}) collective-permute-start(bf16[768,384]{1,0:T(8,128)(2,1)S(1)} %collective-permute-done.7.refs_2_), channel_id=1, source_target_pairs={{0,8},{1,9},{2,10},{3,11},{4,12},{5,13},{6,14},{7,15},{8,0},{9,1},... | collective-permute-start | bytes 1769480 | tf_op jit(solution)/shard_map/ppermute | solution.py:38
  35.8 14.6 %collective-permute-start.10 = (bf16[768,384]{1,0:T(8,128)(2,1)S(1)}, bf16[768,384]{1,0:T(8,128)(2,1)S(1)}, u32[]{:S(2)}, u32[]{:S(2)}) collective-permute-start(bf16[768,384]{1,0:T(8,128)(2,1)S(1)} %collective-permute-done.9.refs_2_), channel_id=1, source_target_pairs={{0,8},{1,9},{2,10},{3,11},{4,12},{5,13},{6,14},{7,15},{8,0},{9,1},... | collective-permute-start | bytes 1769480 | tf_op jit(solution)/shard_map/ppermute | solution.py:38
  52.4 9.5 %collective-permute-start.12 = (bf16[768,256]{1,0:T(8,128)(2,1)S(1)}, bf16[768,256]{1,0:T(8,128)(2,1)S(1)}, u32[]{:S(2)}, u32[]{:S(2)}) collective-permute-start(bf16[768,256]{1,0:T(8,128)(2,1)S(1)} %get-tuple-element.45), channel_id=1, source_target_pairs={{0,68},{8,9},{1,69},{9,8},{2,70},{10,11},{3,71},{11,10},{64,4},{72... | collective-permute-start | bytes 1179656 | tf_op jit(solution)/shard_map/ppermute | solution.py:34
  54.2 13.4 %collective-permute-start.11 = (bf16[768,256]{1,0:T(8,128)(2,1)S(1)}, bf16[768,256]{1,0:T(8,128)(2,1)S(1)}, u32[]{:S(2)}, u32[]{:S(2)}) collective-permute-start(bf16[768,256]{1,0:T(8,128)(2,1)S(1)} %shard_map.59), channel_id=1, source_target_pairs={{0,68},{8,9},{1,69},{9,8},{2,70},{10,11},{3,71},{11,10},{64,4},{72... | collective-permute-start | bytes 1179656 | tf_op jit(solution)/shard_map/ppermute | solution.py:34
  62.0 8.2 %collective-permute-start.13 = (bf16[384,256]{1,0:T(8,128)(2,1)S(1)}, bf16[384,256]{1,0:T(8,128)(2,1)S(1)}, u32[]{:S(2)}, u32[]{:S(2)}) collective-permute-start(bf16[384,256]{1,0:T(8,128)(2,1)S(1)} %get-tuple-element.47), channel_id=1, source_target_pairs={{0,3},{8,76},{1,2},{9,77},{2,1},{10,78},{3,0},{11,79},{64,67},{72,... | collective-permute-start | bytes 589832 | tf_op jit(solution)/shard_map/ppermute | solution.py:34
  64.8 3.1 %copy-start.1 = (bf16[384,256]{1,0:T(8,128)(2,1)S(1)}, bf16[384,256]{1,0:T(8,128)(2,1)}, u32[]{:S(2)}) copy-start(bf16[384,256]{1,0:T(8,128)(2,1)} %probe_hbm.1) | copy-start | bytes 589828
  64.8 3.1 %copy-start.2 = (f32[384]{0:T(512)S(1)}, f32[384]{0:T(512)}, u32[]{:S(2)}) copy-start(f32[384]{0:T(512)} %param.6) | copy-start | bytes 4612
  64.8 9.0 %collective-permute-start.14 = (bf16[384,256]{1,0:T(8,128)(2,1)S(1)}, bf16[384,256]{1,0:T(8,128)(2,1)S(1)}, u32[]{:S(2)}, u32[]{:S(2)}) collective-permute-start(bf16[384,256]{1,0:T(8,128)(2,1)S(1)} %get-tuple-element.48), channel_id=1, source_target_pairs={{0,2},{8,79},{1,3},{9,78},{2,0},{10,77},{3,1},{11,76},{64,66},{72,... | collective-permute-start | bytes 589832 | tf_op jit(solution)/shard_map/ppermute | solution.py:34
  67.7 9.2 %collective-permute-start.15 = (bf16[384,256]{1,0:T(8,128)(2,1)S(1)}, bf16[384,256]{1,0:T(8,128)(2,1)S(1)}, u32[]{:S(2)}, u32[]{:S(2)}) collective-permute-start(bf16[384,256]{1,0:T(8,128)(2,1)S(1)} %add_convert_fusion), channel_id=1, source_target_pairs={{0,1},{8,11},{1,0},{9,10},{2,3},{10,9},{3,2},{11,8},{64,65},{72,75... | collective-permute-start | bytes 589832 | tf_op jit(solution)/shard_map/ppermute | solution.py:34

commit v6 on v5

--- a/solution.py
+++ b/solution.py
@@ -102,20 +102,22 @@
     )(embeddings_t, inv_length, probes)
 
 
-def join(a, b):
-    width = b.shape[1]
-
-    def body(a_ref, b_ref, out_ref):
-        out_ref[: a.shape[0], :] = a_ref[:, :width]
-        out_ref[a.shape[0] :, :] = b_ref[...]
-
-    return pl.pallas_call(
-        body,
-        in_specs=[VMEM] * 2,
+def join(first, *others):
+    count, width = others[0].shape
+
+    def body(*refs):
+        out_ref = refs[-1]
+        out_ref[:count, :] = refs[0][:, :width]
+        for i, ref in enumerate(refs[1:-1], 1):
+            out_ref[i * count : (i + 1) * count, :] = ref[...]
+
+    return pl.pallas_call(
+        body,
+        in_specs=[VMEM] * (1 + len(others)),
         out_specs=VMEM,
-        out_shape=jax.ShapeDtypeStruct((a.shape[0] + b.shape[0], width), a.dtype),
+        out_shape=jax.ShapeDtypeStruct(((1 + len(others)) * count, width), first.dtype),
         compiler_params=pltpu.CompilerParams(vmem_limit_bytes=8 << 20),
-    )(a, b)
+    )(first, *others)
 
 
 def prepare_rows(block, sources, groups):
@@ -206,6 +208,27 @@
     )(*lead, *flat)
 
 
+def apply_each(rows, columns):
+    n, width = len(rows), columns[0][1].shape[1]
+    flat = [a for pair in columns for a in pair]
+
+    def body(*refs):
+        rest, outs = refs[n : n + len(flat)], refs[n + len(flat) :]
+        for row_ref, out_ref in zip(refs[:n], outs, strict=True):
+            out_ref[...] = sum(
+                fold(row_ref, slice(None), rest[k][...], rest[k + 1][...]) for k in range(0, len(rest), 2)
+            )
+
+    return pl.pallas_call(
+        body,
+        in_specs=[VMEM] * (n + len(flat)),
+        out_specs=[VMEM] * n,
+        out_shape=[jax.ShapeDtypeStruct((r.shape[0], width), jnp.float32) for r in rows],
+        cost_estimate=cost(sum(r.shape[0] for r in rows), sum(c[0].shape[0] for c in columns), width),
+        compiler_params=params(28),
+    )(*rows, *flat)
+
+
 COL_MOVES = ((("x", 1), ("x", 3)), (("x", 3), ("y", 1)), (("y", 1), ("x", 1)))
 ROW_MOVES = ((("z", 1), ("z", 3)), (("z", 3), ("y", 3)), (("y", 3), ("z", 1)))
 
@@ -224,14 +247,14 @@
 
     got_a = swap(own, move_a)
     rows_p = swap(pair, move_p)
-    pairs = join(own, rows_p)
-    rows_q = swap(pairs, move_q)
+    rows_q = swap(pair, move_q)
+    rows_qp = swap(pair, move_q, move_p)
     pack_a = join(own, got_a)
     pack_b = swap(pack_a, move_b)
+    quads = join(own, rows_p, rows_q, rows_qp)
+    rows_r = swap(quads, move_r)
+    other_a = partner(pack_a)
     pack_c = swap(pack_a, move_c)
-    other_a = partner(pack_a)
-    quads = join(pairs, rows_q)
-    rows_r = swap(quads, move_r)
 
     near = prepare_rows(block, [quads], [[(0, 2), (0, 3)], [(0, 1)], [(0, 0)]])
     row_n, row_p, row_own = near
@@ -241,10 +264,9 @@
     pack_d = swap(pack_b, move_c)
     far = prepare_rows(block, [rows_r], [[(0, 2), (0, 3)], [(0, 0), (0, 1)]])
     row_f1, row_f2 = far
-    f1 = apply_rows(row_f1, None, [aug_a], f32)
+    f1, f2 = apply_each(far, [aug_a])
     f1, *aug_b = accumulate([row_f1], [f1], [pack_b, other_b], [f32])
     f1, *aug_c = accumulate([row_f1], [f1], [pack_c, other_c], [f32])
-    f2 = apply_rows(row_f2, None, [aug_a], f32)
     other_d = partner(pack_d)
     f2 = apply_rows(row_f2, f2, [aug_b, aug_c], f32)
     f1, *aug_d = accumulate([row_f1], [f1], [pack_d, other_d], [bf16])
@@ -254,9 +276,9 @@
 
     columns = [aug_b, aug_c, aug_d]
     n = apply_rows(row_n, n, columns, f32)
-    beside = apply_rows(row_p, beside, columns, f32)
     from_q = swap((n[:block] + in_1[:block].astype(f32)).astype(bf16), move_q)
     from_qp = swap((n[block:] + in_1[block:].astype(f32)).astype(bf16), move_q, move_p)
+    beside = apply_rows(row_p, beside, columns, f32)
     from_p = swap((beside + in_2[block:].astype(f32)).astype(bf16), move_p)
     total = apply_rows(row_own, total, columns, f32)
     total = total + diag + in_2[:block].astype(f32)

time: 77.9 us -> 78.7 us (1.010); the launches traced: 77.8 us -> 77.7 us
  waiting for transfers between devices: 15.1 us -> 16.4 us
  starting transfers between devices: 31.6 us -> 30.6 us
    ppermute x4, starting transfers between devices: 12.4 us -> 6.71 us  [partner(): return lax.ppermute(value, AXES, [(i, i ^ 8) for i in range(128)])]
    ppermute x12 -> x13, starting transfers between devices: 19.1 us -> 23.9 us  [swap(): return lax.ppermute(value, AXES, pairs)]
    pallas_call x7 -> x5, Pallas kernels: 15.6 us -> 12.6 us  [apply_rows(): pl.pallas_call(body, in_specs=[VMEM] * (len(lead) + len(flat)), out_specs...]
    pallas_call x3, Pallas kernels: 0.1 us -> 2.85 us  [the longest x1 2.76 us: apply_each(): pl.pallas_call(body, in_specs=[VMEM] * (n + len(flat)), out_specs=[VMEM]...]
    ppermute x12 -> x13, waiting for transfers between devices: 15.1 us -> 16.4 us  [swap(): return lax.ppermute(value, AXES, pairs)]
  transfers between devices with their start and end apart: 16 -> 17, of which waited for: 6 -> 6; matrix products, arithmetic and copies ran while one was open for 0% -> 0% of each run, Pallas kernels for 32% -> 30%
where the time goes in v6:
time: 78.7 us; the launch traced here: 77.7 us
  starting transfers between devices  30.6 us (39%)
  Pallas kernels  28.4 us (36%)
  waiting for transfers between devices  16.4 us (21%)
  other arithmetic  1.11 us (1%)
  local copies, waits for them, and re-layouts  0.98 us (1%)
    ppermute x13, starting transfers between devices, swap(): return lax.ppermute(value, AXES, pairs)  23.9 us
    ppermute x13, waiting for transfers between devices, swap(): return lax.ppermute(value, AXES, pairs)  16.4 us
    pallas_call x5, Pallas kernels, apply_rows(): pl.pallas_call(body, in_specs=[VMEM] * (len(lead) + len(flat)), out_specs...  12.6 us
    pallas_call x4, Pallas kernels, accumulate(): pl.pallas_call(body, in_specs=[VMEM] * (n + m + p), out_specs=[VMEM] * (n...  9.78 us
    ppermute x4, starting transfers between devices, partner(): return lax.ppermute(value, AXES, [(i, i ^ 8) for i in range(128)])  6.71 us
    pallas_call x1, Pallas kernels, apply_each(): pl.pallas_call(body, in_specs=[VMEM] * (n + len(flat)), out_specs=[VMEM]...  2.76 us
    pallas_call x1, Pallas kernels, pack_own(): pl.pallas_call(body, in_specs=[pl.BlockSpec(memory_space=pltpu.HBM)] * 3,...  1.84 us
  transfers between devices with their start and end apart: 17, of which 6 were waited for; matrix products, arithmetic and copies ran while one was open for 0% of the time, Pallas kernels for 30%

profile of v6, /device:TPU:1, one launch (start us, length us, event | category | flops | bytes accessed | tf_op | source)
XLA Modules:
  0.0 77.7 jit_solution(69335201351792767)
XLA Ops:
  0.0 1.8 %pack_own.1 = (bf16[384,384]{1,0:T(8,128)(2,1)}, bf16[384,128]{1,0:T(8,128)(2,1)}) custom-call(f32[64,384]{1,0:T(8,128)} %bitcast.2, f32[1,64]{1,0:T(1,128)} %bitcast.3, bf16[384,256]{1,0:T(8,128)(2,1)} %probe_hbm.1), custom_call_target="tpu_custom_call" | custom-call | tf_op jit(solution)/shard_map/pack_own/pallas_call | solution.py:87
  1.8 3.4 %collective-permute-start.3 = (bf16[384,384]{1,0:T(8,128)(2,1)}, bf16[384,384]{1,0:T(8,128)(2,1)S(1)}, u32[]{:S(2)}, u32[]{:S(2)}) collective-permute-start(bf16[384,384]{1,0:T(8,128)(2,1)} %get-tuple-element.28.refs_0_), channel_id=1, source_target_pairs={{0,16},{8,56},{1,17},{9,57},{2,18},{10,58},{3,19},{11,59},{64,80},... | collective-permute-start | bytes 884744 | tf_op jit(solution)/shard_map/ppermute | solution.py:34
  5.2 4.3 %collective-permute-done.3.refs_1_ = bf16[384,384]{1,0:T(8,128)(2,1)S(1)} collective-permute-done((bf16[384,384]{1,0:T(8,128)(2,1)}, bf16[384,384]{1,0:T(8,128)(2,1)S(1)}, u32[]{:S(2)}, u32[]{:S(2)}) %collective-permute-start.3) | collective-permute-done | bytes 294944 | tf_op jit(solution)/shard_map/ppermute | solution.py:34
  9.5 0.0 copy-start
  9.5 1.0 %copy-done = bf16[384,384]{1,0:T(8,128)(2,1)S(1)} copy-done((bf16[384,384]{1,0:T(8,128)(2,1)S(1)}, bf16[384,384]{1,0:T(8,128)(2,1)}, u32[]{:S(2)}) %copy-start) | copy-done | bytes 294936
  10.5 0.0 copy-start.3
  10.5 0.1 shard_map.48.refs_3_
  10.6 1.6 %collective-permute-start.6 = (bf16[768,384]{1,0:T(8,128)(2,1)S(1)}, bf16[768,384]{1,0:T(8,128)(2,1)S(1)}, u32[]{:S(2)}, u32[]{:S(2)}) collective-permute-start(bf16[768,384]{1,0:T(8,128)(2,1)S(1)} %shard_map.48.refs_3_), channel_id=1, source_target_pairs={{0,48},{8,72},{1,49},{9,73},{2,50},{10,74},{3,51},{11,75},{64,112}... | collective-permute-start | bytes 1769480 | tf_op jit(solution)/shard_map/ppermute | solution.py:34
  12.1 0.3 collective-permute-start.8
  12.4 0.0 copy-done.3
  12.4 3.8 %collective-permute-start = (bf16[384,128]{1,0:T(8,128)(2,1)S(1)}, bf16[384,128]{1,0:T(8,128)(2,1)S(1)}, u32[]{:S(2)}, u32[]{:S(2)}) collective-permute-start(bf16[384,128]{1,0:T(8,128)(2,1)S(1)} %copy-done.3), channel_id=1, source_target_pairs={{0,1},{8,11},{1,0},{9,10},{2,3},{10,9},{3,2},{11,8},{64,65},{72,75... | collective-permute-start | bytes 294920 | tf_op jit(solution)/shard_map/ppermute | solution.py:34
  16.2 1.5 %collective-permute-start.4 = (bf16[768,384]{1,0:T(8,128)(2,1)S(1)}, bf16[768,384]{1,0:T(8,128)(2,1)S(1)}, u32[]{:S(2)}, u32[]{:S(2)}) collective-permute-start(bf16[768,384]{1,0:T(8,128)(2,1)S(1)} %shard_map.48.refs_3_), channel_id=1, source_target_pairs={{0,8},{1,9},{2,10},{3,11},{4,12},{5,13},{6,14},{7,15},{8,0},{9,1},... | collective-permute-start | bytes 1769480 | tf_op jit(solution)/shard_map/ppermute | solution.py:38
  17.7 1.9 %collective-permute-start.1 = (bf16[384,128]{1,0:T(8,128)(2,1)S(1)}, bf16[384,128]{1,0:T(8,128)(2,1)S(1)}, u32[]{:S(2)}, u32[]{:S(2)}) collective-permute-start(bf16[384,128]{1,0:T(8,128)(2,1)S(1)} %copy-done.3), channel_id=1, source_target_pairs={{0,3},{8,76},{1,2},{9,77},{2,1},{10,78},{3,0},{11,79},{64,67},{72,... | collective-permute-start | bytes 294920 | tf_op jit(solution)/shard_map/ppermute | solution.py:34
  19.6 0.0 collective-permute-done.refs_1_
  19.6 3.2 %collective-permute-start.2 = (bf16[384,128]{1,0:T(8,128)(2,1)S(1)}, bf16[384,128]{1,0:T(8,128)(2,1)S(1)}, u32[]{:S(2)}, u32[]{:S(2)}) collective-permute-start(bf16[384,128]{1,0:T(8,128)(2,1)S(1)} %copy-done.3), channel_id=1, source_target_pairs={{0,2},{8,79},{1,3},{9,78},{2,0},{10,77},{3,1},{11,76},{64,66},{72,... | collective-permute-start | bytes 294920 | tf_op jit(solution)/shard_map/ppermute | solution.py:34
  22.8 0.0 collective-permute-done.1.refs_2_
  22.8 4.5 %collective-permute-done.2.refs_3_ = bf16[384,128]{1,0:T(8,128)(2,1)S(1)} collective-permute-done((bf16[384,128]{1,0:T(8,128)(2,1)S(1)}, bf16[384,128]{1,0:T(8,128)(2,1)S(1)}, u32[]{:S(2)}, u32[]{:S(2)}) %collective-permute-start.2) | collective-permute-done | bytes 98336 | tf_op jit(solution)/shard_map/ppermute | solution.py:34
  27.3 0.1 collective-permute-start.5
  27.4 0.0 collective-permute-done.6.refs_2_
  27.4 0.1 collective-permute-start.10
  27.5 2.4 %collective-permute-start.7 = (bf16[768,384]{1,0:T(8,128)(2,1)S(1)}, bf16[768,384]{1,0:T(8,128)(2,1)S(1)}, u32[]{:S(2)}, u32[]{:S(2)}) collective-permute-start(bf16[768,384]{1,0:T(8,128)(2,1)S(1)} %collective-permute-done.6.refs_2_), channel_id=1, source_target_pairs={{0,8},{1,9},{2,10},{3,11},{4,12},{5,13},{6,14},{7,15},{8,0},{9,1},... | collective-permute-start | bytes 1769480 | tf_op jit(solution)/shard_map/ppermute | solution.py:38
  29.9 0.0 collective-permute-done.8.refs_2_
  29.9 0.0 collective-permute-start.9
  29.9 0.7 shard_map.47
  30.6 3.7 %collective-permute-done.5.refs_0_ = bf16[1536,128]{1,0:T(8,128)(2,1)S(1)} collective-permute-done((bf16[1536,128]{1,0:T(8,128)(2,1)S(1)}, bf16[1536,128]{1,0:T(8,128)(2,1)S(1)}, u32[]{:S(2)}, u32[]{:S(2)}) %collective-permute-start.5) | collective-permute-done | bytes 393248 | tf_op jit(solution)/shard_map/ppermute | solution.py:34
  34.3 0.7 shard_map.50
  35.0 0.0 collective-permute-done.4.refs_4_
  35.0 3.7 %shard_map.49 = (f32[768,256]{1,0:T(8,128)S(1)}, f32[384,256]{1,0:T(8,128)S(1)}, f32[384,256]{1,0:T(8,128)S(1)}, bf16[1536,256]{1,0:T(8,128)(2,1)S(1)}, bf16[1536,256]{1,0:T(8,128)(2,1)S(1)}) custom-call(bf16[768,256]{1,0:T(8,128)(2,1)S(1)} %get-tuple-element.31.refs_0_, bf16[384,256]{1,0:T(8,128)(2,1)S(1)} %get-tuple-element.32.refs_1_.refs_0_, ...), custom_call_target="tpu_custom_call" | custom-call | flops 2415919104 | bytes 1572864 | tf_op jit(solution)/shard_map/pallas_call | solution.py:177
  38.7 0.0 collective-permute-done.10.refs_2_
  38.7 2.8 %collective-permute-start.11 = (bf16[768,384]{1,0:T(8,128)(2,1)S(1)}, bf16[768,384]{1,0:T(8,128)(2,1)S(1)}, u32[]{:S(2)}, u32[]{:S(2)}) collective-permute-start(bf16[768,384]{1,0:T(8,128)(2,1)S(1)} %collective-permute-done.10.refs_2_), channel_id=1, source_target_pairs={{0,8},{1,9},{2,10},{3,11},{4,12},{5,13},{6,14},{7,15},{8,0},{9,1},... | collective-permute-start | bytes 1769480 | tf_op jit(solution)/shard_map/ppermute | solution.py:38
  41.5 2.8 %shard_map.51 = (f32[768,256]{1,0:T(8,128)S(1)}, f32[768,256]{1,0:T(8,128)S(1)}) custom-call(bf16[768,256]{1,0:T(8,128)(2,1)S(1)} %get-tuple-element.34.refs_0_, bf16[768,256]{1,0:T(8,128)(2,1)S(1)} %get-tuple-element.35.refs_1_.refs_0_, bf16[1536,256]{1,0:T(8,128)(2,1)S(1)} %get-tuple-element.36.refs_2_, bf16[1536,256]{1,0:T(8,128)(2,1)S(1)} %get-tuple-element.37.refs_3_), custom_call_target="tpu_custom_call" | custom-call | flops 2415919104 | bytes 1572864 | tf_op jit(solution)/shard_map/pallas_call | solution.py:222
  44.3 0.0 collective-permute-done.7.refs_3_
  44.3 2.0 %shard_map.52 = (f32[768,256]{1,0:T(8,128)S(1)}, bf16[1536,256]{1,0:T(8,128)(2,1)S(1)}, bf16[1536,256]{1,0:T(8,128)(2,1)S(1)}) custom-call(bf16[768,256]{1,0:T(8,128)(2,1)S(1)} %get-tuple-element.34.refs_0_, f32[768,256]{1,0:T(8,128)S(1)} %get-tuple-element.38.refs_1_, bf16[768,384]{1,0:T(8,128)(2,1)S(1)} %collective-permute-done.6.refs_2_, ...), custom_call_target="tpu_custom_call" | custom-call | flops 1207959552 | bytes 786432 | tf_op jit(solution)/shard_map/pallas_call | solution.py:177
  46.3 0.0 collective-permute-done.9.refs_3_
  46.3 2.0 %shard_map.53 = (f32[768,256]{1,0:T(8,128)S(1)}, bf16[1536,256]{1,0:T(8,128)(2,1)S(1)}, bf16[1536,256]{1,0:T(8,128)(2,1)S(1)}) custom-call(bf16[768,256]{1,0:T(8,128)(2,1)S(1)} %get-tuple-element.34.refs_0_, f32[768,256]{1,0:T(8,128)S(1)} %get-tuple-element.41.refs_1_, bf16[768,384]{1,0:T(8,128)(2,1)S(1)} %collective-permute-done.8.refs_2_, ...), custom_call_target="tpu_custom_call" | custom-call | flops 1207959552 | bytes 786432 | tf_op jit(solution)/shard_map/pallas_call | solution.py:177
  48.4 2.8 %shard_map.56.refs_1_ = f32[768,256]{1,0:T(8,128)S(1)} custom-call(bf16[768,256]{1,0:T(8,128)(2,1)S(1)} %get-tuple-element.35.refs_1_.refs_0_, f32[768,256]{1,0:T(8,128)S(1)} %get-tuple-element.47.refs_1_, bf16[1536,256]{1,0:T(8,128)(2,1)S(1)} %get-tuple-element.39.refs_2_, bf16[1536,256]{1,0:T(8,128)(2,1)S(1)} %get-tuple-element.40.refs_3_, ...), custom_call_target="tpu_custom_call" | custom-call | flops 2415919104 | bytes 786432 | tf_op jit(solution)/shard_map/pallas_call | solution.py:201
  51.1 0.0 collective-permute-done.11.refs_3_
  51.1 2.0 %shard_map.54 = (bf16[768,256]{1,0:T(8,128)(2,1)S(1)}, bf16[1536,256]{1,0:T(8,128)(2,1)S(1)}, bf16[1536,256]{1,0:T(8,128)(2,1)S(1)}) custom-call(bf16[768,256]{1,0:T(8,128)(2,1)S(1)} %get-tuple-element.34.refs_0_, f32[768,256]{1,0:T(8,128)S(1)} %get-tuple-element.44.refs_1_, bf16[768,384]{1,0:T(8,128)(2,1)S(1)} %collective-permute-done.10.refs_2_, ...), custom_call_target="tpu_custom_call" | custom-call | flops 1207959552 | bytes 786432 | tf_op jit(solution)/shard_map/pallas_call | solution.py:177
  53.2 1.5 %shard_map.57 = bf16[768,256]{1,0:T(8,128)(2,1)S(1)} custom-call(bf16[768,256]{1,0:T(8,128)(2,1)S(1)} %get-tuple-element.35.refs_1_.refs_0_, f32[768,256]{1,0:T(8,128)S(1)} %shard_map.56.refs_1_, bf16[1536,256]{1,0:T(8,128)(2,1)S(1)} %get-tuple-element.45.refs_6_.refs_2_, bf16[1536,256]{1,0:T(8,128)(2,1)S(1)} %get-tuple-element.46.refs_7_.refs_3_), custom_call_target="tpu_custom_call" | custom-call | flops 1207959552 | bytes 786432 | tf_op jit(solution)/shard_map/pallas_call | solution.py:201
  54.7 0.7 collective-permute-start.12
  55.5 1.0 %collective-permute-start.13 = (bf16[768,256]{1,0:T(8,128)(2,1)S(1)}, bf16[768,256]{1,0:T(8,128)(2,1)S(1)}, u32[]{:S(2)}, u32[]{:S(2)}) collective-permute-start(bf16[768,256]{1,0:T(8,128)(2,1)S(1)} %get-tuple-element.49), channel_id=1, source_target_pairs={{0,68},{8,9},{1,69},{9,8},{2,70},{10,11},{3,71},{11,10},{64,4},{72... | collective-permute-start | bytes 1179656 | tf_op jit(solution)/shard_map/ppermute | solution.py:34
  56.5 4.0 %shard_map.58 = f32[768,256]{1,0:T(8,128)S(1)} custom-call(bf16[768,256]{1,0:T(8,128)(2,1)S(1)} %get-tuple-element.31.refs_0_, f32[768,256]{1,0:T(8,128)S(1)} %get-tuple-element.48.refs_1_, bf16[1536,256]{1,0:T(8,128)(2,1)S(1)} %get-tuple-element.39.refs_2_, bf16[1536,256]{1,0:T(8,128)(2,1)S(1)} %get-tuple-element.40.refs_3_, ...), custom_call_target="tpu_custom_call" | custom-call | flops 3623878656 | bytes 786432 | tf_op jit(solution)/shard_map/pallas_call | solution.py:201
  60.5 2.1 %shard_map.59 = f32[384,256]{1,0:T(8,128)S(1)} custom-call(bf16[384,256]{1,0:T(8,128)(2,1)S(1)} %get-tuple-element.32.refs_1_.refs_0_, f32[384,256]{1,0:T(8,128)S(1)} %get-tuple-element.50.refs_1_, bf16[1536,256]{1,0:T(8,128)(2,1)S(1)} %get-tuple-element.39.refs_2_, bf16[1536,256]{1,0:T(8,128)(2,1)S(1)} %get-tuple-element.40.refs_3_, ...), custom_call_target="tpu_custom_call" | custom-call | flops 1811939328 | bytes 393216 | tf_op jit(solution)/shard_map/pallas_call | solution.py:201
  62.6 0.0 collective-permute-done.12
  62.7 0.0 copy-start.1
  62.7 2.7 %collective-permute-start.16 = (bf16[384,256]{1,0:T(8,128)(2,1)S(1)}, bf16[384,256]{1,0:T(8,128)(2,1)S(1)}, u32[]{:S(2)}, u32[]{:S(2)}) collective-permute-start(bf16[384,256]{1,0:T(8,128)(2,1)S(1)} %add_convert_fusion), channel_id=1, source_target_pairs={{0,1},{8,11},{1,0},{9,10},{2,3},{10,9},{3,2},{11,8},{64,65},{72,75... | collective-permute-start | bytes 589832 | tf_op jit(solution)/shard_map/ppermute | solution.py:34
  65.5 0.7 collective-permute-done.13
  66.2 0.1 fusion.1
  66.2 0.0 copy-start.2
  66.3 4.3 %collective-permute-start.15 = (bf16[384,256]{1,0:T(8,128)(2,1)S(1)}, bf16[384,256]{1,0:T(8,128)(2,1)S(1)}, u32[]{:S(2)}, u32[]{:S(2)}) collective-permute-start(bf16[384,256]{1,0:T(8,128)(2,1)S(1)} %get-tuple-element.52), channel_id=1, source_target_pairs={{0,2},{8,79},{1,3},{9,78},{2,0},{10,77},{3,1},{11,76},{64,66},{72,... | collective-permute-start | bytes 589832 | tf_op jit(solution)/shard_map/ppermute | solution.py:34
  70.5 0.9 %collective-permute-start.14 = (bf16[384,256]{1,0:T(8,128)(2,1)S(1)}, bf16[384,256]{1,0:T(8,128)(2,1)S(1)}, u32[]{:S(2)}, u32[]{:S(2)}) collective-permute-start(bf16[384,256]{1,0:T(8,128)(2,1)S(1)} %get-tuple-element.51), channel_id=1, source_target_pairs={{0,3},{8,76},{1,2},{9,77},{2,1},{10,78},{3,0},{11,79},{64,67},{72,... | collective-permute-start | bytes 589832 | tf_op jit(solution)/shard_map/ppermute | solution.py:34
  71.4 0.0 copy-done.1
  71.4 0.0 copy-done.2
  71.4 0.1 convert_multiply_fusion
  71.5 2.1 %shard_map.55 = f32[384,256]{1,0:T(8,128)S(1)} custom-call(bf16[384,256]{1,0:T(8,128)(2,1)S(1)} %get-tuple-element.30.refs_2_.refs_0_, f32[384,256]{1,0:T(8,128)S(1)} %get-tuple-element.33.refs_1_, bf16[1536,256]{1,0:T(8,128)(2,1)S(1)} %get-tuple-element.39.refs_2_, bf16[1536,256]{1,0:T(8,128)(2,1)S(1)} %get-tuple-element.40.refs_3_, ...), custom_call_target="tpu_custom_call" | custom-call | flops 1811939328 | bytes 393216 | tf_op jit(solution)/shard_map/pallas_call | solution.py:201
  73.7 0.0 collective-permute-done.16
  73.7 1.7 %collective-permute-done.15 = bf16[384,256]{1,0:T(8,128)(2,1)S(1)} collective-permute-done((bf16[384,256]{1,0:T(8,128)(2,1)S(1)}, bf16[384,256]{1,0:T(8,128)(2,1)S(1)}, u32[]{:S(2)}, u32[]{:S(2)}) %collective-permute-start.15) | collective-permute-done | bytes 196640 | tf_op jit(solution)/shard_map/ppermute | solution.py:34
  75.4 1.5 %collective-permute-done.14 = bf16[384,256]{1,0:T(8,128)(2,1)S(1)} collective-permute-done((bf16[384,256]{1,0:T(8,128)(2,1)S(1)}, bf16[384,256]{1,0:T(8,128)(2,1)S(1)}, u32[]{:S(2)}, u32[]{:S(2)}) %collective-permute-start.14) | collective-permute-done | bytes 196640 | tf_op jit(solution)/shard_map/ppermute | solution.py:34
  76.9 0.9 %convert_add_fusion = f32[384,256]{1,0:T(8,128)} fusion(bf16[384,256]{1,0:T(8,128)(2,1)S(1)} %collective-permute-done.16, bf16[384,256]{1,0:T(8,128)(2,1)S(1)} %collective-permute-done.15, bf16[384,256]{1,0:T(8,128)(2,1)S(1)} %collective-permute-done.14, f32[384,256]{1,0:T(8,128)S(1)} %shard_map.55, f32[384,256]{1,0:T(8,128)S(1)} %convert_multiply_fusion, ...), kind=kLoop, calls=%fused_computation.4 | loop fusion | flops 884736 | bytes 1966080 | tf_op jit(solution)/shard_map/add | solution.py:285
  (2 shorter events, 0.1 us)
Async XLA Ops:
  1.8 7.7 %collective-permute-start.3 = (bf16[384,384]{1,0:T(8,128)(2,1)}, bf16[384,384]{1,0:T(8,128)(2,1)S(1)}, u32[]{:S(2)}, u32[]{:S(2)}) collective-permute-start(bf16[384,384]{1,0:T(8,128)(2,1)} %get-tuple-element.28.refs_0_), channel_id=1, source_target_pairs={{0,16},{8,56},{1,17},{9,57},{2,18},{10,58},{3,19},{11,59},{64,80},... | collective-permute-start | bytes 884744 | tf_op jit(solution)/shard_map/ppermute | solution.py:34
  9.5 1.0 %copy-start = (bf16[384,384]{1,0:T(8,128)(2,1)S(1)}, bf16[384,384]{1,0:T(8,128)(2,1)}, u32[]{:S(2)}) copy-start(bf16[384,384]{1,0:T(8,128)(2,1)} %get-tuple-element.28.refs_0_) | copy-start | bytes 884740
  10.5 1.9 %copy-start.3 = (bf16[384,128]{1,0:T(8,128)(2,1)S(1)}, bf16[384,128]{1,0:T(8,128)(2,1)}, u32[]{:S(2)}) copy-start(bf16[384,128]{1,0:T(8,128)(2,1)} %get-tuple-element.29) | copy-start | bytes 294916
  10.6 16.8 %collective-permute-start.6 = (bf16[768,384]{1,0:T(8,128)(2,1)S(1)}, bf16[768,384]{1,0:T(8,128)(2,1)S(1)}, u32[]{:S(2)}, u32[]{:S(2)}) collective-permute-start(bf16[768,384]{1,0:T(8,128)(2,1)S(1)} %shard_map.48.refs_3_), channel_id=1, source_target_pairs={{0,48},{8,72},{1,49},{9,73},{2,50},{10,74},{3,51},{11,75},{64,112}... | collective-permute-start | bytes 1769480 | tf_op jit(solution)/shard_map/ppermute | solution.py:34
  12.1 17.7 %collective-permute-start.8 = (bf16[768,384]{1,0:T(8,128)(2,1)S(1)}, bf16[768,384]{1,0:T(8,128)(2,1)S(1)}, u32[]{:S(2)}, u32[]{:S(2)}) collective-permute-start(bf16[768,384]{1,0:T(8,128)(2,1)S(1)} %shard_map.48.refs_3_), channel_id=1, source_target_pairs={{0,64},{8,24},{1,65},{9,25},{2,66},{10,26},{3,67},{11,27},{64,0},{... | collective-permute-start | bytes 1769480 | tf_op jit(solution)/shard_map/ppermute | solution.py:34
  12.4 7.2 %collective-permute-start = (bf16[384,128]{1,0:T(8,128)(2,1)S(1)}, bf16[384,128]{1,0:T(8,128)(2,1)S(1)}, u32[]{:S(2)}, u32[]{:S(2)}) collective-permute-start(bf16[384,128]{1,0:T(8,128)(2,1)S(1)} %copy-done.3), channel_id=1, source_target_pairs={{0,1},{8,11},{1,0},{9,10},{2,3},{10,9},{3,2},{11,8},{64,65},{72,75... | collective-permute-start | bytes 294920 | tf_op jit(solution)/shard_map/ppermute | solution.py:34
  16.2 18.8 %collective-permute-start.4 = (bf16[768,384]{1,0:T(8,128)(2,1)S(1)}, bf16[768,384]{1,0:T(8,128)(2,1)S(1)}, u32[]{:S(2)}, u32[]{:S(2)}) collective-permute-start(bf16[768,384]{1,0:T(8,128)(2,1)S(1)} %shard_map.48.refs_3_), channel_id=1, source_target_pairs={{0,8},{1,9},{2,10},{3,11},{4,12},{5,13},{6,14},{7,15},{8,0},{9,1},... | collective-permute-start | bytes 1769480 | tf_op jit(solution)/shard_map/ppermute | solution.py:38
  17.7 5.1 %collective-permute-start.1 = (bf16[384,128]{1,0:T(8,128)(2,1)S(1)}, bf16[384,128]{1,0:T(8,128)(2,1)S(1)}, u32[]{:S(2)}, u32[]{:S(2)}) collective-permute-start(bf16[384,128]{1,0:T(8,128)(2,1)S(1)} %copy-done.3), channel_id=1, source_target_pairs={{0,3},{8,76},{1,2},{9,77},{2,1},{10,78},{3,0},{11,79},{64,67},{72,... | collective-permute-start | bytes 294920 | tf_op jit(solution)/shard_map/ppermute | solution.py:34
  19.6 7.6 %collective-permute-start.2 = (bf16[384,128]{1,0:T(8,128)(2,1)S(1)}, bf16[384,128]{1,0:T(8,128)(2,1)S(1)}, u32[]{:S(2)}, u32[]{:S(2)}) collective-permute-start(bf16[384,128]{1,0:T(8,128)(2,1)S(1)} %copy-done.3), channel_id=1, source_target_pairs={{0,2},{8,79},{1,3},{9,78},{2,0},{10,77},{3,1},{11,76},{64,66},{72,... | collective-permute-start | bytes 294920 | tf_op jit(solution)/shard_map/ppermute | solution.py:34
  27.3 7.0 %collective-permute-start.5 = (bf16[1536,128]{1,0:T(8,128)(2,1)S(1)}, bf16[1536,128]{1,0:T(8,128)(2,1)S(1)}, u32[]{:S(2)}, u32[]{:S(2)}) collective-permute-start(bf16[1536,128]{1,0:T(8,128)(2,1)S(1)} %shard_map.46.refs_0_), channel_id=1, source_target_pairs={{0,68},{8,9},{1,69},{9,8},{2,70},{10,11},{3,71},{11,10},{64,4},{72... | collective-permute-start | bytes 1179656 | tf_op jit(solution)/shard_map/ppermute | solution.py:34
  27.4 11.3 %collective-permute-start.10 = (bf16[768,384]{1,0:T(8,128)(2,1)S(1)}, bf16[768,384]{1,0:T(8,128)(2,1)S(1)}, u32[]{:S(2)}, u32[]{:S(2)}) collective-permute-start(bf16[768,384]{1,0:T(8,128)(2,1)S(1)} %collective-permute-done.6.refs_2_), channel_id=1, source_target_pairs={{0,64},{8,24},{1,65},{9,25},{2,66},{10,26},{3,67},{11,27},{64,0},{... | collective-permute-start | bytes 1769480 | tf_op jit(solution)/shard_map/ppermute | solution.py:34
  27.5 16.8 %collective-permute-start.7 = (bf16[768,384]{1,0:T(8,128)(2,1)S(1)}, bf16[768,384]{1,0:T(8,128)(2,1)S(1)}, u32[]{:S(2)}, u32[]{:S(2)}) collective-permute-start(bf16[768,384]{1,0:T(8,128)(2,1)S(1)} %collective-permute-done.6.refs_2_), channel_id=1, source_target_pairs={{0,8},{1,9},{2,10},{3,11},{4,12},{5,13},{6,14},{7,15},{8,0},{9,1},... | collective-permute-start | bytes 1769480 | tf_op jit(solution)/shard_map/ppermute | solution.py:38
  29.9 16.4 %collective-permute-start.9 = (bf16[768,384]{1,0:T(8,128)(2,1)S(1)}, bf16[768,384]{1,0:T(8,128)(2,1)S(1)}, u32[]{:S(2)}, u32[]{:S(2)}) collective-permute-start(bf16[768,384]{1,0:T(8,128)(2,1)S(1)} %collective-permute-done.8.refs_2_), channel_id=1, source_target_pairs={{0,8},{1,9},{2,10},{3,11},{4,12},{5,13},{6,14},{7,15},{8,0},{9,1},... | collective-permute-start | bytes 1769480 | tf_op jit(solution)/shard_map/ppermute | solution.py:38
  38.7 12.4 %collective-permute-start.11 = (bf16[768,384]{1,0:T(8,128)(2,1)S(1)}, bf16[768,384]{1,0:T(8,128)(2,1)S(1)}, u32[]{:S(2)}, u32[]{:S(2)}) collective-permute-start(bf16[768,384]{1,0:T(8,128)(2,1)S(1)} %collective-permute-done.10.refs_2_), channel_id=1, source_target_pairs={{0,8},{1,9},{2,10},{3,11},{4,12},{5,13},{6,14},{7,15},{8,0},{9,1},... | collective-permute-start | bytes 1769480 | tf_op jit(solution)/shard_map/ppermute | solution.py:38
  54.7 7.9 %collective-permute-start.12 = (bf16[768,256]{1,0:T(8,128)(2,1)S(1)}, bf16[768,256]{1,0:T(8,128)(2,1)S(1)}, u32[]{:S(2)}, u32[]{:S(2)}) collective-permute-start(bf16[768,256]{1,0:T(8,128)(2,1)S(1)} %shard_map.57), channel_id=1, source_target_pairs={{0,68},{8,9},{1,69},{9,8},{2,70},{10,11},{3,71},{11,10},{64,4},{72... | collective-permute-start | bytes 1179656 | tf_op jit(solution)/shard_map/ppermute | solution.py:34
  55.5 10.7 %collective-permute-start.13 = (bf16[768,256]{1,0:T(8,128)(2,1)S(1)}, bf16[768,256]{1,0:T(8,128)(2,1)S(1)}, u32[]{:S(2)}, u32[]{:S(2)}) collective-permute-start(bf16[768,256]{1,0:T(8,128)(2,1)S(1)} %get-tuple-element.49), channel_id=1, source_target_pairs={{0,68},{8,9},{1,69},{9,8},{2,70},{10,11},{3,71},{11,10},{64,4},{72... | collective-permute-start | bytes 1179656 | tf_op jit(solution)/shard_map/ppermute | solution.py:34
  62.7 8.7 %copy-start.1 = (bf16[384,256]{1,0:T(8,128)(2,1)S(1)}, bf16[384,256]{1,0:T(8,128)(2,1)}, u32[]{:S(2)}) copy-start(bf16[384,256]{1,0:T(8,128)(2,1)} %probe_hbm.1) | copy-start | bytes 589828
  62.7 11.0 %collective-permute-start.16 = (bf16[384,256]{1,0:T(8,128)(2,1)S(1)}, bf16[384,256]{1,0:T(8,128)(2,1)S(1)}, u32[]{:S(2)}, u32[]{:S(2)}) collective-permute-start(bf16[384,256]{1,0:T(8,128)(2,1)S(1)} %add_convert_fusion), channel_id=1, source_target_pairs={{0,1},{8,11},{1,0},{9,10},{2,3},{10,9},{3,2},{11,8},{64,65},{72,75... | collective-permute-start | bytes 589832 | tf_op jit(solution)/shard_map/ppermute | solution.py:34
  66.2 5.2 %copy-start.2 = (f32[384]{0:T(512)S(1)}, f32[384]{0:T(512)}, u32[]{:S(2)}) copy-start(f32[384]{0:T(512)} %param.6) | copy-start | bytes 4612
  66.3 9.1 %collective-permute-start.15 = (bf16[384,256]{1,0:T(8,128)(2,1)S(1)}, bf16[384,256]{1,0:T(8,128)(2,1)S(1)}, u32[]{:S(2)}, u32[]{:S(2)}) collective-permute-start(bf16[384,256]{1,0:T(8,128)(2,1)S(1)} %get-tuple-element.52), channel_id=1, source_target_pairs={{0,2},{8,79},{1,3},{9,78},{2,0},{10,77},{3,1},{11,76},{64,66},{72,... | collective-permute-start | bytes 589832 | tf_op jit(solution)/shard_map/ppermute | solution.py:34
  70.5 6.3 %collective-permute-start.14 = (bf16[384,256]{1,0:T(8,128)(2,1)S(1)}, bf16[384,256]{1,0:T(8,128)(2,1)S(1)}, u32[]{:S(2)}, u32[]{:S(2)}) collective-permute-start(bf16[384,256]{1,0:T(8,128)(2,1)S(1)} %get-tuple-element.51), channel_id=1, source_target_pairs={{0,3},{8,76},{1,2},{9,77},{2,1},{10,78},{3,0},{11,79},{64,67},{72,... | collective-permute-start | bytes 589832 | tf_op jit(solution)/shard_map/ppermute | solution.py:34

commit v7 on v6

--- a/solution.py
+++ b/solution.py
@@ -12,6 +12,7 @@
 NT = (((1,), (1,)), ((), ()))
 LANES = 128
 HALF = 64
+BLOCK = 384
 AXES = ("row", "col")
 VMEM = pl.BlockSpec(memory_space=pltpu.VMEM)
 
@@ -120,24 +121,6 @@
     )(first, *others)
 
 
-def prepare_rows(block, sources, groups):
-    def body(*refs):
-        ins, outs = refs[: len(sources)], refs[len(sources) :]
-        for group, out in zip(groups, outs, strict=True):
-            for i, (source, k) in enumerate(group):
-                a, b = augment(ins[source][k * block : (k + 1) * block, :], False)
-                out[i * block : (i + 1) * block, :LANES] = a
-                out[i * block : (i + 1) * block, LANES:] = b
-
-    return pl.pallas_call(
-        body,
-        in_specs=[VMEM] * len(sources),
-        out_specs=[VMEM] * len(groups),
-        out_shape=[jax.ShapeDtypeStruct((len(g) * block, 2 * LANES), jnp.bfloat16) for g in groups],
-        compiler_params=pltpu.CompilerParams(vmem_limit_bytes=12 << 20),
-    )(*sources)
-
-
 def params(mib):
     return pltpu.CompilerParams(vmem_limit_bytes=mib << 20)
 
@@ -153,80 +136,99 @@
     return jnp.dot(jnp.exp2(gram).astype(jnp.bfloat16), probe, preferred_element_type=jnp.float32)
 
 
-def accumulate(rows, olds, packs, out_types):
-    n, m, p = len(rows), len(olds), len(packs)
+def fill_rows(pair_ref, left):
+    for k in range(0, pair_ref.shape[0], BLOCK):
+        a, b = augment(pair_ref[k : k + BLOCK, :], False)
+        left[k : k + BLOCK, :LANES] = a
+        left[k : k + BLOCK, LANES:] = b
+
+
+def fill_columns(pack_refs, right, probes):
+    start = 0
+    for src in pack_refs:
+        for k in range(0, src.shape[0], BLOCK):
+            a, b = augment(src[k : k + BLOCK, :LANES], True)
+            right[start : start + BLOCK, :LANES] = a
+            right[start : start + BLOCK, LANES:] = b
+            probes[start : start + BLOCK, :] = src[k : k + BLOCK, LANES:]
+            start += BLOCK
+
+
+def columns_shape(packs):
+    cols = sum(q.shape[0] for q in packs)
     width = packs[0].shape[1] - LANES
-    cols = sum(q.shape[0] for q in packs)
-    block = 384
-
-    def body(*refs):
-        row_refs, old_refs, pack_refs = refs[:n], refs[n : n + m], refs[n + m : n + m + p]
-        out_refs, (right, probes) = refs[n + m + p : -2], refs[-2:]
-        start = 0
-        for src in pack_refs:
-            for k in range(0, src.shape[0], block):
-                a, b = augment(src[k : k + block, :LANES], True)
-                right[start : start + block, :LANES] = a
-                right[start : start + block, LANES:] = b
-                probes[start : start + block, :] = src[k : k + block, LANES:]
-                start += block
-        for k in range(n):
-            part = fold(row_refs[k], slice(None), right[...], probes[...])
-            out_refs[k][...] = (old_refs[k][...] + part if m else part).astype(out_refs[k].dtype)
-
-    return pl.pallas_call(
-        body,
-        in_specs=[VMEM] * (n + m + p),
-        out_specs=[VMEM] * (n + 2),
-        out_shape=[jax.ShapeDtypeStruct((r.shape[0], width), t) for r, t in zip(rows, out_types, strict=True)]
-        + [jax.ShapeDtypeStruct((cols, 2 * LANES), jnp.bfloat16), jax.ShapeDtypeStruct((cols, width), jnp.bfloat16)],
-        cost_estimate=cost(sum(r.shape[0] for r in rows), cols, width),
+    return [jax.ShapeDtypeStruct((cols, 2 * LANES), jnp.bfloat16), jax.ShapeDtypeStruct((cols, width), jnp.bfloat16)]
+
+
+def first_round(pairs, cuts, packs, columns):
+    count = pairs.shape[0]
+    shape = columns_shape(packs) if packs else [columns[0], columns[1]]
+    width, cols = shape[1].shape[1], shape[1].shape[0]
+    sides = packs or list(columns)
+
+    def body(*refs):
+        pair_ref, side_refs, outs = refs[0], refs[1 : 1 + len(sides)], refs[1 + len(sides) :]
+        left, sums = outs[0], outs[1 : len(cuts) + 1]
+        right, probes = outs[-2:] if packs else side_refs
+        fill_rows(pair_ref, left)
+        if packs:
+            fill_columns(side_refs, right, probes)
+        part = fold(left, slice(None), right[...], probes[...])
+        for at, ref in zip(cuts, sums, strict=True):
+            ref[...] = part[at : at + ref.shape[0], :]
+
+    ends = cuts[1:] + [count]
+    return pl.pallas_call(
+        body,
+        in_specs=[VMEM] * (1 + len(sides)),
+        out_specs=[VMEM] * (1 + len(cuts) + (2 if packs else 0)),
+        out_shape=[jax.ShapeDtypeStruct((count, 2 * LANES), jnp.bfloat16)]
+        + [jax.ShapeDtypeStruct((end - at, width), jnp.float32) for at, end in zip(cuts, ends, strict=True)]
+        + (shape if packs else []),
+        cost_estimate=cost(count, cols, width),
+        compiler_params=params(36),
+    )(pairs, *sides)
+
+
+def accumulate(rows, at, old, packs, out_type):
+    count, width = old.shape
+    shape = columns_shape(packs)
+
+    def body(*refs):
+        row_ref, old_ref, pack_refs, (out_ref, right, probes) = refs[0], refs[1], refs[2:-3], refs[-3:]
+        fill_columns(pack_refs, right, probes)
+        part = fold(row_ref, pl.ds(at, count), right[...], probes[...])
+        out_ref[...] = (old_ref[...] + part).astype(out_type)
+
+    return pl.pallas_call(
+        body,
+        in_specs=[VMEM] * (2 + len(packs)),
+        out_specs=[VMEM] * 3,
+        out_shape=[jax.ShapeDtypeStruct((count, width), out_type)] + shape,
+        cost_estimate=cost(count, shape[0].shape[0], width),
         compiler_params=params(28),
-    )(*rows, *olds, *packs)
-
-
-def apply_rows(rows, old, columns, out_type):
-    count, width = rows.shape[0], columns[0][1].shape[1]
+    )(rows, old, *packs)
+
+
+def apply_rows(rows, at, old, columns, out_type):
+    count, width = old.shape
     flat = [a for pair in columns for a in pair]
-    lead = [rows] if old is None else [rows, old]
-
-    def body(*refs):
-        row_ref, out_ref, rest = refs[0], refs[-1], refs[len(lead) : -1]
-        part = None if old is None else refs[1][...]
+
+    def body(*refs):
+        row_ref, old_ref, rest, out_ref = refs[0], refs[1], refs[2:-1], refs[-1]
+        part = old_ref[...]
         for k in range(0, len(rest), 2):
-            more = fold(row_ref, slice(None), rest[k][...], rest[k + 1][...])
-            part = more if part is None else part + more
+            part = part + fold(row_ref, pl.ds(at, count), rest[k][...], rest[k + 1][...])
         out_ref[...] = part.astype(out_type)
 
     return pl.pallas_call(
         body,
-        in_specs=[VMEM] * (len(lead) + len(flat)),
+        in_specs=[VMEM] * (2 + len(flat)),
         out_specs=VMEM,
         out_shape=jax.ShapeDtypeStruct((count, width), out_type),
         cost_estimate=cost(count, sum(c[0].shape[0] for c in columns), width),
         compiler_params=params(28),
-    )(*lead, *flat)
-
-
-def apply_each(rows, columns):
-    n, width = len(rows), columns[0][1].shape[1]
-    flat = [a for pair in columns for a in pair]
-
-    def body(*refs):
-        rest, outs = refs[n : n + len(flat)], refs[n + len(flat) :]
-        for row_ref, out_ref in zip(refs[:n], outs, strict=True):
-            out_ref[...] = sum(
-                fold(row_ref, slice(None), rest[k][...], rest[k + 1][...]) for k in range(0, len(rest), 2)
-            )
-
-    return pl.pallas_call(
-        body,
-        in_specs=[VMEM] * (n + len(flat)),
-        out_specs=[VMEM] * n,
-        out_shape=[jax.ShapeDtypeStruct((r.shape[0], width), jnp.float32) for r in rows],
-        cost_estimate=cost(sum(r.shape[0] for r in rows), sum(c[0].shape[0] for c in columns), width),
-        compiler_params=params(28),
-    )(*rows, *flat)
+    )(rows, old, *flat)
 
 
 COL_MOVES = ((("x", 1), ("x", 3)), (("x", 3), ("y", 1)), (("y", 1), ("x", 1)))
@@ -256,31 +258,27 @@
     other_a = partner(pack_a)
     pack_c = swap(pack_a, move_c)
 
-    near = prepare_rows(block, [quads], [[(0, 2), (0, 3)], [(0, 1)], [(0, 0)]])
-    row_n, row_p, row_own = near
-    n, beside, total, *aug_a = accumulate(near, [], [pack_a, other_a], [f32, f32, f32])
+    near, total, beside, n, *aug_a = first_round(quads, [0, block, 2 * block], [pack_a, other_a], None)
 
     other_b, other_c = partner(pack_b), partner(pack_c)
     pack_d = swap(pack_b, move_c)
-    far = prepare_rows(block, [rows_r], [[(0, 2), (0, 3)], [(0, 0), (0, 1)]])
-    row_f1, row_f2 = far
-    f1, f2 = apply_each(far, [aug_a])
-    f1, *aug_b = accumulate([row_f1], [f1], [pack_b, other_b], [f32])
-    f1, *aug_c = accumulate([row_f1], [f1], [pack_c, other_c], [f32])
+    far, f2, f1 = first_round(rows_r, [0, 2 * block], [], aug_a)
+    f1, *aug_b = accumulate(far, 2 * block, f1, [pack_b, other_b], f32)
+    f1, *aug_c = accumulate(far, 2 * block, f1, [pack_c, other_c], f32)
     other_d = partner(pack_d)
-    f2 = apply_rows(row_f2, f2, [aug_b, aug_c], f32)
-    f1, *aug_d = accumulate([row_f1], [f1], [pack_d, other_d], [bf16])
+    f2 = apply_rows(far, 0, f2, [aug_b, aug_c], f32)
+    f1, *aug_d = accumulate(far, 2 * block, f1, [pack_d, other_d], bf16)
     in_1 = swap(f1, move_r)
-    f2 = apply_rows(row_f2, f2, [aug_d], bf16)
+    f2 = apply_rows(far, 0, f2, [aug_d], bf16)
     in_2 = swap(f2, move_r)
 
     columns = [aug_b, aug_c, aug_d]
-    n = apply_rows(row_n, n, columns, f32)
+    n = apply_rows(near, 2 * block, n, columns, f32)
     from_q = swap((n[:block] + in_1[:block].astype(f32)).astype(bf16), move_q)
     from_qp = swap((n[block:] + in_1[block:].astype(f32)).astype(bf16), move_q, move_p)
-    beside = apply_rows(row_p, beside, columns, f32)
+    beside = apply_rows(near, block, beside, columns, f32)
     from_p = swap((beside + in_2[block:].astype(f32)).astype(bf16), move_p)
-    total = apply_rows(row_own, total, columns, f32)
+    total = apply_rows(near, 0, total, columns, f32)
     total = total + diag + in_2[:block].astype(f32)
     return total + from_q.astype(f32) + from_qp.astype(f32) + from_p.astype(f32)
 

time: 78.7 us -> 80.8 us (1.027)
  the two profiles are of different devices: /device:TPU:1 before, /device:TPU:6 now
where the time goes in v7:
time: 80.8 us; the launch traced here: 80.7 us
  waiting for transfers between devices  30.5 us (38%)
  Pallas kernels  29.3 us (36%)
  starting transfers between devices  18.6 us (23%)
  other arithmetic  1.11 us (1%)
  local copies, waits for them, and re-layouts  0.98 us (1%)
    ppermute x13, waiting for transfers between devices, swap(): return lax.ppermute(value, AXES, pairs)  30.5 us
    ppermute x13, starting transfers between devices, swap(): return lax.ppermute(value, AXES, pairs)  17.8 us
    pallas_call x5, Pallas kernels, apply_rows(): pl.pallas_call(body, in_specs=[VMEM] * (2 + len(flat)), out_specs=VMEM, o...  12.8 us
    pallas_call x2, Pallas kernels, first_round(): pl.pallas_call(body, in_specs=[VMEM] * (1 + len(sides)), out_specs=[VMEM]...  8.44 us
    pallas_call x3, Pallas kernels, accumulate(): pl.pallas_call(body, in_specs=[VMEM] * (2 + len(packs)), out_specs=[VMEM]...  6.09 us
    pallas_call x1, Pallas kernels, pack_own(): pl.pallas_call(body, in_specs=[pl.BlockSpec(memory_space=pltpu.HBM)] * 3,...  1.84 us
  transfers between devices with their start and end apart: 17, of which 8 were waited for; matrix products, arithmetic and copies ran while one was open for 0% of the time, Pallas kernels for 29%

profile of v7, /device:TPU:6, one launch (start us, length us, event | category | flops | bytes accessed | tf_op | source)
XLA Modules:
  0.0 80.7 jit_solution(13589438383811071202)
XLA Ops:
  0.0 1.8 %pack_own.1 = (bf16[384,384]{1,0:T(8,128)(2,1)}, bf16[384,128]{1,0:T(8,128)(2,1)}) custom-call(f32[64,384]{1,0:T(8,128)} %bitcast.2, f32[1,64]{1,0:T(1,128)} %bitcast.3, bf16[384,256]{1,0:T(8,128)(2,1)} %probe_hbm.1), custom_call_target="tpu_custom_call" | custom-call | tf_op jit(solution)/shard_map/pack_own/pallas_call | solution.py:88
  1.8 0.9 %collective-permute-start.3 = (bf16[384,384]{1,0:T(8,128)(2,1)}, bf16[384,384]{1,0:T(8,128)(2,1)S(1)}, u32[]{:S(2)}, u32[]{:S(2)}) collective-permute-start(bf16[384,384]{1,0:T(8,128)(2,1)} %get-tuple-element.25.refs_0_), channel_id=1, source_target_pairs={{0,16},{8,56},{1,17},{9,57},{2,18},{10,58},{3,19},{11,59},{64,80},... | collective-permute-start | bytes 884744 | tf_op jit(solution)/shard_map/ppermute | solution.py:35
  2.8 6.1 %collective-permute-done.3.refs_1_ = bf16[384,384]{1,0:T(8,128)(2,1)S(1)} collective-permute-done((bf16[384,384]{1,0:T(8,128)(2,1)}, bf16[384,384]{1,0:T(8,128)(2,1)S(1)}, u32[]{:S(2)}, u32[]{:S(2)}) %collective-permute-start.3) | collective-permute-done | bytes 294944 | tf_op jit(solution)/shard_map/ppermute | solution.py:35
  8.9 0.0 copy-start
  8.9 1.0 %copy-done = bf16[384,384]{1,0:T(8,128)(2,1)S(1)} copy-done((bf16[384,384]{1,0:T(8,128)(2,1)S(1)}, bf16[384,384]{1,0:T(8,128)(2,1)}, u32[]{:S(2)}) %copy-start) | copy-done | bytes 294936
  9.8 0.0 copy-start.3
  9.8 0.1 shard_map.47.refs_1_
  9.9 0.4 collective-permute-start.6
  10.3 1.7 %collective-permute-start.8 = (bf16[768,384]{1,0:T(8,128)(2,1)S(1)}, bf16[768,384]{1,0:T(8,128)(2,1)S(1)}, u32[]{:S(2)}, u32[]{:S(2)}) collective-permute-start(bf16[768,384]{1,0:T(8,128)(2,1)S(1)} %shard_map.47.refs_1_), channel_id=1, source_target_pairs={{0,64},{8,24},{1,65},{9,25},{2,66},{10,26},{3,67},{11,27},{64,0},{... | collective-permute-start | bytes 1769480 | tf_op jit(solution)/shard_map/ppermute | solution.py:35
  12.0 0.0 collective-permute-start.4
  12.0 0.0 copy-done.3
  12.0 1.9 %collective-permute-start = (bf16[384,128]{1,0:T(8,128)(2,1)S(1)}, bf16[384,128]{1,0:T(8,128)(2,1)S(1)}, u32[]{:S(2)}, u32[]{:S(2)}) collective-permute-start(bf16[384,128]{1,0:T(8,128)(2,1)S(1)} %copy-done.3), channel_id=1, source_target_pairs={{0,1},{8,11},{1,0},{9,10},{2,3},{10,9},{3,2},{11,8},{64,65},{72,75... | collective-permute-start | bytes 294920 | tf_op jit(solution)/shard_map/ppermute | solution.py:35
  13.9 7.1 %collective-permute-done.6.refs_2_ = bf16[768,384]{1,0:T(8,128)(2,1)S(1)} collective-permute-done((bf16[768,384]{1,0:T(8,128)(2,1)S(1)}, bf16[768,384]{1,0:T(8,128)(2,1)S(1)}, u32[]{:S(2)}, u32[]{:S(2)}) %collective-permute-start.6) | collective-permute-done | bytes 589856 | tf_op jit(solution)/shard_map/ppermute | solution.py:35
  21.1 1.6 %collective-permute-start.10 = (bf16[768,384]{1,0:T(8,128)(2,1)S(1)}, bf16[768,384]{1,0:T(8,128)(2,1)S(1)}, u32[]{:S(2)}, u32[]{:S(2)}) collective-permute-start(bf16[768,384]{1,0:T(8,128)(2,1)S(1)} %collective-permute-done.6.refs_2_), channel_id=1, source_target_pairs={{0,64},{8,24},{1,65},{9,25},{2,66},{10,26},{3,67},{11,27},{64,0},{... | collective-permute-start | bytes 1769480 | tf_op jit(solution)/shard_map/ppermute | solution.py:35
  22.6 4.0 %collective-permute-start.1 = (bf16[384,128]{1,0:T(8,128)(2,1)S(1)}, bf16[384,128]{1,0:T(8,128)(2,1)S(1)}, u32[]{:S(2)}, u32[]{:S(2)}) collective-permute-start(bf16[384,128]{1,0:T(8,128)(2,1)S(1)} %copy-done.3), channel_id=1, source_target_pairs={{0,3},{8,76},{1,2},{9,77},{2,1},{10,78},{3,0},{11,79},{64,67},{72,... | collective-permute-start | bytes 294920 | tf_op jit(solution)/shard_map/ppermute | solution.py:35
  26.7 0.0 collective-permute-done.refs_1_
  26.7 0.0 collective-permute-start.2
  26.7 3.2 %collective-permute-done.1.refs_2_ = bf16[384,128]{1,0:T(8,128)(2,1)S(1)} collective-permute-done((bf16[384,128]{1,0:T(8,128)(2,1)S(1)}, bf16[384,128]{1,0:T(8,128)(2,1)S(1)}, u32[]{:S(2)}, u32[]{:S(2)}) %collective-permute-start.1) | collective-permute-done | bytes 98336 | tf_op jit(solution)/shard_map/ppermute | solution.py:35
  29.9 3.4 %collective-permute-done.2.refs_3_ = bf16[384,128]{1,0:T(8,128)(2,1)S(1)} collective-permute-done((bf16[384,128]{1,0:T(8,128)(2,1)S(1)}, bf16[384,128]{1,0:T(8,128)(2,1)S(1)}, u32[]{:S(2)}, u32[]{:S(2)}) %collective-permute-start.2) | collective-permute-done | bytes 98336 | tf_op jit(solution)/shard_map/ppermute | solution.py:35
  33.3 1.8 %collective-permute-start.5 = (bf16[1536,128]{1,0:T(8,128)(2,1)S(1)}, bf16[1536,128]{1,0:T(8,128)(2,1)S(1)}, u32[]{:S(2)}, u32[]{:S(2)}) collective-permute-start(bf16[1536,128]{1,0:T(8,128)(2,1)S(1)} %shard_map.46.refs_0_), channel_id=1, source_target_pairs={{0,68},{8,9},{1,69},{9,8},{2,70},{10,11},{3,71},{11,10},{64,4},{72... | collective-permute-start | bytes 1179656 | tf_op jit(solution)/shard_map/ppermute | solution.py:35
  35.1 0.0 collective-permute-start.7
  35.1 0.0 collective-permute-done.8.refs_2_
  35.1 0.5 collective-permute-start.9
  35.6 0.0 collective-permute-done.4.refs_2_
  35.6 4.5 %shard_map.48 = (bf16[1536,256]{1,0:T(8,128)(2,1)S(1)}, f32[384,256]{1,0:T(8,128)S(1)}, f32[384,256]{1,0:T(8,128)S(1)}, f32[768,256]{1,0:T(8,128)S(1)}, bf16[153...) custom-call(bf16[1536,128]{1,0:T(8,128)(2,1)S(1)} %shard_map.46.refs_0_, bf16[768,384]{1,0:T(8,128)(2,1)S(1)} %shard_map.47.refs_1_, ...), custom_call_target="tpu_custom_call" | custom-call | flops 2415919104 | bytes 1572864 | tf_op jit(solution)/shard_map/pallas_call | solution.py:181
  40.1 0.0 collective-permute-done.10.refs_2_
  40.1 0.3 collective-permute-start.11
  40.4 2.0 %collective-permute-done.5.refs_0_ = bf16[1536,128]{1,0:T(8,128)(2,1)S(1)} collective-permute-done((bf16[1536,128]{1,0:T(8,128)(2,1)S(1)}, bf16[1536,128]{1,0:T(8,128)(2,1)S(1)}, u32[]{:S(2)}, u32[]{:S(2)}) %collective-permute-start.5) | collective-permute-done | bytes 393248 | tf_op jit(solution)/shard_map/ppermute | solution.py:35
  42.4 4.0 %shard_map.49 = (bf16[1536,256]{1,0:T(8,128)(2,1)S(1)}, f32[768,256]{1,0:T(8,128)S(1)}, f32[768,256]{1,0:T(8,128)S(1)}) custom-call(bf16[1536,128]{1,0:T(8,128)(2,1)S(1)} %collective-permute-done.5.refs_0_, bf16[1536,256]{1,0:T(8,128)(2,1)S(1)} %get-tuple-element.29.refs_1_, bf16[1536,256]{1,0:T(8,128)(2,1)S(1)} %get-tuple-element.30.refs_2_), custom_call_target="tpu_custom_call" | custom-call | flops 2415919104 | bytes 1572864 | tf_op jit(solution)/shard_map/pallas_call | solution.py:181
  46.4 0.0 collective-permute-done.7.refs_3_
  46.4 2.0 %shard_map.50 = (f32[768,256]{1,0:T(8,128)S(1)}, bf16[1536,256]{1,0:T(8,128)(2,1)S(1)}, bf16[1536,256]{1,0:T(8,128)(2,1)S(1)}) custom-call(bf16[1536,256]{1,0:T(8,128)(2,1)S(1)} %get-tuple-element.31.refs_0_, f32[768,256]{1,0:T(8,128)S(1)} %get-tuple-element.32.refs_1_, bf16[768,384]{1,0:T(8,128)(2,1)S(1)} %collective-permute-done.6.refs_2_, ...), custom_call_target="tpu_custom_call" | custom-call | flops 1207959552 | bytes 786432 | tf_op jit(solution)/shard_map/pallas_call | solution.py:203
  48.4 0.0 collective-permute-done.9.refs_3_
  48.4 2.0 %shard_map.51 = (f32[768,256]{1,0:T(8,128)S(1)}, bf16[1536,256]{1,0:T(8,128)(2,1)S(1)}, bf16[1536,256]{1,0:T(8,128)(2,1)S(1)}) custom-call(bf16[1536,256]{1,0:T(8,128)(2,1)S(1)} %get-tuple-element.31.refs_0_, f32[768,256]{1,0:T(8,128)S(1)} %get-tuple-element.35.refs_1_, bf16[768,384]{1,0:T(8,128)(2,1)S(1)} %collective-permute-done.8.refs_2_, ...), custom_call_target="tpu_custom_call" | custom-call | flops 1207959552 | bytes 786432 | tf_op jit(solution)/shard_map/pallas_call | solution.py:203
  50.5 2.8 %shard_map.54.refs_1_ = f32[768,256]{1,0:T(8,128)S(1)} custom-call(bf16[1536,256]{1,0:T(8,128)(2,1)S(1)} %get-tuple-element.31.refs_0_, f32[768,256]{1,0:T(8,128)S(1)} %get-tuple-element.41.refs_1_, bf16[1536,256]{1,0:T(8,128)(2,1)S(1)} %get-tuple-element.33.refs_2_, bf16[1536,256]{1,0:T(8,128)(2,1)S(1)} %get-tuple-element.34.refs_3_, ...), custom_call_target="tpu_custom_call" | custom-call | flops 2415919104 | bytes 786432 | tf_op jit(solution)/shard_map/pallas_call | solution.py:224
  53.2 0.0 collective-permute-done.11.refs_3_
  53.2 2.0 %shard_map.52 = (bf16[768,256]{1,0:T(8,128)(2,1)S(1)}, bf16[1536,256]{1,0:T(8,128)(2,1)S(1)}, bf16[1536,256]{1,0:T(8,128)(2,1)S(1)}) custom-call(bf16[1536,256]{1,0:T(8,128)(2,1)S(1)} %get-tuple-element.31.refs_0_, f32[768,256]{1,0:T(8,128)S(1)} %get-tuple-element.38.refs_1_, bf16[768,384]{1,0:T(8,128)(2,1)S(1)} %collective-permute-done.10.refs_2_, ...), custom_call_target="tpu_custom_call" | custom-call | flops 1207959552 | bytes 786432 | tf_op jit(solution)/shard_map/pallas_call | solution.py:203
  55.3 1.8 %shard_map.55 = bf16[768,256]{1,0:T(8,128)(2,1)S(1)} custom-call(bf16[1536,256]{1,0:T(8,128)(2,1)S(1)} %get-tuple-element.31.refs_0_, f32[768,256]{1,0:T(8,128)S(1)} %shard_map.54.refs_1_, bf16[1536,256]{1,0:T(8,128)(2,1)S(1)} %get-tuple-element.39.refs_6_.refs_2_, bf16[1536,256]{1,0:T(8,128)(2,1)S(1)} %get-tuple-element.40.refs_7_.refs_3_), custom_call_target="tpu_custom_call" | custom-call | flops 1207959552 | bytes 786432 | tf_op jit(solution)/shard_map/pallas_call | solution.py:224
  57.1 1.8 %collective-permute-start.12 = (bf16[768,256]{1,0:T(8,128)(2,1)S(1)}, bf16[768,256]{1,0:T(8,128)(2,1)S(1)}, u32[]{:S(2)}, u32[]{:S(2)}) collective-permute-start(bf16[768,256]{1,0:T(8,128)(2,1)S(1)} %shard_map.55), channel_id=1, source_target_pairs={{0,68},{8,9},{1,69},{9,8},{2,70},{10,11},{3,71},{11,10},{64,4},{72... | collective-permute-start | bytes 1179656 | tf_op jit(solution)/shard_map/ppermute | solution.py:35
  58.8 1.5 %collective-permute-start.13 = (bf16[768,256]{1,0:T(8,128)(2,1)S(1)}, bf16[768,256]{1,0:T(8,128)(2,1)S(1)}, u32[]{:S(2)}, u32[]{:S(2)}) collective-permute-start(bf16[768,256]{1,0:T(8,128)(2,1)S(1)} %get-tuple-element.43), channel_id=1, source_target_pairs={{0,68},{8,9},{1,69},{9,8},{2,70},{10,11},{3,71},{11,10},{64,4},{72... | collective-permute-start | bytes 1179656 | tf_op jit(solution)/shard_map/ppermute | solution.py:35
  60.4 4.0 %shard_map.56 = f32[768,256]{1,0:T(8,128)S(1)} custom-call(bf16[1536,256]{1,0:T(8,128)(2,1)S(1)} %get-tuple-element.27.refs_0_, f32[768,256]{1,0:T(8,128)S(1)} %get-tuple-element.42.refs_1_, bf16[1536,256]{1,0:T(8,128)(2,1)S(1)} %get-tuple-element.33.refs_2_, bf16[1536,256]{1,0:T(8,128)(2,1)S(1)} %get-tuple-element.34.refs_3_, ...), custom_call_target="tpu_custom_call" | custom-call | flops 3623878656 | bytes 786432 | tf_op jit(solution)/shard_map/pallas_call | solution.py:224
  64.4 2.1 %shard_map.57 = f32[384,256]{1,0:T(8,128)S(1)} custom-call(bf16[1536,256]{1,0:T(8,128)(2,1)S(1)} %get-tuple-element.27.refs_0_, f32[384,256]{1,0:T(8,128)S(1)} %get-tuple-element.44.refs_1_, bf16[1536,256]{1,0:T(8,128)(2,1)S(1)} %get-tuple-element.33.refs_2_, bf16[1536,256]{1,0:T(8,128)(2,1)S(1)} %get-tuple-element.34.refs_3_, ...), custom_call_target="tpu_custom_call" | custom-call | flops 1811939328 | bytes 393216 | tf_op jit(solution)/shard_map/pallas_call | solution.py:224
  66.5 0.0 collective-permute-done.12
  66.6 0.0 copy-start.1
  66.6 0.1 collective-permute-start.16
  66.7 3.6 %collective-permute-done.13 = bf16[768,256]{1,0:T(8,128)(2,1)S(1)} collective-permute-done((bf16[768,256]{1,0:T(8,128)(2,1)S(1)}, bf16[768,256]{1,0:T(8,128)(2,1)S(1)}, u32[]{:S(2)}, u32[]{:S(2)}) %collective-permute-start.13) | collective-permute-done | bytes 393248 | tf_op jit(solution)/shard_map/ppermute | solution.py:35
  70.3 0.1 fusion.1
  70.4 0.0 copy-start.2
  70.4 1.5 %collective-permute-start.15 = (bf16[384,256]{1,0:T(8,128)(2,1)S(1)}, bf16[384,256]{1,0:T(8,128)(2,1)S(1)}, u32[]{:S(2)}, u32[]{:S(2)}) collective-permute-start(bf16[384,256]{1,0:T(8,128)(2,1)S(1)} %get-tuple-element.46), channel_id=1, source_target_pairs={{0,2},{8,79},{1,3},{9,78},{2,0},{10,77},{3,1},{11,76},{64,66},{72,... | collective-permute-start | bytes 589832 | tf_op jit(solution)/shard_map/ppermute | solution.py:35
  71.9 0.6 collective-permute-start.14
  72.5 0.0 copy-done.1
  72.5 0.0 copy-done.2
  72.5 0.1 convert_multiply_fusion
  72.6 2.1 %shard_map.53 = f32[384,256]{1,0:T(8,128)S(1)} custom-call(bf16[1536,256]{1,0:T(8,128)(2,1)S(1)} %get-tuple-element.27.refs_0_, f32[384,256]{1,0:T(8,128)S(1)} %get-tuple-element.28.refs_1_, bf16[1536,256]{1,0:T(8,128)(2,1)S(1)} %get-tuple-element.33.refs_2_, bf16[1536,256]{1,0:T(8,128)(2,1)S(1)} %get-tuple-element.34.refs_3_, ...), custom_call_target="tpu_custom_call" | custom-call | flops 1811939328 | bytes 393216 | tf_op jit(solution)/shard_map/pallas_call | solution.py:224
  74.8 0.0 collective-permute-done.16
  74.8 3.0 %collective-permute-done.15 = bf16[384,256]{1,0:T(8,128)(2,1)S(1)} collective-permute-done((bf16[384,256]{1,0:T(8,128)(2,1)S(1)}, bf16[384,256]{1,0:T(8,128)(2,1)S(1)}, u32[]{:S(2)}, u32[]{:S(2)}) %collective-permute-start.15) | collective-permute-done | bytes 196640 | tf_op jit(solution)/shard_map/ppermute | solution.py:35
  77.8 2.0 %collective-permute-done.14 = bf16[384,256]{1,0:T(8,128)(2,1)S(1)} collective-permute-done((bf16[384,256]{1,0:T(8,128)(2,1)S(1)}, bf16[384,256]{1,0:T(8,128)(2,1)S(1)}, u32[]{:S(2)}, u32[]{:S(2)}) %collective-permute-start.14) | collective-permute-done | bytes 196640 | tf_op jit(solution)/shard_map/ppermute | solution.py:35
  79.8 0.9 %convert_add_fusion = f32[384,256]{1,0:T(8,128)} fusion(bf16[384,256]{1,0:T(8,128)(2,1)S(1)} %collective-permute-done.16, bf16[384,256]{1,0:T(8,128)(2,1)S(1)} %collective-permute-done.15, bf16[384,256]{1,0:T(8,128)(2,1)S(1)} %collective-permute-done.14, f32[384,256]{1,0:T(8,128)S(1)} %shard_map.53, f32[384,256]{1,0:T(8,128)S(1)} %convert_multiply_fusion, ...), kind=kLoop, calls=%fused_computation.4 | loop fusion | flops 884736 | bytes 1966080 | tf_op jit(solution)/shard_map/add | solution.py:283
  (2 shorter events, 0.1 us)
Async XLA Ops:
  1.8 7.0 %collective-permute-start.3 = (bf16[384,384]{1,0:T(8,128)(2,1)}, bf16[384,384]{1,0:T(8,128)(2,1)S(1)}, u32[]{:S(2)}, u32[]{:S(2)}) collective-permute-start(bf16[384,384]{1,0:T(8,128)(2,1)} %get-tuple-element.25.refs_0_), channel_id=1, source_target_pairs={{0,16},{8,56},{1,17},{9,57},{2,18},{10,58},{3,19},{11,59},{64,80},... | collective-permute-start | bytes 884744 | tf_op jit(solution)/shard_map/ppermute | solution.py:35
  8.9 1.0 %copy-start = (bf16[384,384]{1,0:T(8,128)(2,1)S(1)}, bf16[384,384]{1,0:T(8,128)(2,1)}, u32[]{:S(2)}) copy-start(bf16[384,384]{1,0:T(8,128)(2,1)} %get-tuple-element.25.refs_0_) | copy-start | bytes 884740
  9.8 2.2 %copy-start.3 = (bf16[384,128]{1,0:T(8,128)(2,1)S(1)}, bf16[384,128]{1,0:T(8,128)(2,1)}, u32[]{:S(2)}) copy-start(bf16[384,128]{1,0:T(8,128)(2,1)} %get-tuple-element.26) | copy-start | bytes 294916
  9.9 11.2 %collective-permute-start.6 = (bf16[768,384]{1,0:T(8,128)(2,1)S(1)}, bf16[768,384]{1,0:T(8,128)(2,1)S(1)}, u32[]{:S(2)}, u32[]{:S(2)}) collective-permute-start(bf16[768,384]{1,0:T(8,128)(2,1)S(1)} %shard_map.47.refs_1_), channel_id=1, source_target_pairs={{0,48},{8,72},{1,49},{9,73},{2,50},{10,74},{3,51},{11,75},{64,112}... | collective-permute-start | bytes 1769480 | tf_op jit(solution)/shard_map/ppermute | solution.py:35
  10.3 24.8 %collective-permute-start.8 = (bf16[768,384]{1,0:T(8,128)(2,1)S(1)}, bf16[768,384]{1,0:T(8,128)(2,1)S(1)}, u32[]{:S(2)}, u32[]{:S(2)}) collective-permute-start(bf16[768,384]{1,0:T(8,128)(2,1)S(1)} %shard_map.47.refs_1_), channel_id=1, source_target_pairs={{0,64},{8,24},{1,65},{9,25},{2,66},{10,26},{3,67},{11,27},{64,0},{... | collective-permute-start | bytes 1769480 | tf_op jit(solution)/shard_map/ppermute | solution.py:35
  12.0 23.6 %collective-permute-start.4 = (bf16[768,384]{1,0:T(8,128)(2,1)S(1)}, bf16[768,384]{1,0:T(8,128)(2,1)S(1)}, u32[]{:S(2)}, u32[]{:S(2)}) collective-permute-start(bf16[768,384]{1,0:T(8,128)(2,1)S(1)} %shard_map.47.refs_1_), channel_id=1, source_target_pairs={{0,8},{1,9},{2,10},{3,11},{4,12},{5,13},{6,14},{7,15},{8,0},{9,1},... | collective-permute-start | bytes 1769480 | tf_op jit(solution)/shard_map/ppermute | solution.py:39
  12.0 14.7 %collective-permute-start = (bf16[384,128]{1,0:T(8,128)(2,1)S(1)}, bf16[384,128]{1,0:T(8,128)(2,1)S(1)}, u32[]{:S(2)}, u32[]{:S(2)}) collective-permute-start(bf16[384,128]{1,0:T(8,128)(2,1)S(1)} %copy-done.3), channel_id=1, source_target_pairs={{0,1},{8,11},{1,0},{9,10},{2,3},{10,9},{3,2},{11,8},{64,65},{72,75... | collective-permute-start | bytes 294920 | tf_op jit(solution)/shard_map/ppermute | solution.py:35
  21.1 19.0 %collective-permute-start.10 = (bf16[768,384]{1,0:T(8,128)(2,1)S(1)}, bf16[768,384]{1,0:T(8,128)(2,1)S(1)}, u32[]{:S(2)}, u32[]{:S(2)}) collective-permute-start(bf16[768,384]{1,0:T(8,128)(2,1)S(1)} %collective-permute-done.6.refs_2_), channel_id=1, source_target_pairs={{0,64},{8,24},{1,65},{9,25},{2,66},{10,26},{3,67},{11,27},{64,0},{... | collective-permute-start | bytes 1769480 | tf_op jit(solution)/shard_map/ppermute | solution.py:35
  22.6 7.3 %collective-permute-start.1 = (bf16[384,128]{1,0:T(8,128)(2,1)S(1)}, bf16[384,128]{1,0:T(8,128)(2,1)S(1)}, u32[]{:S(2)}, u32[]{:S(2)}) collective-permute-start(bf16[384,128]{1,0:T(8,128)(2,1)S(1)} %copy-done.3), channel_id=1, source_target_pairs={{0,3},{8,76},{1,2},{9,77},{2,1},{10,78},{3,0},{11,79},{64,67},{72,... | collective-permute-start | bytes 294920 | tf_op jit(solution)/shard_map/ppermute | solution.py:35
  26.7 6.6 %collective-permute-start.2 = (bf16[384,128]{1,0:T(8,128)(2,1)S(1)}, bf16[384,128]{1,0:T(8,128)(2,1)S(1)}, u32[]{:S(2)}, u32[]{:S(2)}) collective-permute-start(bf16[384,128]{1,0:T(8,128)(2,1)S(1)} %copy-done.3), channel_id=1, source_target_pairs={{0,2},{8,79},{1,3},{9,78},{2,0},{10,77},{3,1},{11,76},{64,66},{72,... | collective-permute-start | bytes 294920 | tf_op jit(solution)/shard_map/ppermute | solution.py:35
  33.3 9.1 %collective-permute-start.5 = (bf16[1536,128]{1,0:T(8,128)(2,1)S(1)}, bf16[1536,128]{1,0:T(8,128)(2,1)S(1)}, u32[]{:S(2)}, u32[]{:S(2)}) collective-permute-start(bf16[1536,128]{1,0:T(8,128)(2,1)S(1)} %shard_map.46.refs_0_), channel_id=1, source_target_pairs={{0,68},{8,9},{1,69},{9,8},{2,70},{10,11},{3,71},{11,10},{64,4},{72... | collective-permute-start | bytes 1179656 | tf_op jit(solution)/shard_map/ppermute | solution.py:35
  35.1 11.3 %collective-permute-start.7 = (bf16[768,384]{1,0:T(8,128)(2,1)S(1)}, bf16[768,384]{1,0:T(8,128)(2,1)S(1)}, u32[]{:S(2)}, u32[]{:S(2)}) collective-permute-start(bf16[768,384]{1,0:T(8,128)(2,1)S(1)} %collective-permute-done.6.refs_2_), channel_id=1, source_target_pairs={{0,8},{1,9},{2,10},{3,11},{4,12},{5,13},{6,14},{7,15},{8,0},{9,1},... | collective-permute-start | bytes 1769480 | tf_op jit(solution)/shard_map/ppermute | solution.py:39
  35.1 13.3 %collective-permute-start.9 = (bf16[768,384]{1,0:T(8,128)(2,1)S(1)}, bf16[768,384]{1,0:T(8,128)(2,1)S(1)}, u32[]{:S(2)}, u32[]{:S(2)}) collective-permute-start(bf16[768,384]{1,0:T(8,128)(2,1)S(1)} %collective-permute-done.8.refs_2_), channel_id=1, source_target_pairs={{0,8},{1,9},{2,10},{3,11},{4,12},{5,13},{6,14},{7,15},{8,0},{9,1},... | collective-permute-start | bytes 1769480 | tf_op jit(solution)/shard_map/ppermute | solution.py:39
  40.1 13.1 %collective-permute-start.11 = (bf16[768,384]{1,0:T(8,128)(2,1)S(1)}, bf16[768,384]{1,0:T(8,128)(2,1)S(1)}, u32[]{:S(2)}, u32[]{:S(2)}) collective-permute-start(bf16[768,384]{1,0:T(8,128)(2,1)S(1)} %collective-permute-done.10.refs_2_), channel_id=1, source_target_pairs={{0,8},{1,9},{2,10},{3,11},{4,12},{5,13},{6,14},{7,15},{8,0},{9,1},... | collective-permute-start | bytes 1769480 | tf_op jit(solution)/shard_map/ppermute | solution.py:39
  57.1 9.5 %collective-permute-start.12 = (bf16[768,256]{1,0:T(8,128)(2,1)S(1)}, bf16[768,256]{1,0:T(8,128)(2,1)S(1)}, u32[]{:S(2)}, u32[]{:S(2)}) collective-permute-start(bf16[768,256]{1,0:T(8,128)(2,1)S(1)} %shard_map.55), channel_id=1, source_target_pairs={{0,68},{8,9},{1,69},{9,8},{2,70},{10,11},{3,71},{11,10},{64,4},{72... | collective-permute-start | bytes 1179656 | tf_op jit(solution)/shard_map/ppermute | solution.py:35
  58.8 11.5 %collective-permute-start.13 = (bf16[768,256]{1,0:T(8,128)(2,1)S(1)}, bf16[768,256]{1,0:T(8,128)(2,1)S(1)}, u32[]{:S(2)}, u32[]{:S(2)}) collective-permute-start(bf16[768,256]{1,0:T(8,128)(2,1)S(1)} %get-tuple-element.43), channel_id=1, source_target_pairs={{0,68},{8,9},{1,69},{9,8},{2,70},{10,11},{3,71},{11,10},{64,4},{72... | collective-permute-start | bytes 1179656 | tf_op jit(solution)/shard_map/ppermute | solution.py:35
  66.6 5.9 %copy-start.1 = (bf16[384,256]{1,0:T(8,128)(2,1)S(1)}, bf16[384,256]{1,0:T(8,128)(2,1)}, u32[]{:S(2)}) copy-start(bf16[384,256]{1,0:T(8,128)(2,1)} %probe_hbm.1) | copy-start | bytes 589828
  66.6 8.2 %collective-permute-start.16 = (bf16[384,256]{1,0:T(8,128)(2,1)S(1)}, bf16[384,256]{1,0:T(8,128)(2,1)S(1)}, u32[]{:S(2)}, u32[]{:S(2)}) collective-permute-start(bf16[384,256]{1,0:T(8,128)(2,1)S(1)} %add_convert_fusion), channel_id=1, source_target_pairs={{0,1},{8,11},{1,0},{9,10},{2,3},{10,9},{3,2},{11,8},{64,65},{72,75... | collective-permute-start | bytes 589832 | tf_op jit(solution)/shard_map/ppermute | solution.py:35
  70.4 2.1 %copy-start.2 = (f32[384]{0:T(512)S(1)}, f32[384]{0:T(512)}, u32[]{:S(2)}) copy-start(f32[384]{0:T(512)} %param.6) | copy-start | bytes 4612
  70.4 7.4 %collective-permute-start.15 = (bf16[384,256]{1,0:T(8,128)(2,1)S(1)}, bf16[384,256]{1,0:T(8,128)(2,1)S(1)}, u32[]{:S(2)}, u32[]{:S(2)}) collective-permute-start(bf16[384,256]{1,0:T(8,128)(2,1)S(1)} %get-tuple-element.46), channel_id=1, source_target_pairs={{0,2},{8,79},{1,3},{9,78},{2,0},{10,77},{3,1},{11,76},{64,66},{72,... | collective-permute-start | bytes 589832 | tf_op jit(solution)/shard_map/ppermute | solution.py:35
  71.9 7.9 %collective-permute-start.14 = (bf16[384,256]{1,0:T(8,128)(2,1)S(1)}, bf16[384,256]{1,0:T(8,128)(2,1)S(1)}, u32[]{:S(2)}, u32[]{:S(2)}) collective-permute-start(bf16[384,256]{1,0:T(8,128)(2,1)S(1)} %get-tuple-element.45), channel_id=1, source_target_pairs={{0,3},{8,76},{1,2},{9,77},{2,1},{10,78},{3,0},{11,79},{64,67},{72,... | collective-permute-start | bytes 589832 | tf_op jit(solution)/shard_map/ppermute | solution.py:35

commit v8 on v7

--- a/solution.py
+++ b/solution.py
@@ -131,9 +131,10 @@
     )
 
 
-def fold(row_ref, at, column, probe):
-    gram = lax.dot_general(row_ref[at, :], column, NT, preferred_element_type=jnp.float32)
-    return jnp.dot(jnp.exp2(gram).astype(jnp.bfloat16), probe, preferred_element_type=jnp.float32)
+def fold(rows, pack_ref, half):
+    column = jnp.concatenate([pack_ref[:, :LANES], half], axis=1)
+    gram = lax.dot_general(rows, column, NT, preferred_element_type=jnp.float32)
+    return jnp.dot(jnp.exp2(gram).astype(jnp.bfloat16), pack_ref[:, LANES:], preferred_element_type=jnp.float32)
 
 
 def fill_rows(pair_ref, left):
@@ -143,92 +144,82 @@
         left[k : k + BLOCK, LANES:] = b
 
 
-def fill_columns(pack_refs, right, probes):
-    start = 0
-    for src in pack_refs:
-        for k in range(0, src.shape[0], BLOCK):
-            a, b = augment(src[k : k + BLOCK, :LANES], True)
-            right[start : start + BLOCK, :LANES] = a
-            right[start : start + BLOCK, LANES:] = b
-            probes[start : start + BLOCK, :] = src[k : k + BLOCK, LANES:]
-            start += BLOCK
-
-
-def columns_shape(packs):
-    cols = sum(q.shape[0] for q in packs)
-    width = packs[0].shape[1] - LANES
-    return [jax.ShapeDtypeStruct((cols, 2 * LANES), jnp.bfloat16), jax.ShapeDtypeStruct((cols, width), jnp.bfloat16)]
-
-
-def first_round(pairs, cuts, packs, columns):
-    count = pairs.shape[0]
-    shape = columns_shape(packs) if packs else [columns[0], columns[1]]
-    width, cols = shape[1].shape[1], shape[1].shape[0]
-    sides = packs or list(columns)
+def fill_half(pack_ref, half):
+    for k in range(0, pack_ref.shape[0], BLOCK):
+        half[k : k + BLOCK, :] = augment(pack_ref[k : k + BLOCK, :LANES], True)[1]
+
+
+def half_of(pack):
+    return jax.ShapeDtypeStruct((pack.shape[0], LANES), jnp.bfloat16)
+
+
+def call(body, inputs, outputs, rows, packs):
+    cols = sum(pack.shape[0] for pack in packs)
+    return pl.pallas_call(
+        body,
+        in_specs=[VMEM] * len(inputs),
+        out_specs=[VMEM] * len(outputs),
+        out_shape=outputs,
+        cost_estimate=cost(rows, cols, packs[0].shape[1] - LANES),
+        compiler_params=params(28),
+    )(*inputs)
+
+
+def first_round(pairs, cuts, known, packs):
+    count, width = pairs.shape[0], (known[0][0] if known else packs[0]).shape[1] - LANES
+    ready, fresh, step = len(known), len(packs), 2 * BLOCK
+    ends = cuts[1:] + [count]
 
     def body(*refs):
-        pair_ref, side_refs, outs = refs[0], refs[1 : 1 + len(sides)], refs[1 + len(sides) :]
-        left, sums = outs[0], outs[1 : len(cuts) + 1]
-        right, probes = outs[-2:] if packs else side_refs
+        pair_ref, refs = refs[0], refs[1:]
+        sides = [(refs[2 * i], refs[2 * i + 1]) for i in range(ready)]
+        pack_refs, outs = refs[2 * ready : 2 * ready + fresh], refs[2 * ready + fresh :]
+        left, sums, halves = outs[0], outs[1 : 1 + len(cuts)], outs[1 + len(cuts) :]
         fill_rows(pair_ref, left)
-        if packs:
-            fill_columns(side_refs, right, probes)
-        part = fold(left, slice(None), right[...], probes[...])
-        for at, ref in zip(cuts, sums, strict=True):
-            ref[...] = part[at : at + ref.shape[0], :]
-
-    ends = cuts[1:] + [count]
-    return pl.pallas_call(
-        body,
-        in_specs=[VMEM] * (1 + len(sides)),
-        out_specs=[VMEM] * (1 + len(cuts) + (2 if packs else 0)),
-        out_shape=[jax.ShapeDtypeStruct((count, 2 * LANES), jnp.bfloat16)]
+        for pack_ref, half in zip(pack_refs, halves, strict=True):
+            fill_half(pack_ref, half)
+            sides.append((pack_ref, half))
+        for row in range(0, count, step):
+            part = sum(fold(left[row : row + step, :], pack_ref, half[...]) for pack_ref, half in sides)
+            for at, end, ref in zip(cuts, ends, sums, strict=True):
+                low, high = max(at, row), min(end, row + step)
+                if low < high:
+                    ref[low - at : high - at, :] = part[low - row : high - row, :]
+
+    return call(
+        body,
+        [pairs, *(x for side in known for x in side), *packs],
+        [jax.ShapeDtypeStruct((count, 2 * LANES), jnp.bfloat16)]
         + [jax.ShapeDtypeStruct((end - at, width), jnp.float32) for at, end in zip(cuts, ends, strict=True)]
-        + (shape if packs else []),
-        cost_estimate=cost(count, cols, width),
-        compiler_params=params(36),
-    )(pairs, *sides)
-
-
-def accumulate(rows, at, old, packs, out_type):
-    count, width = old.shape
-    shape = columns_shape(packs)
+        + [half_of(pack) for pack in packs],
+        count,
+        [side[0] for side in known] + list(packs),
+    )
+
+
+def add_round(rows, at, old, known, packs, out_type):
+    count = old.shape[0]
+    ready, fresh = len(known), len(packs)
 
     def body(*refs):
-        row_ref, old_ref, pack_refs, (out_ref, right, probes) = refs[0], refs[1], refs[2:-3], refs[-3:]
-        fill_columns(pack_refs, right, probes)
-        part = fold(row_ref, pl.ds(at, count), right[...], probes[...])
-        out_ref[...] = (old_ref[...] + part).astype(out_type)
-
-    return pl.pallas_call(
-        body,
-        in_specs=[VMEM] * (2 + len(packs)),
-        out_specs=[VMEM] * 3,
-        out_shape=[jax.ShapeDtypeStruct((count, width), out_type)] + shape,
-        cost_estimate=cost(count, shape[0].shape[0], width),
-        compiler_params=params(28),
-    )(rows, old, *packs)
-
-
-def apply_rows(rows, at, old, columns, out_type):
-    count, width = old.shape
-    flat = [a for pair in columns for a in pair]
-
-    def body(*refs):
-        row_ref, old_ref, rest, out_ref = refs[0], refs[1], refs[2:-1], refs[-1]
+        row_ref, old_ref, refs = refs[0], refs[1], refs[2:]
+        sides = [(refs[2 * i], refs[2 * i + 1]) for i in range(ready)]
+        pack_refs, out_ref, halves = refs[2 * ready : 2 * ready + fresh], refs[2 * ready + fresh], refs[2 * ready + fresh + 1 :]
+        for pack_ref, half in zip(pack_refs, halves, strict=True):
+            fill_half(pack_ref, half)
+            sides.append((pack_ref, half))
         part = old_ref[...]
-        for k in range(0, len(rest), 2):
-            part = part + fold(row_ref, pl.ds(at, count), rest[k][...], rest[k + 1][...])
+        for pack_ref, half in sides:
+            part = part + fold(row_ref[at : at + count, :], pack_ref, half[...])
         out_ref[...] = part.astype(out_type)
 
-    return pl.pallas_call(
-        body,
-        in_specs=[VMEM] * (2 + len(flat)),
-        out_specs=VMEM,
-        out_shape=jax.ShapeDtypeStruct((count, width), out_type),
-        cost_estimate=cost(count, sum(c[0].shape[0] for c in columns), width),
-        compiler_params=params(28),
-    )(rows, old, *flat)
+    return call(
+        body,
+        [rows, old, *(x for side in known for x in side), *packs],
+        [jax.ShapeDtypeStruct(old.shape, out_type)] + [half_of(pack) for pack in packs],
+        count,
+        [side[0] for side in known] + list(packs),
+    )
 
 
 COL_MOVES = ((("x", 1), ("x", 3)), (("x", 3), ("y", 1)), (("y", 1), ("x", 1)))
@@ -247,38 +238,43 @@
     own, pair = pack_own(embeddings.T, inv_length[None, :], probes)
     diag = diagonal(noise, probes)
 
-    got_a = swap(own, move_a)
+    got_a, got_b, got_c = (swap(own, m) for m in (move_a, move_b, move_c))
     rows_p = swap(pair, move_p)
     rows_q = swap(pair, move_q)
     rows_qp = swap(pair, move_q, move_p)
-    pack_a = join(own, got_a)
-    pack_b = swap(pack_a, move_b)
+    got_ab = swap(got_a, move_b)
+    pack_3 = swap(join(got_a, got_b), move_c)
     quads = join(own, rows_p, rows_q, rows_qp)
     rows_r = swap(quads, move_r)
-    other_a = partner(pack_a)
-    pack_c = swap(pack_a, move_c)
-
-    near, total, beside, n, *aug_a = first_round(quads, [0, block, 2 * block], [pack_a, other_a], None)
-
-    other_b, other_c = partner(pack_b), partner(pack_c)
-    pack_d = swap(pack_b, move_c)
-    far, f2, f1 = first_round(rows_r, [0, 2 * block], [], aug_a)
-    f1, *aug_b = accumulate(far, 2 * block, f1, [pack_b, other_b], f32)
-    f1, *aug_c = accumulate(far, 2 * block, f1, [pack_c, other_c], f32)
-    other_d = partner(pack_d)
-    f2 = apply_rows(far, 0, f2, [aug_b, aug_c], f32)
-    f1, *aug_d = accumulate(far, 2 * block, f1, [pack_d, other_d], bf16)
+    pack_1 = join(own, got_a)
+    other_1 = partner(pack_1)
+    pack_2 = join(got_b, got_c)
+    other_2 = partner(pack_2)
+
+    near, total, beside, n, *halves = first_round(quads, [0, block, 2 * block], [], [pack_1, other_1])
+    side_1 = list(zip([pack_1, other_1], halves, strict=True))
+
+    got_abc = swap(got_ab, move_c)
+    other_3 = partner(pack_3)
+    far, f2, f1, *halves = first_round(rows_r, [0, 2 * block], side_1, [pack_2, other_2])
+    side_2 = list(zip([pack_2, other_2], halves, strict=True))
+    pack_4 = join(got_ab, got_abc)
+    other_4 = partner(pack_4)
+    f1, *halves = add_round(far, 2 * block, f1, [], [pack_3, other_3], f32)
+    side_3 = list(zip([pack_3, other_3], halves, strict=True))
+    f1, *halves = add_round(far, 2 * block, f1, [], [pack_4, other_4], bf16)
+    side_4 = list(zip([pack_4, other_4], halves, strict=True))
     in_1 = swap(f1, move_r)
-    f2 = apply_rows(far, 0, f2, [aug_d], bf16)
+    (f2,) = add_round(far, 0, f2, side_3 + side_4, [], bf16)
     in_2 = swap(f2, move_r)
 
-    columns = [aug_b, aug_c, aug_d]
-    n = apply_rows(near, 2 * block, n, columns, f32)
+    sides = side_2 + side_3 + side_4
+    (n,) = add_round(near, 2 * block, n, sides, [], f32)
     from_q = swap((n[:block] + in_1[:block].astype(f32)).astype(bf16), move_q)
     from_qp = swap((n[block:] + in_1[block:].astype(f32)).astype(bf16), move_q, move_p)
-    beside = apply_rows(near, block, beside, columns, f32)
+    (beside,) = add_round(near, block, beside, sides, [], f32)
     from_p = swap((beside + in_2[block:].astype(f32)).astype(bf16), move_p)
-    total = apply_rows(near, 0, total, columns, f32)
+    (total,) = add_round(near, 0, total, sides, [], f32)
     total = total + diag + in_2[:block].astype(f32)
     return total + from_q.astype(f32) + from_qp.astype(f32) + from_p.astype(f32)
 

time: 80.8 us -> 77 us (0.953)
  the two profiles are of different devices: /device:TPU:6 before, /device:TPU:1 now
where the time goes in v8:
time: 77 us; the launch traced here: 76.7 us
  starting transfers between devices  33.3 us (43%)
  Pallas kernels  28.7 us (37%)
  waiting for transfers between devices  13.2 us (17%)
  other arithmetic  1.11 us (1%)
    ppermute x15, starting transfers between devices, swap(): return lax.ppermute(value, AXES, pairs)  26.9 us
    pallas_call x8, Pallas kernels, call(): pl.pallas_call(body, in_specs=[VMEM] * len(inputs), out_specs=[VMEM] * le...  26.6 us
    ppermute x15, waiting for transfers between devices, swap(): return lax.ppermute(value, AXES, pairs)  13.2 us
    ppermute x4, starting transfers between devices, partner(): return lax.ppermute(value, AXES, [(i, i ^ 8) for i in range(128)])  6.44 us
    pallas_call x1, Pallas kernels, pack_own(): pl.pallas_call(body, in_specs=[pl.BlockSpec(memory_space=pltpu.HBM)] * 3,...  1.85 us
  transfers between devices with their start and end apart: 19, of which 6 were waited for; matrix products, arithmetic and copies ran while one was open for 0% of the time, Pallas kernels for 29%

profile of v8, /device:TPU:1, one launch (start us, length us, event | category | flops | bytes accessed | tf_op | source)
XLA Modules:
  0.0 76.7 jit_solution(16079165402461688201)
XLA Ops:
  0.0 1.9 %pack_own.1 = (bf16[384,384]{1,0:T(8,128)(2,1)}, bf16[384,128]{1,0:T(8,128)(2,1)}) custom-call(f32[64,384]{1,0:T(8,128)} %bitcast.2, f32[1,64]{1,0:T(1,128)} %bitcast.3, bf16[384,256]{1,0:T(8,128)(2,1)} %probe_hbm.1), custom_call_target="tpu_custom_call" | custom-call | tf_op jit(solution)/shard_map/pack_own/pallas_call | solution.py:88
  1.9 0.0 copy-start
  1.9 3.4 %collective-permute-start.3 = (bf16[384,384]{1,0:T(8,128)(2,1)}, bf16[384,384]{1,0:T(8,128)(2,1)S(1)}, u32[]{:S(2)}, u32[]{:S(2)}) collective-permute-start(bf16[384,384]{1,0:T(8,128)(2,1)} %get-tuple-element.24.refs_0_), channel_id=1, source_target_pairs={{0,16},{8,56},{1,17},{9,57},{2,18},{10,58},{3,19},{11,59},{64,80},... | collective-permute-start | bytes 884744 | tf_op jit(solution)/shard_map/ppermute | solution.py:35
  5.3 1.3 %collective-permute-start.5 = (bf16[384,384]{1,0:T(8,128)(2,1)}, bf16[384,384]{1,0:T(8,128)(2,1)S(1)}, u32[]{:S(2)}, u32[]{:S(2)}) collective-permute-start(bf16[384,384]{1,0:T(8,128)(2,1)} %get-tuple-element.24.refs_0_), channel_id=1, source_target_pairs={{0,48},{8,72},{1,49},{9,73},{2,50},{10,74},{3,51},{11,75},{64,112}... | collective-permute-start | bytes 884744 | tf_op jit(solution)/shard_map/ppermute | solution.py:35
  6.5 0.0 collective-permute-start.6
  6.6 3.9 %collective-permute-done.3.refs_1_.refs_0_ = bf16[384,384]{1,0:T(8,128)(2,1)S(1)} collective-permute-done((bf16[384,384]{1,0:T(8,128)(2,1)}, bf16[384,384]{1,0:T(8,128)(2,1)S(1)}, u32[]{:S(2)}, u32[]{:S(2)}) %collective-permute-start.3) | collective-permute-done | bytes 294944 | tf_op jit(solution)/shard_map/ppermute | solution.py:35
  10.4 1.5 %collective-permute-start.11 = (bf16[384,384]{1,0:T(8,128)(2,1)S(1)}, bf16[384,384]{1,0:T(8,128)(2,1)S(1)}, u32[]{:S(2)}, u32[]{:S(2)}) collective-permute-start(bf16[384,384]{1,0:T(8,128)(2,1)S(1)} %collective-permute-done.3.refs_1_.refs_0_), channel_id=1, source_target_pairs={{0,48},{8,72},{1,49},{9,73},{2,50},{10,74},{3,51},{11,75},{64,112}... | collective-permute-start | bytes 884744 | tf_op jit(solution)/shard_map/ppermute | solution.py:35
  11.9 0.3 collective-permute-done.5.refs_0_.refs_1_
  12.2 0.1 shard_map.51
  12.3 0.0 copy-start.3
  12.3 0.5 collective-permute-start.9
  12.8 0.0 copy-done
  12.8 0.1 shard_map.47.refs_1_
  12.9 4.4 %collective-permute-start.4 = (bf16[768,384]{1,0:T(8,128)(2,1)S(1)}, bf16[768,384]{1,0:T(8,128)(2,1)S(1)}, u32[]{:S(2)}, u32[]{:S(2)}) collective-permute-start(bf16[768,384]{1,0:T(8,128)(2,1)S(1)} %shard_map.47.refs_1_), channel_id=1, source_target_pairs={{0,8},{1,9},{2,10},{3,11},{4,12},{5,13},{6,14},{7,15},{8,0},{9,1},... | collective-permute-start | bytes 1769480 | tf_op jit(solution)/shard_map/ppermute | solution.py:39
  17.3 0.0 copy-done.3
  17.3 3.9 %collective-permute-start = (bf16[384,128]{1,0:T(8,128)(2,1)S(1)}, bf16[384,128]{1,0:T(8,128)(2,1)S(1)}, u32[]{:S(2)}, u32[]{:S(2)}) collective-permute-start(bf16[384,128]{1,0:T(8,128)(2,1)S(1)} %copy-done.3), channel_id=1, source_target_pairs={{0,1},{8,11},{1,0},{9,10},{2,3},{10,9},{3,2},{11,8},{64,65},{72,75... | collective-permute-start | bytes 294920 | tf_op jit(solution)/shard_map/ppermute | solution.py:35
  21.2 0.0 collective-permute-done.6.refs_1_
  21.2 2.6 %collective-permute-start.1 = (bf16[384,128]{1,0:T(8,128)(2,1)S(1)}, bf16[384,128]{1,0:T(8,128)(2,1)S(1)}, u32[]{:S(2)}, u32[]{:S(2)}) collective-permute-start(bf16[384,128]{1,0:T(8,128)(2,1)S(1)} %copy-done.3), channel_id=1, source_target_pairs={{0,3},{8,76},{1,2},{9,77},{2,1},{10,78},{3,0},{11,79},{64,67},{72,... | collective-permute-start | bytes 294920 | tf_op jit(solution)/shard_map/ppermute | solution.py:35
  23.8 0.1 shard_map.49.refs_5_.refs_2_
  23.8 0.0 collective-permute-done.refs_1_
  23.8 0.1 collective-permute-start.8
  23.9 0.0 collective-permute-done.11.refs_0_
  23.9 0.1 collective-permute-start.12
  24.0 1.8 %collective-permute-done.1.refs_2_ = bf16[384,128]{1,0:T(8,128)(2,1)S(1)} collective-permute-done((bf16[384,128]{1,0:T(8,128)(2,1)S(1)}, bf16[384,128]{1,0:T(8,128)(2,1)S(1)}, u32[]{:S(2)}, u32[]{:S(2)}) %collective-permute-start.1) | collective-permute-done | bytes 98336 | tf_op jit(solution)/shard_map/ppermute | solution.py:35
  25.8 2.8 %collective-permute-start.2 = (bf16[384,128]{1,0:T(8,128)(2,1)S(1)}, bf16[384,128]{1,0:T(8,128)(2,1)S(1)}, u32[]{:S(2)}, u32[]{:S(2)}) collective-permute-start(bf16[384,128]{1,0:T(8,128)(2,1)S(1)} %copy-done.3), channel_id=1, source_target_pairs={{0,2},{8,79},{1,3},{9,78},{2,0},{10,77},{3,1},{11,76},{64,66},{72,... | collective-permute-start | bytes 294920 | tf_op jit(solution)/shard_map/ppermute | solution.py:35
  28.6 4.0 %collective-permute-done.2.refs_3_ = bf16[384,128]{1,0:T(8,128)(2,1)S(1)} collective-permute-done((bf16[384,128]{1,0:T(8,128)(2,1)S(1)}, bf16[384,128]{1,0:T(8,128)(2,1)S(1)}, u32[]{:S(2)}, u32[]{:S(2)}) %collective-permute-start.2) | collective-permute-done | bytes 98336 | tf_op jit(solution)/shard_map/ppermute | solution.py:35
  32.7 0.1 collective-permute-start.7
  32.8 0.0 collective-permute-done.12.refs_1_
  32.8 0.1 shard_map.53.refs_2_.refs_10_.refs_6_
  32.8 1.7 %collective-permute-start.13 = (bf16[768,384]{1,0:T(8,128)(2,1)S(1)}, bf16[768,384]{1,0:T(8,128)(2,1)S(1)}, u32[]{:S(2)}, u32[]{:S(2)}) collective-permute-start(bf16[768,384]{1,0:T(8,128)(2,1)S(1)} %shard_map.53.refs_2_.refs_10_.refs_6_), channel_id=1, source_target_pairs={{0,8},{1,9},{2,10},{3,11},{4,12},{5,13},{6,14},{7,15},{8,0},{9,1},... | collective-permute-start | bytes 1769480 | tf_op jit(solution)/shard_map/ppermute | solution.py:39
  34.5 0.0 collective-permute-done.9.refs_2_.refs_6_
  34.5 0.3 collective-permute-start.10
  34.8 0.0 collective-permute-done.4.refs_2_.refs_3_
  34.8 5.0 %shard_map.48 = (bf16[1536,256]{1,0:T(8,128)(2,1)S(1)}, f32[384,256]{1,0:T(8,128)S(1)}, f32[384,256]{1,0:T(8,128)S(1)}, f32[768,256]{1,0:T(8,128)S(1)}, bf16[768...) custom-call(bf16[1536,128]{1,0:T(8,128)(2,1)S(1)} %shard_map.46.refs_0_, bf16[768,384]{1,0:T(8,128)(2,1)S(1)} %shard_map.47.refs_1_, ...), custom_call_target="tpu_custom_call" | custom-call | flops 2415919104 | bytes 1572864 | tf_op jit(solution)/shard_map/pallas_call | solution.py:158
  39.7 0.0 collective-permute-done.7.refs_0_
  39.8 0.0 collective-permute-done.8.refs_6_.refs_4_
  39.8 6.4 %shard_map.50 = (bf16[1536,256]{1,0:T(8,128)(2,1)S(1)}, f32[768,256]{1,0:T(8,128)S(1)}, f32[768,256]{1,0:T(8,128)S(1)}, bf16[768,128]{1,0:T(8,128)(2,1)S(1)}, bf16[768,128]{1,0:T(8,128)(2,1)S(1)}) custom-call(bf16[1536,128]{1,0:T(8,128)(2,1)S(1)} %collective-permute-done.7.refs_0_, bf16[768,384]{1,0:T(8,128)(2,1)S(1)} %shard_map.47.refs_1_, ...), custom_call_target="tpu_custom_call" | custom-call | flops 4831838208 | bytes 1572864 | tf_op jit(solution)/shard_map/pallas_call | solution.py:158
  46.1 0.0 collective-permute-done.10.refs_3_.refs_8_.refs_4_
  46.1 2.0 %shard_map.52 = (f32[768,256]{1,0:T(8,128)S(1)}, bf16[768,128]{1,0:T(8,128)(2,1)S(1)}, bf16[768,128]{1,0:T(8,128)(2,1)S(1)}) custom-call(bf16[1536,256]{1,0:T(8,128)(2,1)S(1)} %get-tuple-element.32.refs_0_, f32[768,256]{1,0:T(8,128)S(1)} %get-tuple-element.33.refs_1_, bf16[768,384]{1,0:T(8,128)(2,1)S(1)} %collective-permute-done.9.refs_2_.refs_6_, ...), custom_call_target="tpu_custom_call" | custom-call | flops 1207959552 | bytes 786432 | tf_op jit(solution)/shard_map/pallas_call | solution.py:158
  48.2 0.0 collective-permute-done.13.refs_3_.refs_12_.refs_8_
  48.2 2.3 %shard_map.54 = (bf16[768,256]{1,0:T(8,128)(2,1)S(1)}, bf16[768,128]{1,0:T(8,128)(2,1)S(1)}, bf16[768,128]{1,0:T(8,128)(2,1)S(1)}) custom-call(bf16[1536,256]{1,0:T(8,128)(2,1)S(1)} %get-tuple-element.32.refs_0_, f32[768,256]{1,0:T(8,128)S(1)} %get-tuple-element.36.refs_1_, bf16[768,384]{1,0:T(8,128)(2,1)S(1)} %shard_map.53.refs_2_.refs_10_.refs_6_, ...), custom_call_target="tpu_custom_call" | custom-call | flops 1207959552 | bytes 786432 | tf_op jit(solution)/shard_map/pallas_call | solution.py:158
  50.4 2.8 %shard_map.56 = bf16[768,256]{1,0:T(8,128)(2,1)S(1)} custom-call(bf16[1536,256]{1,0:T(8,128)(2,1)S(1)} %get-tuple-element.32.refs_0_, f32[768,256]{1,0:T(8,128)S(1)} %get-tuple-element.39.refs_1_, bf16[768,384]{1,0:T(8,128)(2,1)S(1)} %collective-permute-done.9.refs_2_.refs_6_, bf16[768,128]{1,0:T(8,128)(2,1)S(1)} %get-tuple-element.34.refs_7_.refs_3_, ...), custom_call_target="tpu_custom_call" | custom-call | flops 2415919104 | bytes 786432 | tf_op jit(solution)/shard_map/pallas_call | solution.py:158
  53.2 0.9 %collective-permute-start.14 = (bf16[768,256]{1,0:T(8,128)(2,1)S(1)}, bf16[768,256]{1,0:T(8,128)(2,1)S(1)}, u32[]{:S(2)}, u32[]{:S(2)}) collective-permute-start(bf16[768,256]{1,0:T(8,128)(2,1)S(1)} %shard_map.56), channel_id=1, source_target_pairs={{0,68},{8,9},{1,69},{9,8},{2,70},{10,11},{3,71},{11,10},{64,4},{72... | collective-permute-start | bytes 1179656 | tf_op jit(solution)/shard_map/ppermute | solution.py:35
  54.1 0.6 collective-permute-start.15
  54.8 4.0 %shard_map.57 = f32[768,256]{1,0:T(8,128)S(1)} custom-call(bf16[1536,256]{1,0:T(8,128)(2,1)S(1)} %get-tuple-element.26.refs_0_, f32[768,256]{1,0:T(8,128)S(1)} %get-tuple-element.40.refs_1_, bf16[768,384]{1,0:T(8,128)(2,1)S(1)} %shard_map.49.refs_5_.refs_2_, bf16[768,128]{1,0:T(8,128)(2,1)S(1)} %get-tuple-element.30.refs_3_, ...), custom_call_target="tpu_custom_call" | custom-call | flops 3623878656 | bytes 786432 | tf_op jit(solution)/shard_map/pallas_call | solution.py:158
  58.8 2.1 %shard_map.58 = f32[384,256]{1,0:T(8,128)S(1)} custom-call(bf16[1536,256]{1,0:T(8,128)(2,1)S(1)} %get-tuple-element.26.refs_0_, f32[384,256]{1,0:T(8,128)S(1)} %get-tuple-element.42.refs_1_, bf16[768,384]{1,0:T(8,128)(2,1)S(1)} %shard_map.49.refs_5_.refs_2_, bf16[768,128]{1,0:T(8,128)(2,1)S(1)} %get-tuple-element.30.refs_3_, ...), custom_call_target="tpu_custom_call" | custom-call | flops 1811939328 | bytes 393216 | tf_op jit(solution)/shard_map/pallas_call | solution.py:158
  60.9 0.0 collective-permute-done.14
  61.0 0.0 copy-start.1
  61.0 3.4 %collective-permute-start.18 = (bf16[384,256]{1,0:T(8,128)(2,1)S(1)}, bf16[384,256]{1,0:T(8,128)(2,1)S(1)}, u32[]{:S(2)}, u32[]{:S(2)}) collective-permute-start(bf16[384,256]{1,0:T(8,128)(2,1)S(1)} %add_convert_fusion), channel_id=1, source_target_pairs={{0,1},{8,11},{1,0},{9,10},{2,3},{10,9},{3,2},{11,8},{64,65},{72,75... | collective-permute-start | bytes 589832 | tf_op jit(solution)/shard_map/ppermute | solution.py:35
  64.4 0.0 collective-permute-done.15
  64.4 0.1 fusion.1
  64.5 0.0 copy-start.2
  64.5 3.8 %collective-permute-start.17 = (bf16[384,256]{1,0:T(8,128)(2,1)S(1)}, bf16[384,256]{1,0:T(8,128)(2,1)S(1)}, u32[]{:S(2)}, u32[]{:S(2)}) collective-permute-start(bf16[384,256]{1,0:T(8,128)(2,1)S(1)} %get-tuple-element.44), channel_id=1, source_target_pairs={{0,2},{8,79},{1,3},{9,78},{2,0},{10,77},{3,1},{11,76},{64,66},{72,... | collective-permute-start | bytes 589832 | tf_op jit(solution)/shard_map/ppermute | solution.py:35
  68.3 2.1 %collective-permute-start.16 = (bf16[384,256]{1,0:T(8,128)(2,1)S(1)}, bf16[384,256]{1,0:T(8,128)(2,1)S(1)}, u32[]{:S(2)}, u32[]{:S(2)}) collective-permute-start(bf16[384,256]{1,0:T(8,128)(2,1)S(1)} %get-tuple-element.43), channel_id=1, source_target_pairs={{0,3},{8,76},{1,2},{9,77},{2,1},{10,78},{3,0},{11,79},{64,67},{72,... | collective-permute-start | bytes 589832 | tf_op jit(solution)/shard_map/ppermute | solution.py:35
  70.4 0.0 copy-done.1
  70.4 0.0 copy-done.2
  70.4 0.1 convert_multiply_fusion
  70.5 2.1 %shard_map.55 = f32[384,256]{1,0:T(8,128)S(1)} custom-call(bf16[1536,256]{1,0:T(8,128)(2,1)S(1)} %get-tuple-element.26.refs_0_, f32[384,256]{1,0:T(8,128)S(1)} %get-tuple-element.27.refs_1_, bf16[768,384]{1,0:T(8,128)(2,1)S(1)} %shard_map.49.refs_5_.refs_2_, bf16[768,128]{1,0:T(8,128)(2,1)S(1)} %get-tuple-element.30.refs_3_, ...), custom_call_target="tpu_custom_call" | custom-call | flops 1811939328 | bytes 393216 | tf_op jit(solution)/shard_map/pallas_call | solution.py:158
  72.6 0.0 collective-permute-done.18
  72.6 0.5 collective-permute-done.17
  73.1 2.7 %collective-permute-done.16 = bf16[384,256]{1,0:T(8,128)(2,1)S(1)} collective-permute-done((bf16[384,256]{1,0:T(8,128)(2,1)S(1)}, bf16[384,256]{1,0:T(8,128)(2,1)S(1)}, u32[]{:S(2)}, u32[]{:S(2)}) %collective-permute-start.16) | collective-permute-done | bytes 196640 | tf_op jit(solution)/shard_map/ppermute | solution.py:35
  75.8 0.9 %convert_add_fusion = f32[384,256]{1,0:T(8,128)} fusion(bf16[384,256]{1,0:T(8,128)(2,1)S(1)} %collective-permute-done.18, bf16[384,256]{1,0:T(8,128)(2,1)S(1)} %collective-permute-done.17, bf16[384,256]{1,0:T(8,128)(2,1)S(1)} %collective-permute-done.16, f32[384,256]{1,0:T(8,128)S(1)} %shard_map.55, f32[384,256]{1,0:T(8,128)S(1)} %convert_multiply_fusion, ...), kind=kLoop, calls=%fused_computation.4 | loop fusion | flops 884736 | bytes 1966080 | tf_op jit(solution)/shard_map/add | solution.py:279
  (2 shorter events, 0.1 us)
Async XLA Ops:
  1.9 11.0 %copy-start = (bf16[384,384]{1,0:T(8,128)(2,1)S(1)}, bf16[384,384]{1,0:T(8,128)(2,1)}, u32[]{:S(2)}) copy-start(bf16[384,384]{1,0:T(8,128)(2,1)} %get-tuple-element.24.refs_0_) | copy-start | bytes 884740
  1.9 8.6 %collective-permute-start.3 = (bf16[384,384]{1,0:T(8,128)(2,1)}, bf16[384,384]{1,0:T(8,128)(2,1)S(1)}, u32[]{:S(2)}, u32[]{:S(2)}) collective-permute-start(bf16[384,384]{1,0:T(8,128)(2,1)} %get-tuple-element.24.refs_0_), channel_id=1, source_target_pairs={{0,16},{8,56},{1,17},{9,57},{2,18},{10,58},{3,19},{11,59},{64,80},... | collective-permute-start | bytes 884744 | tf_op jit(solution)/shard_map/ppermute | solution.py:35
  5.3 7.0 %collective-permute-start.5 = (bf16[384,384]{1,0:T(8,128)(2,1)}, bf16[384,384]{1,0:T(8,128)(2,1)S(1)}, u32[]{:S(2)}, u32[]{:S(2)}) collective-permute-start(bf16[384,384]{1,0:T(8,128)(2,1)} %get-tuple-element.24.refs_0_), channel_id=1, source_target_pairs={{0,48},{8,72},{1,49},{9,73},{2,50},{10,74},{3,51},{11,75},{64,112}... | collective-permute-start | bytes 884744 | tf_op jit(solution)/shard_map/ppermute | solution.py:35
  6.5 14.6 %collective-permute-start.6 = (bf16[384,384]{1,0:T(8,128)(2,1)}, bf16[384,384]{1,0:T(8,128)(2,1)S(1)}, u32[]{:S(2)}, u32[]{:S(2)}) collective-permute-start(bf16[384,384]{1,0:T(8,128)(2,1)} %get-tuple-element.24.refs_0_), channel_id=1, source_target_pairs={{0,64},{8,24},{1,65},{9,25},{2,66},{10,26},{3,67},{11,27},{64,0},{... | collective-permute-start | bytes 884744 | tf_op jit(solution)/shard_map/ppermute | solution.py:35
  10.4 13.5 %collective-permute-start.11 = (bf16[384,384]{1,0:T(8,128)(2,1)S(1)}, bf16[384,384]{1,0:T(8,128)(2,1)S(1)}, u32[]{:S(2)}, u32[]{:S(2)}) collective-permute-start(bf16[384,384]{1,0:T(8,128)(2,1)S(1)} %collective-permute-done.3.refs_1_.refs_0_), channel_id=1, source_target_pairs={{0,48},{8,72},{1,49},{9,73},{2,50},{10,74},{3,51},{11,75},{64,112}... | collective-permute-start | bytes 884744 | tf_op jit(solution)/shard_map/ppermute | solution.py:35
  12.3 5.0 %copy-start.3 = (bf16[384,128]{1,0:T(8,128)(2,1)S(1)}, bf16[384,128]{1,0:T(8,128)(2,1)}, u32[]{:S(2)}) copy-start(bf16[384,128]{1,0:T(8,128)(2,1)} %get-tuple-element.25) | copy-start | bytes 294916
  12.3 22.2 %collective-permute-start.9 = (bf16[768,384]{1,0:T(8,128)(2,1)S(1)}, bf16[768,384]{1,0:T(8,128)(2,1)S(1)}, u32[]{:S(2)}, u32[]{:S(2)}) collective-permute-start(bf16[768,384]{1,0:T(8,128)(2,1)S(1)} %shard_map.51), channel_id=1, source_target_pairs={{0,64},{8,24},{1,65},{9,25},{2,66},{10,26},{3,67},{11,27},{64,0},{... | collective-permute-start | bytes 1769480 | tf_op jit(solution)/shard_map/ppermute | solution.py:35
  12.9 21.9 %collective-permute-start.4 = (bf16[768,384]{1,0:T(8,128)(2,1)S(1)}, bf16[768,384]{1,0:T(8,128)(2,1)S(1)}, u32[]{:S(2)}, u32[]{:S(2)}) collective-permute-start(bf16[768,384]{1,0:T(8,128)(2,1)S(1)} %shard_map.47.refs_1_), channel_id=1, source_target_pairs={{0,8},{1,9},{2,10},{3,11},{4,12},{5,13},{6,14},{7,15},{8,0},{9,1},... | collective-permute-start | bytes 1769480 | tf_op jit(solution)/shard_map/ppermute | solution.py:39
  17.3 6.5 %collective-permute-start = (bf16[384,128]{1,0:T(8,128)(2,1)S(1)}, bf16[384,128]{1,0:T(8,128)(2,1)S(1)}, u32[]{:S(2)}, u32[]{:S(2)}) collective-permute-start(bf16[384,128]{1,0:T(8,128)(2,1)S(1)} %copy-done.3), channel_id=1, source_target_pairs={{0,1},{8,11},{1,0},{9,10},{2,3},{10,9},{3,2},{11,8},{64,65},{72,75... | collective-permute-start | bytes 294920 | tf_op jit(solution)/shard_map/ppermute | solution.py:35
  21.2 4.7 %collective-permute-start.1 = (bf16[384,128]{1,0:T(8,128)(2,1)S(1)}, bf16[384,128]{1,0:T(8,128)(2,1)S(1)}, u32[]{:S(2)}, u32[]{:S(2)}) collective-permute-start(bf16[384,128]{1,0:T(8,128)(2,1)S(1)} %copy-done.3), channel_id=1, source_target_pairs={{0,3},{8,76},{1,2},{9,77},{2,1},{10,78},{3,0},{11,79},{64,67},{72,... | collective-permute-start | bytes 294920 | tf_op jit(solution)/shard_map/ppermute | solution.py:35
  23.8 15.9 %collective-permute-start.8 = (bf16[768,384]{1,0:T(8,128)(2,1)S(1)}, bf16[768,384]{1,0:T(8,128)(2,1)S(1)}, u32[]{:S(2)}, u32[]{:S(2)}) collective-permute-start(bf16[768,384]{1,0:T(8,128)(2,1)S(1)} %shard_map.49.refs_5_.refs_2_), channel_id=1, source_target_pairs={{0,8},{1,9},{2,10},{3,11},{4,12},{5,13},{6,14},{7,15},{8,0},{9,1},... | collective-permute-start | bytes 1769480 | tf_op jit(solution)/shard_map/ppermute | solution.py:39
  23.9 8.8 %collective-permute-start.12 = (bf16[384,384]{1,0:T(8,128)(2,1)S(1)}, bf16[384,384]{1,0:T(8,128)(2,1)S(1)}, u32[]{:S(2)}, u32[]{:S(2)}) collective-permute-start(bf16[384,384]{1,0:T(8,128)(2,1)S(1)} %collective-permute-done.11.refs_0_), channel_id=1, source_target_pairs={{0,64},{8,24},{1,65},{9,25},{2,66},{10,26},{3,67},{11,27},{64,0},{... | collective-permute-start | bytes 884744 | tf_op jit(solution)/shard_map/ppermute | solution.py:35
  25.8 6.8 %collective-permute-start.2 = (bf16[384,128]{1,0:T(8,128)(2,1)S(1)}, bf16[384,128]{1,0:T(8,128)(2,1)S(1)}, u32[]{:S(2)}, u32[]{:S(2)}) collective-permute-start(bf16[384,128]{1,0:T(8,128)(2,1)S(1)} %copy-done.3), channel_id=1, source_target_pairs={{0,2},{8,79},{1,3},{9,78},{2,0},{10,77},{3,1},{11,76},{64,66},{72,... | collective-permute-start | bytes 294920 | tf_op jit(solution)/shard_map/ppermute | solution.py:35
  32.7 7.1 %collective-permute-start.7 = (bf16[1536,128]{1,0:T(8,128)(2,1)S(1)}, bf16[1536,128]{1,0:T(8,128)(2,1)S(1)}, u32[]{:S(2)}, u32[]{:S(2)}) collective-permute-start(bf16[1536,128]{1,0:T(8,128)(2,1)S(1)} %shard_map.46.refs_0_), channel_id=1, source_target_pairs={{0,68},{8,9},{1,69},{9,8},{2,70},{10,11},{3,71},{11,10},{64,4},{72... | collective-permute-start | bytes 1179656 | tf_op jit(solution)/shard_map/ppermute | solution.py:35
  32.8 15.3 %collective-permute-start.13 = (bf16[768,384]{1,0:T(8,128)(2,1)S(1)}, bf16[768,384]{1,0:T(8,128)(2,1)S(1)}, u32[]{:S(2)}, u32[]{:S(2)}) collective-permute-start(bf16[768,384]{1,0:T(8,128)(2,1)S(1)} %shard_map.53.refs_2_.refs_10_.refs_6_), channel_id=1, source_target_pairs={{0,8},{1,9},{2,10},{3,11},{4,12},{5,13},{6,14},{7,15},{8,0},{9,1},... | collective-permute-start | bytes 1769480 | tf_op jit(solution)/shard_map/ppermute | solution.py:39
  34.5 11.6 %collective-permute-start.10 = (bf16[768,384]{1,0:T(8,128)(2,1)S(1)}, bf16[768,384]{1,0:T(8,128)(2,1)S(1)}, u32[]{:S(2)}, u32[]{:S(2)}) collective-permute-start(bf16[768,384]{1,0:T(8,128)(2,1)S(1)} %collective-permute-done.9.refs_2_.refs_6_), channel_id=1, source_target_pairs={{0,8},{1,9},{2,10},{3,11},{4,12},{5,13},{6,14},{7,15},{8,0},{9,1},... | collective-permute-start | bytes 1769480 | tf_op jit(solution)/shard_map/ppermute | solution.py:39
  53.2 7.7 %collective-permute-start.14 = (bf16[768,256]{1,0:T(8,128)(2,1)S(1)}, bf16[768,256]{1,0:T(8,128)(2,1)S(1)}, u32[]{:S(2)}, u32[]{:S(2)}) collective-permute-start(bf16[768,256]{1,0:T(8,128)(2,1)S(1)} %shard_map.56), channel_id=1, source_target_pairs={{0,68},{8,9},{1,69},{9,8},{2,70},{10,11},{3,71},{11,10},{64,4},{72... | collective-permute-start | bytes 1179656 | tf_op jit(solution)/shard_map/ppermute | solution.py:35
  54.1 10.3 %collective-permute-start.15 = (bf16[768,256]{1,0:T(8,128)(2,1)S(1)}, bf16[768,256]{1,0:T(8,128)(2,1)S(1)}, u32[]{:S(2)}, u32[]{:S(2)}) collective-permute-start(bf16[768,256]{1,0:T(8,128)(2,1)S(1)} %get-tuple-element.41), channel_id=1, source_target_pairs={{0,68},{8,9},{1,69},{9,8},{2,70},{10,11},{3,71},{11,10},{64,4},{72... | collective-permute-start | bytes 1179656 | tf_op jit(solution)/shard_map/ppermute | solution.py:35
  61.0 9.4 %copy-start.1 = (bf16[384,256]{1,0:T(8,128)(2,1)S(1)}, bf16[384,256]{1,0:T(8,128)(2,1)}, u32[]{:S(2)}) copy-start(bf16[384,256]{1,0:T(8,128)(2,1)} %probe_hbm.1) | copy-start | bytes 589828
  61.0 11.7 %collective-permute-start.18 = (bf16[384,256]{1,0:T(8,128)(2,1)S(1)}, bf16[384,256]{1,0:T(8,128)(2,1)S(1)}, u32[]{:S(2)}, u32[]{:S(2)}) collective-permute-start(bf16[384,256]{1,0:T(8,128)(2,1)S(1)} %add_convert_fusion), channel_id=1, source_target_pairs={{0,1},{8,11},{1,0},{9,10},{2,3},{10,9},{3,2},{11,8},{64,65},{72,75... | collective-permute-start | bytes 589832 | tf_op jit(solution)/shard_map/ppermute | solution.py:35
  64.5 5.8 %copy-start.2 = (f32[384]{0:T(512)S(1)}, f32[384]{0:T(512)}, u32[]{:S(2)}) copy-start(f32[384]{0:T(512)} %param.6) | copy-start | bytes 4612
  64.5 8.6 %collective-permute-start.17 = (bf16[384,256]{1,0:T(8,128)(2,1)S(1)}, bf16[384,256]{1,0:T(8,128)(2,1)S(1)}, u32[]{:S(2)}, u32[]{:S(2)}) collective-permute-start(bf16[384,256]{1,0:T(8,128)(2,1)S(1)} %get-tuple-element.44), channel_id=1, source_target_pairs={{0,2},{8,79},{1,3},{9,78},{2,0},{10,77},{3,1},{11,76},{64,66},{72,... | collective-permute-start | bytes 589832 | tf_op jit(solution)/shard_map/ppermute | solution.py:35
  68.3 7.5 %collective-permute-start.16 = (bf16[384,256]{1,0:T(8,128)(2,1)S(1)}, bf16[384,256]{1,0:T(8,128)(2,1)S(1)}, u32[]{:S(2)}, u32[]{:S(2)}) collective-permute-start(bf16[384,256]{1,0:T(8,128)(2,1)S(1)} %get-tuple-element.43), channel_id=1, source_target_pairs={{0,3},{8,76},{1,2},{9,77},{2,1},{10,78},{3,0},{11,79},{64,67},{72,... | collective-permute-start | bytes 589832 | tf_op jit(solution)/shard_map/ppermute | solution.py:35

commit v9 on v7

--- a/solution.py
+++ b/solution.py
@@ -160,34 +160,104 @@
     return [jax.ShapeDtypeStruct((cols, 2 * LANES), jnp.bfloat16), jax.ShapeDtypeStruct((cols, width), jnp.bfloat16)]
 
 
-def first_round(pairs, cuts, packs, columns):
-    count = pairs.shape[0]
-    shape = columns_shape(packs) if packs else [columns[0], columns[1]]
-    width, cols = shape[1].shape[1], shape[1].shape[0]
-    sides = packs or list(columns)
-
-    def body(*refs):
-        pair_ref, side_refs, outs = refs[0], refs[1 : 1 + len(sides)], refs[1 + len(sides) :]
-        left, sums = outs[0], outs[1 : len(cuts) + 1]
-        right, probes = outs[-2:] if packs else side_refs
+def take_pair(own):
+    def body(own_ref, out_ref):
+        out_ref[...] = own_ref[:, :LANES]
+
+    return pl.pallas_call(
+        body,
+        in_specs=[VMEM],
+        out_specs=VMEM,
+        out_shape=half_of(own),
+        compiler_params=params(8),
+        name="take_pair",
+    )(own)
+
+
+def half_of(pack):
+    return jax.ShapeDtypeStruct((pack.shape[0], LANES), jnp.bfloat16)
+
+
+def prepare_rows(pairs):
+    def body(pair_ref, left):
         fill_rows(pair_ref, left)
-        if packs:
-            fill_columns(side_refs, right, probes)
-        part = fold(left, slice(None), right[...], probes[...])
-        for at, ref in zip(cuts, sums, strict=True):
-            ref[...] = part[at : at + ref.shape[0], :]
-
-    ends = cuts[1:] + [count]
-    return pl.pallas_call(
-        body,
-        in_specs=[VMEM] * (1 + len(sides)),
-        out_specs=[VMEM] * (1 + len(cuts) + (2 if packs else 0)),
+
+    return pl.pallas_call(
+        body,
+        in_specs=[VMEM],
+        out_specs=VMEM,
+        out_shape=jax.ShapeDtypeStruct((pairs.shape[0], 2 * LANES), jnp.bfloat16),
+        compiler_params=params(12),
+    )(pairs)
+
+
+def near_round(rows, packs):
+    count = rows.shape[0]
+    shape = columns_shape(packs)
+    width = shape[1].shape[1]
+    sizes = (BLOCK, BLOCK, 2 * BLOCK)
+
+    def body(*refs):
+        row_ref, pack_refs, (own_ref, beside_ref, rest_ref, right, probes) = refs[0], refs[1:-5], refs[-5:]
+        fill_columns(pack_refs, right, probes)
+        part = fold(row_ref, pl.ds(0, 2 * BLOCK), right[...], probes[...])
+        own_ref[...] = part[:BLOCK, :]
+        beside_ref[...] = part[BLOCK:, :]
+        rest_ref[...] = fold(row_ref, pl.ds(2 * BLOCK, 2 * BLOCK), right[...], probes[...])
+
+    return pl.pallas_call(
+        body,
+        in_specs=[VMEM] * (1 + len(packs)),
+        out_specs=[VMEM] * 5,
+        out_shape=[jax.ShapeDtypeStruct((size, width), jnp.float32) for size in sizes] + shape,
+        cost_estimate=cost(count, shape[0].shape[0], width),
+        compiler_params=params(28),
+    )(rows, *packs)
+
+
+def far_round(pairs, columns):
+    count, width, step = pairs.shape[0], columns[0][1].shape[1], 2 * BLOCK
+    flat = [x for side in columns for x in side]
+
+    def body(*refs):
+        pair_ref, rest, (left, *outs) = refs[0], refs[1:-3], refs[-3:]
+        fill_rows(pair_ref, left)
+        for i, ref in enumerate(outs):
+            at = pl.ds(i * step, step)
+            part = fold(left, at, rest[0][...], rest[1][...])
+            for k in range(2, len(rest), 2):
+                part = part + fold(left, at, rest[k][...], rest[k + 1][...])
+            ref[...] = part
+
+    return pl.pallas_call(
+        body,
+        in_specs=[VMEM] * (1 + len(flat)),
+        out_specs=[VMEM] * 3,
         out_shape=[jax.ShapeDtypeStruct((count, 2 * LANES), jnp.bfloat16)]
-        + [jax.ShapeDtypeStruct((end - at, width), jnp.float32) for at, end in zip(cuts, ends, strict=True)]
-        + (shape if packs else []),
-        cost_estimate=cost(count, cols, width),
-        compiler_params=params(36),
-    )(pairs, *sides)
+        + [jax.ShapeDtypeStruct((step, width), jnp.float32)] * 2,
+        cost_estimate=cost(count, sum(side[0].shape[0] for side in columns), width),
+        compiler_params=params(28),
+    )(pairs, *flat)
+
+
+def far_more(rows, olds, packs):
+    shape, step, n = columns_shape(packs), olds[0].shape[0], len(olds)
+
+    def body(*refs):
+        row_ref, old_refs, pack_refs = refs[0], refs[1 : 1 + n], refs[1 + n : 1 + n + len(packs)]
+        outs, (right, probes) = refs[-2 - n : -2], refs[-2:]
+        fill_columns(pack_refs, right, probes)
+        for i in range(n):
+            outs[i][...] = old_refs[i][...] + fold(row_ref, pl.ds(i * step, step), right[...], probes[...])
+
+    return pl.pallas_call(
+        body,
+        in_specs=[VMEM] * (1 + n + len(packs)),
+        out_specs=[VMEM] * (n + 2),
+        out_shape=[jax.ShapeDtypeStruct(old.shape, jnp.float32) for old in olds] + shape,
+        cost_estimate=cost(n * step, shape[0].shape[0], olds[0].shape[1]),
+        compiler_params=params(28),
+    )(rows, *olds, *packs)
 
 
 def accumulate(rows, at, old, packs, out_type):
@@ -248,32 +318,32 @@
     diag = diagonal(noise, probes)
 
     got_a = swap(own, move_a)
+    got_ab = swap(own, move_b, move_a)
+    got_b = swap(own, move_b)
     rows_p = swap(pair, move_p)
     rows_q = swap(pair, move_q)
     rows_qp = swap(pair, move_q, move_p)
-    pack_a = join(own, got_a)
-    pack_b = swap(pack_a, move_b)
-    quads = join(own, rows_p, rows_q, rows_qp)
+    four = join(own, got_a, got_b, got_ab)
+    pack_c = swap(four, move_c)
+    near_pair = take_pair(own)
+    quads = join(near_pair, rows_p, rows_q, rows_qp)
     rows_r = swap(quads, move_r)
-    other_a = partner(pack_a)
-    pack_c = swap(pack_a, move_c)
-
-    near, total, beside, n, *aug_a = first_round(quads, [0, block, 2 * block], [pack_a, other_a], None)
-
-    other_b, other_c = partner(pack_b), partner(pack_c)
-    pack_d = swap(pack_b, move_c)
-    far, f2, f1 = first_round(rows_r, [0, 2 * block], [], aug_a)
-    f1, *aug_b = accumulate(far, 2 * block, f1, [pack_b, other_b], f32)
-    f1, *aug_c = accumulate(far, 2 * block, f1, [pack_c, other_c], f32)
-    other_d = partner(pack_d)
-    f2 = apply_rows(far, 0, f2, [aug_b, aug_c], f32)
-    f1, *aug_d = accumulate(far, 2 * block, f1, [pack_d, other_d], bf16)
+    pack_a, pack_b = join(own, got_a), join(got_b, got_ab)
+    other_a, other_b = partner(pack_a), partner(pack_b)
+
+    near = prepare_rows(quads)
+    total, beside, n, *aug_a = near_round(near, [pack_a, other_a])
+    n, *aug_b = accumulate(near, 2 * block, n, [pack_b, other_b], f32)
+    far, f2, f1 = far_round(rows_r, [aug_a, aug_b])
+    other_c = partner(pack_c)
+    f2, f1, *aug_c = far_more(far, [f2, f1], [pack_c])
+    f1, *aug_d = accumulate(far, 2 * block, f1, [other_c], bf16)
     in_1 = swap(f1, move_r)
     f2 = apply_rows(far, 0, f2, [aug_d], bf16)
     in_2 = swap(f2, move_r)
 
     columns = [aug_b, aug_c, aug_d]
-    n = apply_rows(near, 2 * block, n, columns, f32)
+    n = apply_rows(near, 2 * block, n, columns[1:], f32)
     from_q = swap((n[:block] + in_1[:block].astype(f32)).astype(bf16), move_q)
     from_qp = swap((n[block:] + in_1[block:].astype(f32)).astype(bf16), move_q, move_p)
     beside = apply_rows(near, block, beside, columns, f32)

time: 80.8 us -> 93.6 us (1.16)
  the two profiles are of different devices: /device:TPU:6 before, /device:TPU:1 now
where the time goes in v9:
time: 93.6 us; the launch traced here: 93.4 us
  waiting for transfers between devices  38.3 us (41%)
  Pallas kernels  29.1 us (31%)
  starting transfers between devices  23.7 us (25%)
  other arithmetic  1.11 us (1%)
  local copies, waits for them, and re-layouts  0.98 us (1%)
    ppermute x13, waiting for transfers between devices, swap(): return lax.ppermute(value, AXES, pairs)  38.3 us
    ppermute x13, starting transfers between devices, swap(): return lax.ppermute(value, AXES, pairs)  22.8 us
    pallas_call x4, Pallas kernels, apply_rows(): pl.pallas_call(body, in_specs=[VMEM] * (2 + len(flat)), out_specs=VMEM, o...  8.59 us
    pallas_call x1, Pallas kernels, far_round(): pl.pallas_call(body, in_specs=[VMEM] * (1 + len(flat)), out_specs=[VMEM]...  6.96 us
    pallas_call x2, Pallas kernels, accumulate(): pl.pallas_call(body, in_specs=[VMEM] * (2 + len(packs)), out_specs=[VMEM]...  4.06 us
    pallas_call x1, Pallas kernels, far_more(): pl.pallas_call(body, in_specs=[VMEM] * (1 + n + len(packs)), out_specs=[V...  3.49 us
    pallas_call x1, Pallas kernels, near_round(): pl.pallas_call(body, in_specs=[VMEM] * (1 + len(packs)), out_specs=[VMEM]...  3.25 us
  transfers between devices with their start and end apart: 16, of which 8 were waited for; matrix products, arithmetic and copies ran while one was open for 0% of the time, Pallas kernels for 27%

profile of v9, /device:TPU:1, one launch (start us, length us, event | category | flops | bytes accessed | tf_op | source)
XLA Modules:
  0.0 93.4 jit_solution(18002142951576510604)
XLA Ops:
  0.0 1.8 %pack_own.1 = (bf16[384,384]{1,0:T(8,128)(2,1)}, bf16[384,128]{1,0:T(8,128)(2,1)}) custom-call(f32[64,384]{1,0:T(8,128)} %bitcast.2, f32[1,64]{1,0:T(1,128)} %bitcast.3, bf16[384,256]{1,0:T(8,128)(2,1)} %probe_hbm.1), custom_call_target="tpu_custom_call" | custom-call | tf_op jit(solution)/shard_map/pack_own/pallas_call | solution.py:88
  1.8 3.4 %collective-permute-start.3 = (bf16[384,384]{1,0:T(8,128)(2,1)}, bf16[384,384]{1,0:T(8,128)(2,1)S(1)}, u32[]{:S(2)}, u32[]{:S(2)}) collective-permute-start(bf16[384,384]{1,0:T(8,128)(2,1)} %get-tuple-element.25.own_ref.refs_0_), channel_id=1, source_target_pairs={{0,16},{8,56},{1,17},{9,57},{2,18},{10,58},{3,19},{11,59},{64,80},... | collective-permute-start | bytes 884744 | tf_op jit(solution)/shard_map/ppermute | solution.py:35
  5.2 1.3 %collective-permute-start.5 = (bf16[384,384]{1,0:T(8,128)(2,1)}, bf16[384,384]{1,0:T(8,128)(2,1)S(1)}, u32[]{:S(2)}, u32[]{:S(2)}) collective-permute-start(bf16[384,384]{1,0:T(8,128)(2,1)} %get-tuple-element.25.own_ref.refs_0_), channel_id=1, source_target_pairs={{0,48},{8,72},{1,49},{9,73},{2,50},{10,74},{3,51},{11,75},{64,112}... | collective-permute-start | bytes 884744 | tf_op jit(solution)/shard_map/ppermute | solution.py:35
  6.5 0.0 collective-permute-start.6
  6.5 6.9 %collective-permute-done.3.refs_1_ = bf16[384,384]{1,0:T(8,128)(2,1)S(1)} collective-permute-done((bf16[384,384]{1,0:T(8,128)(2,1)}, bf16[384,384]{1,0:T(8,128)(2,1)S(1)}, u32[]{:S(2)}, u32[]{:S(2)}) %collective-permute-start.3) | collective-permute-done | bytes 294944 | tf_op jit(solution)/shard_map/ppermute | solution.py:35
  13.4 0.0 collective-permute-done.5.refs_0_.refs_2_
  13.4 6.8 %collective-permute-done.6.refs_1_.refs_3_ = bf16[384,384]{1,0:T(8,128)(2,1)S(1)} collective-permute-done((bf16[384,384]{1,0:T(8,128)(2,1)}, bf16[384,384]{1,0:T(8,128)(2,1)S(1)}, u32[]{:S(2)}, u32[]{:S(2)}) %collective-permute-start.6) | collective-permute-done | bytes 294944 | tf_op jit(solution)/shard_map/ppermute | solution.py:35
  20.2 0.0 copy-start
  20.2 1.0 %copy-done = bf16[384,384]{1,0:T(8,128)(2,1)S(1)} copy-done((bf16[384,384]{1,0:T(8,128)(2,1)S(1)}, bf16[384,384]{1,0:T(8,128)(2,1)}, u32[]{:S(2)}) %copy-start) | copy-done | bytes 294936
  21.2 0.1 shard_map.53
  21.3 0.0 copy-start.4
  21.3 0.0 copy-start.1
  21.3 0.1 collective-permute-start.9
  21.4 0.1 shard_map.48.refs_1_
  21.5 0.8 collective-permute-start.4
  22.3 0.1 shard_map.50.refs_2_
  22.3 0.1 collective-permute-start.7
  22.4 0.0 copy-done.4
  22.4 3.8 %collective-permute-start = (bf16[384,128]{1,0:T(8,128)(2,1)S(1)}, bf16[384,128]{1,0:T(8,128)(2,1)S(1)}, u32[]{:S(2)}, u32[]{:S(2)}) collective-permute-start(bf16[384,128]{1,0:T(8,128)(2,1)S(1)} %copy-done.4), channel_id=1, source_target_pairs={{0,1},{8,11},{1,0},{9,10},{2,3},{10,9},{3,2},{11,8},{64,65},{72,75... | collective-permute-start | bytes 294920 | tf_op jit(solution)/shard_map/ppermute | solution.py:35
  26.2 10.2 %collective-permute-done.9.refs_3_ = bf16[1536,384]{1,0:T(8,128)(2,1)S(1)} collective-permute-done((bf16[1536,384]{1,0:T(8,128)(2,1)S(1)}, bf16[1536,384]{1,0:T(8,128)(2,1)S(1)}, u32[]{:S(2)}, u32[]{:S(2)}) %collective-permute-start.9) | collective-permute-done | bytes 1179680 | tf_op jit(solution)/shard_map/ppermute | solution.py:35
  36.5 0.0 collective-permute-start.10
  36.5 3.0 %collective-permute-start.1 = (bf16[384,128]{1,0:T(8,128)(2,1)S(1)}, bf16[384,128]{1,0:T(8,128)(2,1)S(1)}, u32[]{:S(2)}, u32[]{:S(2)}) collective-permute-start(bf16[384,128]{1,0:T(8,128)(2,1)S(1)} %copy-done.4), channel_id=1, source_target_pairs={{0,3},{8,76},{1,2},{9,77},{2,1},{10,78},{3,0},{11,79},{64,67},{72,... | collective-permute-start | bytes 294920 | tf_op jit(solution)/shard_map/ppermute | solution.py:35
  39.5 0.0 collective-permute-done.refs_1_
  39.5 3.5 %collective-permute-start.2 = (bf16[384,128]{1,0:T(8,128)(2,1)S(1)}, bf16[384,128]{1,0:T(8,128)(2,1)S(1)}, u32[]{:S(2)}, u32[]{:S(2)}) collective-permute-start(bf16[384,128]{1,0:T(8,128)(2,1)S(1)} %copy-done.4), channel_id=1, source_target_pairs={{0,2},{8,79},{1,3},{9,78},{2,0},{10,77},{3,1},{11,76},{64,66},{72,... | collective-permute-start | bytes 294920 | tf_op jit(solution)/shard_map/ppermute | solution.py:35
  43.0 0.0 copy-done.1
  43.0 0.0 collective-permute-done.1.refs_2_
  43.0 4.2 %collective-permute-done.2.refs_3_ = bf16[384,128]{1,0:T(8,128)(2,1)S(1)} collective-permute-done((bf16[384,128]{1,0:T(8,128)(2,1)S(1)}, bf16[384,128]{1,0:T(8,128)(2,1)S(1)}, u32[]{:S(2)}, u32[]{:S(2)}) %collective-permute-start.2) | collective-permute-done | bytes 98336 | tf_op jit(solution)/shard_map/ppermute | solution.py:35
  47.2 0.3 collective-permute-start.8
  47.5 0.7 shard_map.47.refs_0_
  48.2 0.0 collective-permute-done.4.refs_2_
  48.2 3.3 %shard_map.49 = (f32[384,256]{1,0:T(8,128)S(1)}, f32[384,256]{1,0:T(8,128)S(1)}, f32[768,256]{1,0:T(8,128)S(1)}, bf16[1536,256]{1,0:T(8,128)(2,1)S(1)}, bf16[1536,256]{1,0:T(8,128)(2,1)S(1)}) custom-call(bf16[1536,256]{1,0:T(8,128)(2,1)S(1)} %shard_map.47.refs_0_, bf16[768,384]{1,0:T(8,128)(2,1)S(1)} %shard_map.48.refs_1_, ...), custom_call_target="tpu_custom_call" | custom-call | flops 2415919104 | bytes 1572864 | tf_op jit(solution)/shard_map/pallas_call | solution.py:208
  51.4 0.0 collective-permute-done.7.refs_3_
  51.4 2.0 %shard_map.51 = (f32[768,256]{1,0:T(8,128)S(1)}, bf16[1536,256]{1,0:T(8,128)(2,1)S(1)}, bf16[1536,256]{1,0:T(8,128)(2,1)S(1)}) custom-call(bf16[1536,256]{1,0:T(8,128)(2,1)S(1)} %shard_map.47.refs_0_, f32[768,256]{1,0:T(8,128)S(1)} %get-tuple-element.28.refs_1_, bf16[768,384]{1,0:T(8,128)(2,1)S(1)} %shard_map.50.refs_2_, ...), custom_call_target="tpu_custom_call" | custom-call | flops 1207959552 | bytes 786432 | tf_op jit(solution)/shard_map/pallas_call | solution.py:273
  53.5 0.9 collective-permute-done.8.refs_0_
  54.4 7.0 %shard_map.52 = (bf16[1536,256]{1,0:T(8,128)(2,1)S(1)}, f32[768,256]{1,0:T(8,128)S(1)}, f32[768,256]{1,0:T(8,128)S(1)}) custom-call(bf16[1536,128]{1,0:T(8,128)(2,1)S(1)} %collective-permute-done.8.refs_0_, bf16[1536,256]{1,0:T(8,128)(2,1)S(1)} %get-tuple-element.31.refs_1_, bf16[1536,256]{1,0:T(8,128)(2,1)S(1)} %get-tuple-element.32.refs_2_, ...), custom_call_target="tpu_custom_call" | custom-call | flops 4831838208 | bytes 1572864 | tf_op jit(solution)/shard_map/pallas_call | solution.py:232
  61.3 3.5 %shard_map.54 = (f32[768,256]{1,0:T(8,128)S(1)}, f32[768,256]{1,0:T(8,128)S(1)}, bf16[1536,256]{1,0:T(8,128)(2,1)S(1)}, bf16[1536,256]{1,0:T(8,128)(2,1)S(1)}) custom-call(bf16[1536,256]{1,0:T(8,128)(2,1)S(1)} %get-tuple-element.33.refs_0_, f32[768,256]{1,0:T(8,128)S(1)} %get-tuple-element.34.refs_1_, f32[768,256]{1,0:T(8,128)S(1)} %get-tuple-element.35.refs_2_, ...), custom_call_target="tpu_custom_call" | custom-call | flops 2415919104 | bytes 1572864 | tf_op jit(solution)/shard_map/pallas_call | solution.py:253
  64.8 0.0 collective-permute-done.10.refs_2_
  64.8 2.0 %shard_map.55 = (bf16[768,256]{1,0:T(8,128)(2,1)S(1)}, bf16[1536,256]{1,0:T(8,128)(2,1)S(1)}, bf16[1536,256]{1,0:T(8,128)(2,1)S(1)}) custom-call(bf16[1536,256]{1,0:T(8,128)(2,1)S(1)} %get-tuple-element.33.refs_0_, f32[768,256]{1,0:T(8,128)S(1)} %get-tuple-element.38.refs_1_, bf16[1536,384]{1,0:T(8,128)(2,1)S(1)} %collective-permute-done.10.refs_2_), custom_call_target="tpu_custom_call" | custom-call | flops 1207959552 | bytes 786432 | tf_op jit(solution)/shard_map/pallas_call | solution.py:273
  66.9 0.6 collective-permute-start.12
  67.5 1.5 %shard_map.57 = bf16[768,256]{1,0:T(8,128)(2,1)S(1)} custom-call(bf16[1536,256]{1,0:T(8,128)(2,1)S(1)} %get-tuple-element.33.refs_0_, f32[768,256]{1,0:T(8,128)S(1)} %get-tuple-element.41.refs_1_, bf16[1536,256]{1,0:T(8,128)(2,1)S(1)} %get-tuple-element.39.refs_6_.refs_2_.refs_4_, bf16[1536,256]{1,0:T(8,128)(2,1)S(1)} %get-tuple-element.40.refs_7_.refs_3_.refs_5_), custom_call_target="tpu_custom_call" | custom-call | flops 1207959552 | bytes 786432 | tf_op jit(solution)/shard_map/pallas_call | solution.py:294
  69.1 1.0 %collective-permute-start.11 = (bf16[768,256]{1,0:T(8,128)(2,1)S(1)}, bf16[768,256]{1,0:T(8,128)(2,1)S(1)}, u32[]{:S(2)}, u32[]{:S(2)}) collective-permute-start(bf16[768,256]{1,0:T(8,128)(2,1)S(1)} %shard_map.57), channel_id=1, source_target_pairs={{0,68},{8,9},{1,69},{9,8},{2,70},{10,11},{3,71},{11,10},{64,4},{72... | collective-permute-start | bytes 1179656 | tf_op jit(solution)/shard_map/ppermute | solution.py:35
  70.0 2.8 %shard_map.58 = f32[768,256]{1,0:T(8,128)S(1)} custom-call(bf16[1536,256]{1,0:T(8,128)(2,1)S(1)} %shard_map.47.refs_0_, f32[768,256]{1,0:T(8,128)S(1)} %get-tuple-element.42.refs_1_, bf16[1536,256]{1,0:T(8,128)(2,1)S(1)} %get-tuple-element.36.refs_4_.refs_2_, bf16[1536,256]{1,0:T(8,128)(2,1)S(1)} %get-tuple-element.37.refs_5_.refs_3_, ...), custom_call_target="tpu_custom_call" | custom-call | flops 2415919104 | bytes 786432 | tf_op jit(solution)/shard_map/pallas_call | solution.py:294
  72.8 2.1 %shard_map.59 = f32[384,256]{1,0:T(8,128)S(1)} custom-call(bf16[1536,256]{1,0:T(8,128)(2,1)S(1)} %shard_map.47.refs_0_, f32[384,256]{1,0:T(8,128)S(1)} %get-tuple-element.44.refs_1_, bf16[1536,256]{1,0:T(8,128)(2,1)S(1)} %get-tuple-element.29.refs_3_.refs_2_, bf16[1536,256]{1,0:T(8,128)(2,1)S(1)} %get-tuple-element.30.refs_4_.refs_3_, ...), custom_call_target="tpu_custom_call" | custom-call | flops 1811939328 | bytes 393216 | tf_op jit(solution)/shard_map/pallas_call | solution.py:294
  75.0 0.0 copy-start.2
  75.0 0.0 copy-start.3
  75.0 0.0 collective-permute-done.12
  75.0 0.1 fusion.1
  75.1 2.4 %collective-permute-start.13 = (bf16[384,256]{1,0:T(8,128)(2,1)S(1)}, bf16[384,256]{1,0:T(8,128)(2,1)S(1)}, u32[]{:S(2)}, u32[]{:S(2)}) collective-permute-start(bf16[384,256]{1,0:T(8,128)(2,1)S(1)} %get-tuple-element.45), channel_id=1, source_target_pairs={{0,3},{8,76},{1,2},{9,77},{2,1},{10,78},{3,0},{11,79},{64,67},{72,... | collective-permute-start | bytes 589832 | tf_op jit(solution)/shard_map/ppermute | solution.py:35
  77.5 2.8 %collective-permute-start.14 = (bf16[384,256]{1,0:T(8,128)(2,1)S(1)}, bf16[384,256]{1,0:T(8,128)(2,1)S(1)}, u32[]{:S(2)}, u32[]{:S(2)}) collective-permute-start(bf16[384,256]{1,0:T(8,128)(2,1)S(1)} %get-tuple-element.46), channel_id=1, source_target_pairs={{0,2},{8,79},{1,3},{9,78},{2,0},{10,77},{3,1},{11,76},{64,66},{72,... | collective-permute-start | bytes 589832 | tf_op jit(solution)/shard_map/ppermute | solution.py:35
  80.3 0.0 collective-permute-done.11
  80.4 0.6 collective-permute-start.15
  81.0 0.0 copy-done.2
  81.0 0.0 copy-done.3
  81.0 0.1 convert_multiply_fusion
  81.1 2.1 %shard_map.56 = f32[384,256]{1,0:T(8,128)S(1)} custom-call(bf16[1536,256]{1,0:T(8,128)(2,1)S(1)} %shard_map.47.refs_0_, f32[384,256]{1,0:T(8,128)S(1)} %get-tuple-element.27.refs_1_, bf16[1536,256]{1,0:T(8,128)(2,1)S(1)} %get-tuple-element.29.refs_3_.refs_2_, bf16[1536,256]{1,0:T(8,128)(2,1)S(1)} %get-tuple-element.30.refs_4_.refs_3_, ...), custom_call_target="tpu_custom_call" | custom-call | flops 1811939328 | bytes 393216 | tf_op jit(solution)/shard_map/pallas_call | solution.py:294
  83.2 0.1 collective-permute-done.13
  83.3 5.5 %collective-permute-done.14 = bf16[384,256]{1,0:T(8,128)(2,1)S(1)} collective-permute-done((bf16[384,256]{1,0:T(8,128)(2,1)S(1)}, bf16[384,256]{1,0:T(8,128)(2,1)S(1)}, u32[]{:S(2)}, u32[]{:S(2)}) %collective-permute-start.14) | collective-permute-done | bytes 196640 | tf_op jit(solution)/shard_map/ppermute | solution.py:35
  88.8 3.8 %collective-permute-done.15 = bf16[384,256]{1,0:T(8,128)(2,1)S(1)} collective-permute-done((bf16[384,256]{1,0:T(8,128)(2,1)S(1)}, bf16[384,256]{1,0:T(8,128)(2,1)S(1)}, u32[]{:S(2)}, u32[]{:S(2)}) %collective-permute-start.15) | collective-permute-done | bytes 196640 | tf_op jit(solution)/shard_map/ppermute | solution.py:35
  92.6 0.9 convert_add_fusion
  (3 shorter events, 0.1 us)
Async XLA Ops:
  1.8 11.6 %collective-permute-start.3 = (bf16[384,384]{1,0:T(8,128)(2,1)}, bf16[384,384]{1,0:T(8,128)(2,1)S(1)}, u32[]{:S(2)}, u32[]{:S(2)}) collective-permute-start(bf16[384,384]{1,0:T(8,128)(2,1)} %get-tuple-element.25.own_ref.refs_0_), channel_id=1, source_target_pairs={{0,16},{8,56},{1,17},{9,57},{2,18},{10,58},{3,19},{11,59},{64,80},... | collective-permute-start | bytes 884744 | tf_op jit(solution)/shard_map/ppermute | solution.py:35
  5.2 8.2 %collective-permute-start.5 = (bf16[384,384]{1,0:T(8,128)(2,1)}, bf16[384,384]{1,0:T(8,128)(2,1)S(1)}, u32[]{:S(2)}, u32[]{:S(2)}) collective-permute-start(bf16[384,384]{1,0:T(8,128)(2,1)} %get-tuple-element.25.own_ref.refs_0_), channel_id=1, source_target_pairs={{0,48},{8,72},{1,49},{9,73},{2,50},{10,74},{3,51},{11,75},{64,112}... | collective-permute-start | bytes 884744 | tf_op jit(solution)/shard_map/ppermute | solution.py:35
  6.5 13.7 %collective-permute-start.6 = (bf16[384,384]{1,0:T(8,128)(2,1)}, bf16[384,384]{1,0:T(8,128)(2,1)S(1)}, u32[]{:S(2)}, u32[]{:S(2)}) collective-permute-start(bf16[384,384]{1,0:T(8,128)(2,1)} %get-tuple-element.25.own_ref.refs_0_), channel_id=1, source_target_pairs={{0,32},{8,120},{1,33},{9,121},{2,34},{10,122},{3,35},{11,123},{64,... | collective-permute-start | bytes 884744 | tf_op jit(solution)/shard_map/ppermute | solution.py:35
  20.2 1.0 %copy-start = (bf16[384,384]{1,0:T(8,128)(2,1)S(1)}, bf16[384,384]{1,0:T(8,128)(2,1)}, u32[]{:S(2)}) copy-start(bf16[384,384]{1,0:T(8,128)(2,1)} %get-tuple-element.25.own_ref.refs_0_) | copy-start | bytes 884740
  21.3 1.1 %copy-start.4 = (bf16[384,128]{1,0:T(8,128)(2,1)S(1)}, bf16[384,128]{1,0:T(8,128)(2,1)}, u32[]{:S(2)}) copy-start(bf16[384,128]{1,0:T(8,128)(2,1)} %get-tuple-element.26) | copy-start | bytes 294916
  21.3 21.7 %copy-start.1 = (bf16[384,384]{1,0:T(8,128)(2,1)S(1)}, bf16[384,384]{1,0:T(8,128)(2,1)}, u32[]{:S(2)}) copy-start(bf16[384,384]{1,0:T(8,128)(2,1)} %get-tuple-element.25.own_ref.refs_0_) | copy-start | bytes 884740
  21.3 15.1 %collective-permute-start.9 = (bf16[1536,384]{1,0:T(8,128)(2,1)S(1)}, bf16[1536,384]{1,0:T(8,128)(2,1)S(1)}, u32[]{:S(2)}, u32[]{:S(2)}) collective-permute-start(bf16[1536,384]{1,0:T(8,128)(2,1)S(1)} %shard_map.53), channel_id=1, source_target_pairs={{0,64},{8,24},{1,65},{9,25},{2,66},{10,26},{3,67},{11,27},{64,0},{... | collective-permute-start | bytes 3538952 | tf_op jit(solution)/shard_map/ppermute | solution.py:35
  21.5 26.7 %collective-permute-start.4 = (bf16[768,384]{1,0:T(8,128)(2,1)S(1)}, bf16[768,384]{1,0:T(8,128)(2,1)S(1)}, u32[]{:S(2)}, u32[]{:S(2)}) collective-permute-start(bf16[768,384]{1,0:T(8,128)(2,1)S(1)} %shard_map.48.refs_1_), channel_id=1, source_target_pairs={{0,8},{1,9},{2,10},{3,11},{4,12},{5,13},{6,14},{7,15},{8,0},{9,1},... | collective-permute-start | bytes 1769480 | tf_op jit(solution)/shard_map/ppermute | solution.py:39
  22.3 29.1 %collective-permute-start.7 = (bf16[768,384]{1,0:T(8,128)(2,1)S(1)}, bf16[768,384]{1,0:T(8,128)(2,1)S(1)}, u32[]{:S(2)}, u32[]{:S(2)}) collective-permute-start(bf16[768,384]{1,0:T(8,128)(2,1)S(1)} %shard_map.50.refs_2_), channel_id=1, source_target_pairs={{0,8},{1,9},{2,10},{3,11},{4,12},{5,13},{6,14},{7,15},{8,0},{9,1},... | collective-permute-start | bytes 1769480 | tf_op jit(solution)/shard_map/ppermute | solution.py:39
  22.4 17.1 %collective-permute-start = (bf16[384,128]{1,0:T(8,128)(2,1)S(1)}, bf16[384,128]{1,0:T(8,128)(2,1)S(1)}, u32[]{:S(2)}, u32[]{:S(2)}) collective-permute-start(bf16[384,128]{1,0:T(8,128)(2,1)S(1)} %copy-done.4), channel_id=1, source_target_pairs={{0,1},{8,11},{1,0},{9,10},{2,3},{10,9},{3,2},{11,8},{64,65},{72,75... | collective-permute-start | bytes 294920 | tf_op jit(solution)/shard_map/ppermute | solution.py:35
  36.5 28.4 %collective-permute-start.10 = (bf16[1536,384]{1,0:T(8,128)(2,1)S(1)}, bf16[1536,384]{1,0:T(8,128)(2,1)S(1)}, u32[]{:S(2)}, u32[]{:S(2)}) collective-permute-start(bf16[1536,384]{1,0:T(8,128)(2,1)S(1)} %collective-permute-done.9.refs_3_), channel_id=1, source_target_pairs={{0,8},{1,9},{2,10},{3,11},{4,12},{5,13},{6,14},{7,15},{8,0},{9,1},... | collective-permute-start | bytes 3538952 | tf_op jit(solution)/shard_map/ppermute | solution.py:39
  36.5 6.5 %collective-permute-start.1 = (bf16[384,128]{1,0:T(8,128)(2,1)S(1)}, bf16[384,128]{1,0:T(8,128)(2,1)S(1)}, u32[]{:S(2)}, u32[]{:S(2)}) collective-permute-start(bf16[384,128]{1,0:T(8,128)(2,1)S(1)} %copy-done.4), channel_id=1, source_target_pairs={{0,3},{8,76},{1,2},{9,77},{2,1},{10,78},{3,0},{11,79},{64,67},{72,... | collective-permute-start | bytes 294920 | tf_op jit(solution)/shard_map/ppermute | solution.py:35
  39.5 7.7 %collective-permute-start.2 = (bf16[384,128]{1,0:T(8,128)(2,1)S(1)}, bf16[384,128]{1,0:T(8,128)(2,1)S(1)}, u32[]{:S(2)}, u32[]{:S(2)}) collective-permute-start(bf16[384,128]{1,0:T(8,128)(2,1)S(1)} %copy-done.4), channel_id=1, source_target_pairs={{0,2},{8,79},{1,3},{9,78},{2,0},{10,77},{3,1},{11,76},{64,66},{72,... | collective-permute-start | bytes 294920 | tf_op jit(solution)/shard_map/ppermute | solution.py:35
  47.2 7.2 %collective-permute-start.8 = (bf16[1536,128]{1,0:T(8,128)(2,1)S(1)}, bf16[1536,128]{1,0:T(8,128)(2,1)S(1)}, u32[]{:S(2)}, u32[]{:S(2)}) collective-permute-start(bf16[1536,128]{1,0:T(8,128)(2,1)S(1)} %shard_map.46.pair_ref), channel_id=1, source_target_pairs={{0,68},{8,9},{1,69},{9,8},{2,70},{10,11},{3,71},{11,10},{64,4},{72... | collective-permute-start | bytes 1179656 | tf_op jit(solution)/shard_map/ppermute | solution.py:35
  66.9 8.1 %collective-permute-start.12 = (bf16[768,256]{1,0:T(8,128)(2,1)S(1)}, bf16[768,256]{1,0:T(8,128)(2,1)S(1)}, u32[]{:S(2)}, u32[]{:S(2)}) collective-permute-start(bf16[768,256]{1,0:T(8,128)(2,1)S(1)} %get-tuple-element.43), channel_id=1, source_target_pairs={{0,68},{8,9},{1,69},{9,8},{2,70},{10,11},{3,71},{11,10},{64,4},{72... | collective-permute-start | bytes 1179656 | tf_op jit(solution)/shard_map/ppermute | solution.py:35
  69.1 11.3 %collective-permute-start.11 = (bf16[768,256]{1,0:T(8,128)(2,1)S(1)}, bf16[768,256]{1,0:T(8,128)(2,1)S(1)}, u32[]{:S(2)}, u32[]{:S(2)}) collective-permute-start(bf16[768,256]{1,0:T(8,128)(2,1)S(1)} %shard_map.57), channel_id=1, source_target_pairs={{0,68},{8,9},{1,69},{9,8},{2,70},{10,11},{3,71},{11,10},{64,4},{72... | collective-permute-start | bytes 1179656 | tf_op jit(solution)/shard_map/ppermute | solution.py:35
  75.0 6.0 %copy-start.2 = (bf16[384,256]{1,0:T(8,128)(2,1)S(1)}, bf16[384,256]{1,0:T(8,128)(2,1)}, u32[]{:S(2)}) copy-start(bf16[384,256]{1,0:T(8,128)(2,1)} %probe_hbm.1) | copy-start | bytes 589828
  75.0 6.0 %copy-start.3 = (f32[384]{0:T(512)S(1)}, f32[384]{0:T(512)}, u32[]{:S(2)}) copy-start(f32[384]{0:T(512)} %param.6) | copy-start | bytes 4612
  75.1 8.2 %collective-permute-start.13 = (bf16[384,256]{1,0:T(8,128)(2,1)S(1)}, bf16[384,256]{1,0:T(8,128)(2,1)S(1)}, u32[]{:S(2)}, u32[]{:S(2)}) collective-permute-start(bf16[384,256]{1,0:T(8,128)(2,1)S(1)} %get-tuple-element.45), channel_id=1, source_target_pairs={{0,3},{8,76},{1,2},{9,77},{2,1},{10,78},{3,0},{11,79},{64,67},{72,... | collective-permute-start | bytes 589832 | tf_op jit(solution)/shard_map/ppermute | solution.py:35
  77.5 11.3 %collective-permute-start.14 = (bf16[384,256]{1,0:T(8,128)(2,1)S(1)}, bf16[384,256]{1,0:T(8,128)(2,1)S(1)}, u32[]{:S(2)}, u32[]{:S(2)}) collective-permute-start(bf16[384,256]{1,0:T(8,128)(2,1)S(1)} %get-tuple-element.46), channel_id=1, source_target_pairs={{0,2},{8,79},{1,3},{9,78},{2,0},{10,77},{3,1},{11,76},{64,66},{72,... | collective-permute-start | bytes 589832 | tf_op jit(solution)/shard_map/ppermute | solution.py:35
  80.4 12.2 %collective-permute-start.15 = (bf16[384,256]{1,0:T(8,128)(2,1)S(1)}, bf16[384,256]{1,0:T(8,128)(2,1)S(1)}, u32[]{:S(2)}, u32[]{:S(2)}) collective-permute-start(bf16[384,256]{1,0:T(8,128)(2,1)S(1)} %add_convert_fusion), channel_id=1, source_target_pairs={{0,1},{8,11},{1,0},{9,10},{2,3},{10,9},{3,2},{11,8},{64,65},{72,75... | collective-permute-start | bytes 589832 | tf_op jit(solution)/shard_map/ppermute | solution.py:35

commit v10 on v7

--- a/solution.py
+++ b/solution.py
@@ -160,34 +160,60 @@
     return [jax.ShapeDtypeStruct((cols, 2 * LANES), jnp.bfloat16), jax.ShapeDtypeStruct((cols, width), jnp.bfloat16)]
 
 
-def first_round(pairs, cuts, packs, columns):
-    count = pairs.shape[0]
-    shape = columns_shape(packs) if packs else [columns[0], columns[1]]
-    width, cols = shape[1].shape[1], shape[1].shape[0]
-    sides = packs or list(columns)
+def prepare_rows(pairs):
+    def body(pair_ref, left):
+        fill_rows(pair_ref, left)
+
+    return pl.pallas_call(
+        body,
+        in_specs=[VMEM],
+        out_specs=VMEM,
+        out_shape=jax.ShapeDtypeStruct((pairs.shape[0], 2 * LANES), jnp.bfloat16),
+        compiler_params=params(12),
+    )(pairs)
+
+
+def near_round(rows, packs):
+    count = rows.shape[0]
+    shape = columns_shape(packs)
+    width = shape[1].shape[1]
+    sizes = (BLOCK, BLOCK, 2 * BLOCK)
 
     def body(*refs):
-        pair_ref, side_refs, outs = refs[0], refs[1 : 1 + len(sides)], refs[1 + len(sides) :]
-        left, sums = outs[0], outs[1 : len(cuts) + 1]
-        right, probes = outs[-2:] if packs else side_refs
+        row_ref, pack_refs, (own_ref, beside_ref, rest_ref, right, probes) = refs[0], refs[1:-5], refs[-5:]
+        fill_columns(pack_refs, right, probes)
+        part = fold(row_ref, pl.ds(0, 2 * BLOCK), right[...], probes[...])
+        own_ref[...] = part[:BLOCK, :]
+        beside_ref[...] = part[BLOCK:, :]
+        rest_ref[...] = fold(row_ref, pl.ds(2 * BLOCK, 2 * BLOCK), right[...], probes[...])
+
+    return pl.pallas_call(
+        body,
+        in_specs=[VMEM] * (1 + len(packs)),
+        out_specs=[VMEM] * 5,
+        out_shape=[jax.ShapeDtypeStruct((size, width), jnp.float32) for size in sizes] + shape,
+        cost_estimate=cost(count, shape[0].shape[0], width),
+        compiler_params=params(28),
+    )(rows, *packs)
+
+
+def far_round(pairs, columns):
+    count, width, step = pairs.shape[0], columns[1].shape[1], 2 * BLOCK
+
+    def body(pair_ref, right, probes, left, first_ref, second_ref):
         fill_rows(pair_ref, left)
-        if packs:
-            fill_columns(side_refs, right, probes)
-        part = fold(left, slice(None), right[...], probes[...])
-        for at, ref in zip(cuts, sums, strict=True):
-            ref[...] = part[at : at + ref.shape[0], :]
-
-    ends = cuts[1:] + [count]
-    return pl.pallas_call(
-        body,
-        in_specs=[VMEM] * (1 + len(sides)),
-        out_specs=[VMEM] * (1 + len(cuts) + (2 if packs else 0)),
+        for i, ref in enumerate((first_ref, second_ref)):
+            ref[...] = fold(left, pl.ds(i * step, step), right[...], probes[...])
+
+    return pl.pallas_call(
+        body,
+        in_specs=[VMEM] * 3,
+        out_specs=[VMEM] * 3,
         out_shape=[jax.ShapeDtypeStruct((count, 2 * LANES), jnp.bfloat16)]
-        + [jax.ShapeDtypeStruct((end - at, width), jnp.float32) for at, end in zip(cuts, ends, strict=True)]
-        + (shape if packs else []),
-        cost_estimate=cost(count, cols, width),
-        compiler_params=params(36),
-    )(pairs, *sides)
+        + [jax.ShapeDtypeStruct((step, width), jnp.float32)] * 2,
+        cost_estimate=cost(count, columns[0].shape[0], width),
+        compiler_params=params(28),
+    )(pairs, *columns)
 
 
 def accumulate(rows, at, old, packs, out_type):
@@ -258,13 +284,15 @@
     other_a = partner(pack_a)
     pack_c = swap(pack_a, move_c)
 
-    near, total, beside, n, *aug_a = first_round(quads, [0, block, 2 * block], [pack_a, other_a], None)
+    near = prepare_rows(quads)
+    total, beside, n, *aug_a = near_round(near, [pack_a, other_a])
 
     other_b, other_c = partner(pack_b), partner(pack_c)
     pack_d = swap(pack_b, move_c)
-    far, f2, f1 = first_round(rows_r, [0, 2 * block], [], aug_a)
+    far, f2, f1 = far_round(rows_r, aug_a)
     f1, *aug_b = accumulate(far, 2 * block, f1, [pack_b, other_b], f32)
     f1, *aug_c = accumulate(far, 2 * block, f1, [pack_c, other_c], f32)
+    beside = apply_rows(near, block, beside, [aug_b], f32)
     other_d = partner(pack_d)
     f2 = apply_rows(far, 0, f2, [aug_b, aug_c], f32)
     f1, *aug_d = accumulate(far, 2 * block, f1, [pack_d, other_d], bf16)
@@ -276,7 +304,7 @@
     n = apply_rows(near, 2 * block, n, columns, f32)
     from_q = swap((n[:block] + in_1[:block].astype(f32)).astype(bf16), move_q)
     from_qp = swap((n[block:] + in_1[block:].astype(f32)).astype(bf16), move_q, move_p)
-    beside = apply_rows(near, block, beside, columns, f32)
+    beside = apply_rows(near, block, beside, columns[1:], f32)
     from_p = swap((beside + in_2[block:].astype(f32)).astype(bf16), move_p)
     total = apply_rows(near, 0, total, columns, f32)
     total = total + diag + in_2[:block].astype(f32)

time: 80.8 us -> 81.1 us (level)
  waiting for transfers between devices: 30.5 us -> 31.6 us
  Pallas kernels: 29.3 us -> 28.4 us
    pallas_call x2 -> x3, Pallas kernels: 8.44 us -> 7.27 us  [the longest x1 3.33 us: far_round(): pl.pallas_call(body, in_specs=[VMEM] * 3, out_specs=[VMEM] * 3, out_shape...]
    ppermute x13, waiting for transfers between devices: 30.5 us -> 31.6 us  [swap(): return lax.ppermute(value, AXES, pairs)]
    pallas_call x5 -> x6, Pallas kernels: 12.8 us -> 13.1 us  [apply_rows(): pl.pallas_call(body, in_specs=[VMEM] * (2 + len(flat)), out_specs=VMEM, o...]
  transfers between devices with their start and end apart: 17 -> 17, of which waited for: 8 -> 9; matrix products, arithmetic and copies ran while one was open for 0% -> 0% of each run, Pallas kernels for 29% -> 28%
where the time goes in v10:
time: 81.1 us; the launch traced here: 80.9 us
  waiting for transfers between devices  31.6 us (39%)
  Pallas kernels  28.4 us (35%)
  starting transfers between devices  18.7 us (23%)
  other arithmetic  1.11 us (1%)
  local copies, waits for them, and re-layouts  0.98 us (1%)
    ppermute x13, waiting for transfers between devices, swap(): return lax.ppermute(value, AXES, pairs)  31.6 us
    ppermute x13, starting transfers between devices, swap(): return lax.ppermute(value, AXES, pairs)  17.8 us
    pallas_call x6, Pallas kernels, apply_rows(): pl.pallas_call(body, in_specs=[VMEM] * (2 + len(flat)), out_specs=VMEM, o...  13.1 us
    pallas_call x3, Pallas kernels, accumulate(): pl.pallas_call(body, in_specs=[VMEM] * (2 + len(packs)), out_specs=[VMEM]...  6.09 us
    pallas_call x1, Pallas kernels, far_round(): pl.pallas_call(body, in_specs=[VMEM] * 3, out_specs=[VMEM] * 3, out_shape...  3.33 us
    pallas_call x1, Pallas kernels, near_round(): pl.pallas_call(body, in_specs=[VMEM] * (1 + len(packs)), out_specs=[VMEM]...  3.25 us
    pallas_call x1, Pallas kernels, pack_own(): pl.pallas_call(body, in_specs=[pl.BlockSpec(memory_space=pltpu.HBM)] * 3,...  1.84 us
  transfers between devices with their start and end apart: 17, of which 9 were waited for; matrix products, arithmetic and copies ran while one was open for 0% of the time, Pallas kernels for 28%

profile of v10, /device:TPU:6, one launch (start us, length us, event | category | flops | bytes accessed | tf_op | source)
XLA Modules:
  0.0 80.9 jit_solution(8235556737225539103)
XLA Ops:
  0.0 1.8 %pack_own.1 = (bf16[384,384]{1,0:T(8,128)(2,1)}, bf16[384,128]{1,0:T(8,128)(2,1)}) custom-call(f32[64,384]{1,0:T(8,128)} %bitcast.2, f32[1,64]{1,0:T(1,128)} %bitcast.3, bf16[384,256]{1,0:T(8,128)(2,1)} %probe_hbm.1), custom_call_target="tpu_custom_call" | custom-call | tf_op jit(solution)/shard_map/pack_own/pallas_call | solution.py:88
  1.8 0.9 %collective-permute-start.3 = (bf16[384,384]{1,0:T(8,128)(2,1)}, bf16[384,384]{1,0:T(8,128)(2,1)S(1)}, u32[]{:S(2)}, u32[]{:S(2)}) collective-permute-start(bf16[384,384]{1,0:T(8,128)(2,1)} %get-tuple-element.24.refs_0_), channel_id=1, source_target_pairs={{0,16},{8,56},{1,17},{9,57},{2,18},{10,58},{3,19},{11,59},{64,80},... | collective-permute-start | bytes 884744 | tf_op jit(solution)/shard_map/ppermute | solution.py:35
  2.8 6.1 %collective-permute-done.3.refs_1_ = bf16[384,384]{1,0:T(8,128)(2,1)S(1)} collective-permute-done((bf16[384,384]{1,0:T(8,128)(2,1)}, bf16[384,384]{1,0:T(8,128)(2,1)S(1)}, u32[]{:S(2)}, u32[]{:S(2)}) %collective-permute-start.3) | collective-permute-done | bytes 294944 | tf_op jit(solution)/shard_map/ppermute | solution.py:35
  8.9 0.0 copy-start
  8.9 1.0 %copy-done = bf16[384,384]{1,0:T(8,128)(2,1)S(1)} copy-done((bf16[384,384]{1,0:T(8,128)(2,1)S(1)}, bf16[384,384]{1,0:T(8,128)(2,1)}, u32[]{:S(2)}) %copy-start) | copy-done | bytes 294936
  9.8 0.0 copy-start.3
  9.8 0.1 shard_map.48.refs_1_
  9.9 0.4 collective-permute-start.6
  10.3 1.7 %collective-permute-start.8 = (bf16[768,384]{1,0:T(8,128)(2,1)S(1)}, bf16[768,384]{1,0:T(8,128)(2,1)S(1)}, u32[]{:S(2)}, u32[]{:S(2)}) collective-permute-start(bf16[768,384]{1,0:T(8,128)(2,1)S(1)} %shard_map.48.refs_1_), channel_id=1, source_target_pairs={{0,64},{8,24},{1,65},{9,25},{2,66},{10,26},{3,67},{11,27},{64,0},{... | collective-permute-start | bytes 1769480 | tf_op jit(solution)/shard_map/ppermute | solution.py:35
  12.0 0.0 collective-permute-start.4
  12.0 0.0 copy-done.3
  12.0 1.9 %collective-permute-start = (bf16[384,128]{1,0:T(8,128)(2,1)S(1)}, bf16[384,128]{1,0:T(8,128)(2,1)S(1)}, u32[]{:S(2)}, u32[]{:S(2)}) collective-permute-start(bf16[384,128]{1,0:T(8,128)(2,1)S(1)} %copy-done.3), channel_id=1, source_target_pairs={{0,1},{8,11},{1,0},{9,10},{2,3},{10,9},{3,2},{11,8},{64,65},{72,75... | collective-permute-start | bytes 294920 | tf_op jit(solution)/shard_map/ppermute | solution.py:35
  13.9 7.1 %collective-permute-done.6.refs_2_ = bf16[768,384]{1,0:T(8,128)(2,1)S(1)} collective-permute-done((bf16[768,384]{1,0:T(8,128)(2,1)S(1)}, bf16[768,384]{1,0:T(8,128)(2,1)S(1)}, u32[]{:S(2)}, u32[]{:S(2)}) %collective-permute-start.6) | collective-permute-done | bytes 589856 | tf_op jit(solution)/shard_map/ppermute | solution.py:35
  21.1 1.6 %collective-permute-start.10 = (bf16[768,384]{1,0:T(8,128)(2,1)S(1)}, bf16[768,384]{1,0:T(8,128)(2,1)S(1)}, u32[]{:S(2)}, u32[]{:S(2)}) collective-permute-start(bf16[768,384]{1,0:T(8,128)(2,1)S(1)} %collective-permute-done.6.refs_2_), channel_id=1, source_target_pairs={{0,64},{8,24},{1,65},{9,25},{2,66},{10,26},{3,67},{11,27},{64,0},{... | collective-permute-start | bytes 1769480 | tf_op jit(solution)/shard_map/ppermute | solution.py:35
  22.6 4.0 %collective-permute-start.1 = (bf16[384,128]{1,0:T(8,128)(2,1)S(1)}, bf16[384,128]{1,0:T(8,128)(2,1)S(1)}, u32[]{:S(2)}, u32[]{:S(2)}) collective-permute-start(bf16[384,128]{1,0:T(8,128)(2,1)S(1)} %copy-done.3), channel_id=1, source_target_pairs={{0,3},{8,76},{1,2},{9,77},{2,1},{10,78},{3,0},{11,79},{64,67},{72,... | collective-permute-start | bytes 294920 | tf_op jit(solution)/shard_map/ppermute | solution.py:35
  26.7 0.0 collective-permute-done.refs_1_
  26.7 0.0 collective-permute-start.2
  26.7 3.2 %collective-permute-done.1.refs_2_ = bf16[384,128]{1,0:T(8,128)(2,1)S(1)} collective-permute-done((bf16[384,128]{1,0:T(8,128)(2,1)S(1)}, bf16[384,128]{1,0:T(8,128)(2,1)S(1)}, u32[]{:S(2)}, u32[]{:S(2)}) %collective-permute-start.1) | collective-permute-done | bytes 98336 | tf_op jit(solution)/shard_map/ppermute | solution.py:35
  29.9 3.4 %collective-permute-done.2.refs_3_ = bf16[384,128]{1,0:T(8,128)(2,1)S(1)} collective-permute-done((bf16[384,128]{1,0:T(8,128)(2,1)S(1)}, bf16[384,128]{1,0:T(8,128)(2,1)S(1)}, u32[]{:S(2)}, u32[]{:S(2)}) %collective-permute-start.2) | collective-permute-done | bytes 98336 | tf_op jit(solution)/shard_map/ppermute | solution.py:35
  33.3 1.8 %collective-permute-start.5 = (bf16[1536,128]{1,0:T(8,128)(2,1)S(1)}, bf16[1536,128]{1,0:T(8,128)(2,1)S(1)}, u32[]{:S(2)}, u32[]{:S(2)}) collective-permute-start(bf16[1536,128]{1,0:T(8,128)(2,1)S(1)} %shard_map.46.pair_ref), channel_id=1, source_target_pairs={{0,68},{8,9},{1,69},{9,8},{2,70},{10,11},{3,71},{11,10},{64,4},{72... | collective-permute-start | bytes 1179656 | tf_op jit(solution)/shard_map/ppermute | solution.py:35
  35.1 0.0 collective-permute-start.7
  35.1 0.7 shard_map.47.refs_0_
  35.8 0.0 collective-permute-done.8.refs_2_
  35.8 0.6 collective-permute-start.9
  36.4 0.0 collective-permute-done.4.refs_2_
  36.4 3.3 %shard_map.49 = (f32[384,256]{1,0:T(8,128)S(1)}, f32[384,256]{1,0:T(8,128)S(1)}, f32[768,256]{1,0:T(8,128)S(1)}, bf16[1536,256]{1,0:T(8,128)(2,1)S(1)}, bf16[1536,256]{1,0:T(8,128)(2,1)S(1)}) custom-call(bf16[1536,256]{1,0:T(8,128)(2,1)S(1)} %shard_map.47.refs_0_, bf16[768,384]{1,0:T(8,128)(2,1)S(1)} %shard_map.48.refs_1_, ...), custom_call_target="tpu_custom_call" | custom-call | flops 2415919104 | bytes 1572864 | tf_op jit(solution)/shard_map/pallas_call | solution.py:190
  39.7 0.0 collective-permute-done.10.refs_2_
  39.7 0.3 collective-permute-start.11
  39.9 2.4 %collective-permute-done.5.pair_ref = bf16[1536,128]{1,0:T(8,128)(2,1)S(1)} collective-permute-done((bf16[1536,128]{1,0:T(8,128)(2,1)S(1)}, bf16[1536,128]{1,0:T(8,128)(2,1)S(1)}, u32[]{:S(2)}, u32[]{:S(2)}) %collective-permute-start.5) | collective-permute-done | bytes 393248 | tf_op jit(solution)/shard_map/ppermute | solution.py:35
  42.4 3.3 %shard_map.50 = (bf16[1536,256]{1,0:T(8,128)(2,1)S(1)}, f32[768,256]{1,0:T(8,128)S(1)}, f32[768,256]{1,0:T(8,128)S(1)}) custom-call(bf16[1536,128]{1,0:T(8,128)(2,1)S(1)} %collective-permute-done.5.pair_ref, bf16[1536,256]{1,0:T(8,128)(2,1)S(1)} %get-tuple-element.27.right, bf16[1536,256]{1,0:T(8,128)(2,1)S(1)} %get-tuple-element.28.probes), custom_call_target="tpu_custom_call" | custom-call | flops 2415919104 | bytes 1572864 | tf_op jit(solution)/shard_map/pallas_call | solution.py:208
  45.7 0.0 collective-permute-done.7.refs_3_
  45.7 2.0 %shard_map.51 = (f32[768,256]{1,0:T(8,128)S(1)}, bf16[1536,256]{1,0:T(8,128)(2,1)S(1)}, bf16[1536,256]{1,0:T(8,128)(2,1)S(1)}) custom-call(bf16[1536,256]{1,0:T(8,128)(2,1)S(1)} %get-tuple-element.29.refs_0_, f32[768,256]{1,0:T(8,128)S(1)} %get-tuple-element.30.refs_1_, bf16[768,384]{1,0:T(8,128)(2,1)S(1)} %collective-permute-done.6.refs_2_, ...), custom_call_target="tpu_custom_call" | custom-call | flops 1207959552 | bytes 786432 | tf_op jit(solution)/shard_map/pallas_call | solution.py:229
  47.8 0.9 %shard_map.58.refs_1_ = f32[384,256]{1,0:T(8,128)S(1)} custom-call(bf16[1536,256]{1,0:T(8,128)(2,1)S(1)} %shard_map.47.refs_0_, f32[384,256]{1,0:T(8,128)S(1)} %get-tuple-element.42.refs_1_, bf16[1536,256]{1,0:T(8,128)(2,1)S(1)} %get-tuple-element.31.refs_2_, bf16[1536,256]{1,0:T(8,128)(2,1)S(1)} %get-tuple-element.32.refs_3_), custom_call_target="tpu_custom_call" | custom-call | flops 603979776 | bytes 393216 | tf_op jit(solution)/shard_map/pallas_call | solution.py:250
  48.7 0.0 collective-permute-done.9.refs_3_
  48.7 2.0 %shard_map.52 = (f32[768,256]{1,0:T(8,128)S(1)}, bf16[1536,256]{1,0:T(8,128)(2,1)S(1)}, bf16[1536,256]{1,0:T(8,128)(2,1)S(1)}) custom-call(bf16[1536,256]{1,0:T(8,128)(2,1)S(1)} %get-tuple-element.29.refs_0_, f32[768,256]{1,0:T(8,128)S(1)} %get-tuple-element.33.refs_1_, bf16[768,384]{1,0:T(8,128)(2,1)S(1)} %collective-permute-done.8.refs_2_, ...), custom_call_target="tpu_custom_call" | custom-call | flops 1207959552 | bytes 786432 | tf_op jit(solution)/shard_map/pallas_call | solution.py:229
  50.7 2.8 %shard_map.55.refs_1_ = f32[768,256]{1,0:T(8,128)S(1)} custom-call(bf16[1536,256]{1,0:T(8,128)(2,1)S(1)} %get-tuple-element.29.refs_0_, f32[768,256]{1,0:T(8,128)S(1)} %get-tuple-element.39.refs_1_, bf16[1536,256]{1,0:T(8,128)(2,1)S(1)} %get-tuple-element.31.refs_2_, bf16[1536,256]{1,0:T(8,128)(2,1)S(1)} %get-tuple-element.32.refs_3_, ...), custom_call_target="tpu_custom_call" | custom-call | flops 2415919104 | bytes 786432 | tf_op jit(solution)/shard_map/pallas_call | solution.py:250
  53.5 0.0 collective-permute-done.11.refs_3_
  53.5 2.0 %shard_map.53 = (bf16[768,256]{1,0:T(8,128)(2,1)S(1)}, bf16[1536,256]{1,0:T(8,128)(2,1)S(1)}, bf16[1536,256]{1,0:T(8,128)(2,1)S(1)}) custom-call(bf16[1536,256]{1,0:T(8,128)(2,1)S(1)} %get-tuple-element.29.refs_0_, f32[768,256]{1,0:T(8,128)S(1)} %get-tuple-element.36.refs_1_, bf16[768,384]{1,0:T(8,128)(2,1)S(1)} %collective-permute-done.10.refs_2_, ...), custom_call_target="tpu_custom_call" | custom-call | flops 1207959552 | bytes 786432 | tf_op jit(solution)/shard_map/pallas_call | solution.py:229
  55.5 1.8 %shard_map.56 = bf16[768,256]{1,0:T(8,128)(2,1)S(1)} custom-call(bf16[1536,256]{1,0:T(8,128)(2,1)S(1)} %get-tuple-element.29.refs_0_, f32[768,256]{1,0:T(8,128)S(1)} %shard_map.55.refs_1_, bf16[1536,256]{1,0:T(8,128)(2,1)S(1)} %get-tuple-element.37.refs_6_.refs_2_.refs_4_, bf16[1536,256]{1,0:T(8,128)(2,1)S(1)} %get-tuple-element.38.refs_7_.refs_3_.refs_5_), custom_call_target="tpu_custom_call" | custom-call | flops 1207959552 | bytes 786432 | tf_op jit(solution)/shard_map/pallas_call | solution.py:250
  57.3 1.8 %collective-permute-start.12 = (bf16[768,256]{1,0:T(8,128)(2,1)S(1)}, bf16[768,256]{1,0:T(8,128)(2,1)S(1)}, u32[]{:S(2)}, u32[]{:S(2)}) collective-permute-start(bf16[768,256]{1,0:T(8,128)(2,1)S(1)} %shard_map.56), channel_id=1, source_target_pairs={{0,68},{8,9},{1,69},{9,8},{2,70},{10,11},{3,71},{11,10},{64,4},{72... | collective-permute-start | bytes 1179656 | tf_op jit(solution)/shard_map/ppermute | solution.py:35
  59.1 1.5 %collective-permute-start.13 = (bf16[768,256]{1,0:T(8,128)(2,1)S(1)}, bf16[768,256]{1,0:T(8,128)(2,1)S(1)}, u32[]{:S(2)}, u32[]{:S(2)}) collective-permute-start(bf16[768,256]{1,0:T(8,128)(2,1)S(1)} %get-tuple-element.41), channel_id=1, source_target_pairs={{0,68},{8,9},{1,69},{9,8},{2,70},{10,11},{3,71},{11,10},{64,4},{72... | collective-permute-start | bytes 1179656 | tf_op jit(solution)/shard_map/ppermute | solution.py:35
  60.6 4.0 %shard_map.57 = f32[768,256]{1,0:T(8,128)S(1)} custom-call(bf16[1536,256]{1,0:T(8,128)(2,1)S(1)} %shard_map.47.refs_0_, f32[768,256]{1,0:T(8,128)S(1)} %get-tuple-element.40.refs_1_, bf16[1536,256]{1,0:T(8,128)(2,1)S(1)} %get-tuple-element.31.refs_2_, bf16[1536,256]{1,0:T(8,128)(2,1)S(1)} %get-tuple-element.32.refs_3_, ...), custom_call_target="tpu_custom_call" | custom-call | flops 3623878656 | bytes 786432 | tf_op jit(solution)/shard_map/pallas_call | solution.py:250
  64.6 1.5 %shard_map.59 = f32[384,256]{1,0:T(8,128)S(1)} custom-call(bf16[1536,256]{1,0:T(8,128)(2,1)S(1)} %shard_map.47.refs_0_, f32[384,256]{1,0:T(8,128)S(1)} %shard_map.58.refs_1_, bf16[1536,256]{1,0:T(8,128)(2,1)S(1)} %get-tuple-element.34.refs_4_.refs_2_, bf16[1536,256]{1,0:T(8,128)(2,1)S(1)} %get-tuple-element.35.refs_5_.refs_3_, ...), custom_call_target="tpu_custom_call" | custom-call | flops 1207959552 | bytes 393216 | tf_op jit(solution)/shard_map/pallas_call | solution.py:250
  66.2 0.2 collective-permute-done.12
  66.4 0.0 copy-start.1
  66.4 0.1 collective-permute-start.16
  66.5 4.1 %collective-permute-done.13 = bf16[768,256]{1,0:T(8,128)(2,1)S(1)} collective-permute-done((bf16[768,256]{1,0:T(8,128)(2,1)S(1)}, bf16[768,256]{1,0:T(8,128)(2,1)S(1)}, u32[]{:S(2)}, u32[]{:S(2)}) %collective-permute-start.13) | collective-permute-done | bytes 393248 | tf_op jit(solution)/shard_map/ppermute | solution.py:35
  70.6 0.1 fusion.1
  70.7 0.0 copy-start.2
  70.7 1.0 %collective-permute-start.15 = (bf16[384,256]{1,0:T(8,128)(2,1)S(1)}, bf16[384,256]{1,0:T(8,128)(2,1)S(1)}, u32[]{:S(2)}, u32[]{:S(2)}) collective-permute-start(bf16[384,256]{1,0:T(8,128)(2,1)S(1)} %get-tuple-element.44), channel_id=1, source_target_pairs={{0,2},{8,79},{1,3},{9,78},{2,0},{10,77},{3,1},{11,76},{64,66},{72,... | collective-permute-start | bytes 589832 | tf_op jit(solution)/shard_map/ppermute | solution.py:35
  71.7 1.0 %collective-permute-start.14 = (bf16[384,256]{1,0:T(8,128)(2,1)S(1)}, bf16[384,256]{1,0:T(8,128)(2,1)S(1)}, u32[]{:S(2)}, u32[]{:S(2)}) collective-permute-start(bf16[384,256]{1,0:T(8,128)(2,1)S(1)} %get-tuple-element.43), channel_id=1, source_target_pairs={{0,3},{8,76},{1,2},{9,77},{2,1},{10,78},{3,0},{11,79},{64,67},{72,... | collective-permute-start | bytes 589832 | tf_op jit(solution)/shard_map/ppermute | solution.py:35
  72.8 0.0 copy-done.1
  72.8 0.0 copy-done.2
  72.8 0.1 convert_multiply_fusion
  72.9 2.1 %shard_map.54 = f32[384,256]{1,0:T(8,128)S(1)} custom-call(bf16[1536,256]{1,0:T(8,128)(2,1)S(1)} %shard_map.47.refs_0_, f32[384,256]{1,0:T(8,128)S(1)} %get-tuple-element.26.refs_1_, bf16[1536,256]{1,0:T(8,128)(2,1)S(1)} %get-tuple-element.31.refs_2_, bf16[1536,256]{1,0:T(8,128)(2,1)S(1)} %get-tuple-element.32.refs_3_, ...), custom_call_target="tpu_custom_call" | custom-call | flops 1811939328 | bytes 393216 | tf_op jit(solution)/shard_map/pallas_call | solution.py:250
  75.1 0.0 collective-permute-done.16
  75.1 3.0 %collective-permute-done.15 = bf16[384,256]{1,0:T(8,128)(2,1)S(1)} collective-permute-done((bf16[384,256]{1,0:T(8,128)(2,1)S(1)}, bf16[384,256]{1,0:T(8,128)(2,1)S(1)}, u32[]{:S(2)}, u32[]{:S(2)}) %collective-permute-start.15) | collective-permute-done | bytes 196640 | tf_op jit(solution)/shard_map/ppermute | solution.py:35
  78.1 2.0 %collective-permute-done.14 = bf16[384,256]{1,0:T(8,128)(2,1)S(1)} collective-permute-done((bf16[384,256]{1,0:T(8,128)(2,1)S(1)}, bf16[384,256]{1,0:T(8,128)(2,1)S(1)}, u32[]{:S(2)}, u32[]{:S(2)}) %collective-permute-start.14) | collective-permute-done | bytes 196640 | tf_op jit(solution)/shard_map/ppermute | solution.py:35
  80.1 0.9 %convert_add_fusion = f32[384,256]{1,0:T(8,128)} fusion(bf16[384,256]{1,0:T(8,128)(2,1)S(1)} %collective-permute-done.16, bf16[384,256]{1,0:T(8,128)(2,1)S(1)} %collective-permute-done.15, bf16[384,256]{1,0:T(8,128)(2,1)S(1)} %collective-permute-done.14, f32[384,256]{1,0:T(8,128)S(1)} %shard_map.54, f32[384,256]{1,0:T(8,128)S(1)} %convert_multiply_fusion, ...), kind=kLoop, calls=%fused_computation.4 | loop fusion | flops 884736 | bytes 1966080 | tf_op jit(solution)/shard_map/add | solution.py:311
  (2 shorter events, 0.1 us)
Async XLA Ops:
  1.8 7.0 %collective-permute-start.3 = (bf16[384,384]{1,0:T(8,128)(2,1)}, bf16[384,384]{1,0:T(8,128)(2,1)S(1)}, u32[]{:S(2)}, u32[]{:S(2)}) collective-permute-start(bf16[384,384]{1,0:T(8,128)(2,1)} %get-tuple-element.24.refs_0_), channel_id=1, source_target_pairs={{0,16},{8,56},{1,17},{9,57},{2,18},{10,58},{3,19},{11,59},{64,80},... | collective-permute-start | bytes 884744 | tf_op jit(solution)/shard_map/ppermute | solution.py:35
  8.9 1.0 %copy-start = (bf16[384,384]{1,0:T(8,128)(2,1)S(1)}, bf16[384,384]{1,0:T(8,128)(2,1)}, u32[]{:S(2)}) copy-start(bf16[384,384]{1,0:T(8,128)(2,1)} %get-tuple-element.24.refs_0_) | copy-start | bytes 884740
  9.8 2.2 %copy-start.3 = (bf16[384,128]{1,0:T(8,128)(2,1)S(1)}, bf16[384,128]{1,0:T(8,128)(2,1)}, u32[]{:S(2)}) copy-start(bf16[384,128]{1,0:T(8,128)(2,1)} %get-tuple-element.25) | copy-start | bytes 294916
  9.9 11.2 %collective-permute-start.6 = (bf16[768,384]{1,0:T(8,128)(2,1)S(1)}, bf16[768,384]{1,0:T(8,128)(2,1)S(1)}, u32[]{:S(2)}, u32[]{:S(2)}) collective-permute-start(bf16[768,384]{1,0:T(8,128)(2,1)S(1)} %shard_map.48.refs_1_), channel_id=1, source_target_pairs={{0,48},{8,72},{1,49},{9,73},{2,50},{10,74},{3,51},{11,75},{64,112}... | collective-permute-start | bytes 1769480 | tf_op jit(solution)/shard_map/ppermute | solution.py:35
  10.3 25.5 %collective-permute-start.8 = (bf16[768,384]{1,0:T(8,128)(2,1)S(1)}, bf16[768,384]{1,0:T(8,128)(2,1)S(1)}, u32[]{:S(2)}, u32[]{:S(2)}) collective-permute-start(bf16[768,384]{1,0:T(8,128)(2,1)S(1)} %shard_map.48.refs_1_), channel_id=1, source_target_pairs={{0,64},{8,24},{1,65},{9,25},{2,66},{10,26},{3,67},{11,27},{64,0},{... | collective-permute-start | bytes 1769480 | tf_op jit(solution)/shard_map/ppermute | solution.py:35
  12.0 24.4 %collective-permute-start.4 = (bf16[768,384]{1,0:T(8,128)(2,1)S(1)}, bf16[768,384]{1,0:T(8,128)(2,1)S(1)}, u32[]{:S(2)}, u32[]{:S(2)}) collective-permute-start(bf16[768,384]{1,0:T(8,128)(2,1)S(1)} %shard_map.48.refs_1_), channel_id=1, source_target_pairs={{0,8},{1,9},{2,10},{3,11},{4,12},{5,13},{6,14},{7,15},{8,0},{9,1},... | collective-permute-start | bytes 1769480 | tf_op jit(solution)/shard_map/ppermute | solution.py:39
  12.0 14.7 %collective-permute-start = (bf16[384,128]{1,0:T(8,128)(2,1)S(1)}, bf16[384,128]{1,0:T(8,128)(2,1)S(1)}, u32[]{:S(2)}, u32[]{:S(2)}) collective-permute-start(bf16[384,128]{1,0:T(8,128)(2,1)S(1)} %copy-done.3), channel_id=1, source_target_pairs={{0,1},{8,11},{1,0},{9,10},{2,3},{10,9},{3,2},{11,8},{64,65},{72,75... | collective-permute-start | bytes 294920 | tf_op jit(solution)/shard_map/ppermute | solution.py:35
  21.1 18.6 %collective-permute-start.10 = (bf16[768,384]{1,0:T(8,128)(2,1)S(1)}, bf16[768,384]{1,0:T(8,128)(2,1)S(1)}, u32[]{:S(2)}, u32[]{:S(2)}) collective-permute-start(bf16[768,384]{1,0:T(8,128)(2,1)S(1)} %collective-permute-done.6.refs_2_), channel_id=1, source_target_pairs={{0,64},{8,24},{1,65},{9,25},{2,66},{10,26},{3,67},{11,27},{64,0},{... | collective-permute-start | bytes 1769480 | tf_op jit(solution)/shard_map/ppermute | solution.py:35
  22.6 7.3 %collective-permute-start.1 = (bf16[384,128]{1,0:T(8,128)(2,1)S(1)}, bf16[384,128]{1,0:T(8,128)(2,1)S(1)}, u32[]{:S(2)}, u32[]{:S(2)}) collective-permute-start(bf16[384,128]{1,0:T(8,128)(2,1)S(1)} %copy-done.3), channel_id=1, source_target_pairs={{0,3},{8,76},{1,2},{9,77},{2,1},{10,78},{3,0},{11,79},{64,67},{72,... | collective-permute-start | bytes 294920 | tf_op jit(solution)/shard_map/ppermute | solution.py:35
  26.7 6.6 %collective-permute-start.2 = (bf16[384,128]{1,0:T(8,128)(2,1)S(1)}, bf16[384,128]{1,0:T(8,128)(2,1)S(1)}, u32[]{:S(2)}, u32[]{:S(2)}) collective-permute-start(bf16[384,128]{1,0:T(8,128)(2,1)S(1)} %copy-done.3), channel_id=1, source_target_pairs={{0,2},{8,79},{1,3},{9,78},{2,0},{10,77},{3,1},{11,76},{64,66},{72,... | collective-permute-start | bytes 294920 | tf_op jit(solution)/shard_map/ppermute | solution.py:35
  33.3 9.1 %collective-permute-start.5 = (bf16[1536,128]{1,0:T(8,128)(2,1)S(1)}, bf16[1536,128]{1,0:T(8,128)(2,1)S(1)}, u32[]{:S(2)}, u32[]{:S(2)}) collective-permute-start(bf16[1536,128]{1,0:T(8,128)(2,1)S(1)} %shard_map.46.pair_ref), channel_id=1, source_target_pairs={{0,68},{8,9},{1,69},{9,8},{2,70},{10,11},{3,71},{11,10},{64,4},{72... | collective-permute-start | bytes 1179656 | tf_op jit(solution)/shard_map/ppermute | solution.py:35
  35.1 10.6 %collective-permute-start.7 = (bf16[768,384]{1,0:T(8,128)(2,1)S(1)}, bf16[768,384]{1,0:T(8,128)(2,1)S(1)}, u32[]{:S(2)}, u32[]{:S(2)}) collective-permute-start(bf16[768,384]{1,0:T(8,128)(2,1)S(1)} %collective-permute-done.6.refs_2_), channel_id=1, source_target_pairs={{0,8},{1,9},{2,10},{3,11},{4,12},{5,13},{6,14},{7,15},{8,0},{9,1},... | collective-permute-start | bytes 1769480 | tf_op jit(solution)/shard_map/ppermute | solution.py:39
  35.8 12.9 %collective-permute-start.9 = (bf16[768,384]{1,0:T(8,128)(2,1)S(1)}, bf16[768,384]{1,0:T(8,128)(2,1)S(1)}, u32[]{:S(2)}, u32[]{:S(2)}) collective-permute-start(bf16[768,384]{1,0:T(8,128)(2,1)S(1)} %collective-permute-done.8.refs_2_), channel_id=1, source_target_pairs={{0,8},{1,9},{2,10},{3,11},{4,12},{5,13},{6,14},{7,15},{8,0},{9,1},... | collective-permute-start | bytes 1769480 | tf_op jit(solution)/shard_map/ppermute | solution.py:39
  39.7 13.8 %collective-permute-start.11 = (bf16[768,384]{1,0:T(8,128)(2,1)S(1)}, bf16[768,384]{1,0:T(8,128)(2,1)S(1)}, u32[]{:S(2)}, u32[]{:S(2)}) collective-permute-start(bf16[768,384]{1,0:T(8,128)(2,1)S(1)} %collective-permute-done.10.refs_2_), channel_id=1, source_target_pairs={{0,8},{1,9},{2,10},{3,11},{4,12},{5,13},{6,14},{7,15},{8,0},{9,1},... | collective-permute-start | bytes 1769480 | tf_op jit(solution)/shard_map/ppermute | solution.py:39
  57.3 9.1 %collective-permute-start.12 = (bf16[768,256]{1,0:T(8,128)(2,1)S(1)}, bf16[768,256]{1,0:T(8,128)(2,1)S(1)}, u32[]{:S(2)}, u32[]{:S(2)}) collective-permute-start(bf16[768,256]{1,0:T(8,128)(2,1)S(1)} %shard_map.56), channel_id=1, source_target_pairs={{0,68},{8,9},{1,69},{9,8},{2,70},{10,11},{3,71},{11,10},{64,4},{72... | collective-permute-start | bytes 1179656 | tf_op jit(solution)/shard_map/ppermute | solution.py:35
  59.1 11.5 %collective-permute-start.13 = (bf16[768,256]{1,0:T(8,128)(2,1)S(1)}, bf16[768,256]{1,0:T(8,128)(2,1)S(1)}, u32[]{:S(2)}, u32[]{:S(2)}) collective-permute-start(bf16[768,256]{1,0:T(8,128)(2,1)S(1)} %get-tuple-element.41), channel_id=1, source_target_pairs={{0,68},{8,9},{1,69},{9,8},{2,70},{10,11},{3,71},{11,10},{64,4},{72... | collective-permute-start | bytes 1179656 | tf_op jit(solution)/shard_map/ppermute | solution.py:35
  66.4 6.3 %copy-start.1 = (bf16[384,256]{1,0:T(8,128)(2,1)S(1)}, bf16[384,256]{1,0:T(8,128)(2,1)}, u32[]{:S(2)}) copy-start(bf16[384,256]{1,0:T(8,128)(2,1)} %probe_hbm.1) | copy-start | bytes 589828
  66.4 8.6 %collective-permute-start.16 = (bf16[384,256]{1,0:T(8,128)(2,1)S(1)}, bf16[384,256]{1,0:T(8,128)(2,1)S(1)}, u32[]{:S(2)}, u32[]{:S(2)}) collective-permute-start(bf16[384,256]{1,0:T(8,128)(2,1)S(1)} %add_convert_fusion), channel_id=1, source_target_pairs={{0,1},{8,11},{1,0},{9,10},{2,3},{10,9},{3,2},{11,8},{64,65},{72,75... | collective-permute-start | bytes 589832 | tf_op jit(solution)/shard_map/ppermute | solution.py:35
  70.7 2.1 %copy-start.2 = (f32[384]{0:T(512)S(1)}, f32[384]{0:T(512)}, u32[]{:S(2)}) copy-start(f32[384]{0:T(512)} %param.6) | copy-start | bytes 4612
  70.7 7.4 %collective-permute-start.15 = (bf16[384,256]{1,0:T(8,128)(2,1)S(1)}, bf16[384,256]{1,0:T(8,128)(2,1)S(1)}, u32[]{:S(2)}, u32[]{:S(2)}) collective-permute-start(bf16[384,256]{1,0:T(8,128)(2,1)S(1)} %get-tuple-element.44), channel_id=1, source_target_pairs={{0,2},{8,79},{1,3},{9,78},{2,0},{10,77},{3,1},{11,76},{64,66},{72,... | collective-permute-start | bytes 589832 | tf_op jit(solution)/shard_map/ppermute | solution.py:35
  71.7 8.3 %collective-permute-start.14 = (bf16[384,256]{1,0:T(8,128)(2,1)S(1)}, bf16[384,256]{1,0:T(8,128)(2,1)S(1)}, u32[]{:S(2)}, u32[]{:S(2)}) collective-permute-start(bf16[384,256]{1,0:T(8,128)(2,1)S(1)} %get-tuple-element.43), channel_id=1, source_target_pairs={{0,3},{8,76},{1,2},{9,77},{2,1},{10,78},{3,0},{11,79},{64,67},{72,... | collective-permute-start | bytes 589832 | tf_op jit(solution)/shard_map/ppermute | solution.py:35
